TPU v7x, 128 devices: a whole 4x4x4 slice. The times are simulated.
128 devices in a mesh: fold: 4 (over x_hi, core), tile: 32 (over y, x_lo, z).
Axes of the slice: x: 4 (x_hi: 2, x_lo: 2; x = x_hi * 2 + x_lo), y: 4, z: 4, core: 2. Of those that a mesh axis runs over, the one named last changes fastest.
Arguments:
- design: bfloat16 [8192, 8192], P('fold', 'tile'), may hold values from -0.0625 to 0.0625
- weights: float32 [8192], P('fold'), may hold values from 0.2 to 5
- response: float32 [8192], P('fold'), may hold values from -6 to 6
- fold_of: int32 [32], P('fold'), may hold values from 0 to 7, as said below
- smoothing: float32 [128], P('tile'), may hold values from 0.05 to 1
Outputs:
- complement: float32 [8, 8192, 8192], P('fold', 'tile')
- complement_rhs: float32 [8, 8192], P('fold', 'tile')
Inputs may be any that keep to these rules, and one draw needn't show every extreme that they name: `fold_of`: the slabs of rows g * 2048 to (g + 1) * 2048 - 1 carry only fold ids g * 2 to (g + 1) * 2 - 1, and each of these appears on at least one of those slabs.
All inputs are finite; a program needn't handle non-finite values.
Results may differ from a plain program's by a relative error of at most 0.0029.
Values may be sent and summed in bfloat16 or wider, within the bound.
No kernel may reach another device: no remote copies, remote signals or barrier semaphores. Data moves between devices by JAX's collectives and lax.ppermute only.
A program may use at most 256 MiB of HBM per device.

v0:
```python
import jax
import jax.numpy as jnp
from jax import lax
from jax.sharding import PartitionSpec as P

FOLDS = 8
TERM = 64


def second_differences(width):
    rows = lax.broadcasted_iota(jnp.int32, (width - 2, width), 0)
    cols = lax.broadcasted_iota(jnp.int32, (width - 2, width), 1)
    diffs = (
        jnp.where(cols == rows, 1.0, 0.0)
        + jnp.where(cols == rows + 1, -2.0, 0.0)
        + jnp.where(cols == rows + 2, 1.0, 0.0)
    )
    diffs = diffs.astype(jnp.float32)
    return jnp.dot(
        diffs.T, diffs, precision=lax.Precision.HIGHEST, preferred_element_type=jnp.float32
    )


def body(design, weights, response, fold_of, smoothing):
    rows, block = design.shape
    slab_count = fold_of.shape[0]
    slab_rows = rows // slab_count
    me_tile = lax.axis_index("tile")
    held = FOLDS // lax.axis_size("fold")
    first_fold = lax.axis_index("fold") * held
    root_w = jnp.sqrt(weights)
    rooted = (design.astype(jnp.float32) * root_w[:, None]).astype(jnp.bfloat16)
    target = root_w * response
    member = (fold_of[:, None] == (first_fold + jnp.arange(held, dtype=jnp.int32))[None, :]).astype(
        jnp.float32
    )
    left = rooted.reshape(slab_count, slab_rows, block)
    slab_rhs = jnp.einsum(
        "sr,src->sc",
        target.reshape(slab_count, slab_rows),
        left.astype(jnp.float32),
        precision=lax.Precision.HIGHEST,
    )
    rhs_fold = jnp.einsum("sf,sc->fc", member, slab_rhs, precision=lax.Precision.HIGHEST)
    piece = lax.all_gather(rooted, "tile", axis=1, tiled=True)
    right = piece.reshape(slab_count, slab_rows, piece.shape[1])
    per_slab = jnp.einsum("src,srk->sck", left, right, preferred_element_type=jnp.float32)
    grams = jnp.einsum("sf,sck->fck", member, per_slab, precision=lax.Precision.HIGHEST)
    total_grams, total_rhs = lax.psum((jnp.sum(grams, axis=0), jnp.sum(rhs_fold, axis=0)), "fold")
    complement = total_grams[None] - grams
    complement_rhs = total_rhs[None] - rhs_fold
    penalty = jnp.kron(jnp.diag(smoothing), second_differences(TERM))
    column = me_tile * block
    current = lax.dynamic_slice_in_dim(complement, column, block, 2)
    complement = lax.dynamic_update_slice_in_dim(complement, current + penalty[None], column, 2)
    return (complement, complement_rhs)


def solution(mesh):
    in_specs = (P("fold", "tile"), P("fold"), P("fold"), P("fold"), P("tile"))
    out_specs = (P("fold", "tile", None), P("fold", "tile"))
    return jax.shard_map(body, mesh=mesh, in_specs=in_specs, out_specs=out_specs, check_vma=False)
```

profile of v0, /device:TPU:1, one launch (start us, length us, event | category | flops | bytes accessed | tf_op | source)
XLA Modules:
  0.0 752.4 jit_solution(17748182123532269160)
XLA Ops:
  7.2 0.0 all-gather.2.cloned.1.call-start
  7.2 0.7 sqrt_multiply_fusion
  7.9 2.5 multiply_convert_fusion
  10.5 0.0 all-gather.2.cloned.1.call-update
  10.5 0.0 all-reduce.2.cloned.1.call-start
  10.6 385.0 %all-gather.2.cloned.1.call-done = bf16[2048,8192]{1,0:T(8,128)(2,1)} async-done(((bf16[2048,256]{1,0:T(8,128)(2,1)}), bf16[2048,8192]{1,0:T(8,128)(2,1)}) %all-gather.2.cloned.1.call-update) | async-done | bytes 33554448 | tf_op jit(solution)/shard_map/all_gather | solution.py:45
  395.6 0.0 copy-start.2
  395.6 33.6 %fusion.27 = f32[8,256,8192]{2,1,0:T(8,128)} fusion(bf16[8,256,256]{2,1,0:T(8,128)(2,1)} %bitcast.20, bf16[8,256,8192]{2,1,0:T(8,128)(2,1)} %bitcast.19), kind=kOutput, calls=%fused_computation.41 | convolution fusion | flops 8589934592 | bytes 101711872 | tf_op jit(solution)/shard_map/src,srk->sck/dot_general | solution.py:47
  429.2 0.0 copy-done.2
  429.2 0.0 copy-start.1
  429.2 0.0 copy-start
  429.2 101.3 %fusion.25 = (f32[256,8192]{1,0:T(8,128)}, f32[2,256,8192]{2,0,1:T(2,128)}) fusion(f32[8,256,8192]{2,1,0:T(8,128)} %fusion.27, s32[8]{0:T(128)S(1)} %copy-done.2, s32[2]{0:T(128)S(1)} %iota_add_fusion.2), kind=kOutput, calls=%fused_computation.39 | convolution fusion | flops 404750336 | bytes 92274728 | tf_op jit(solution)/shard_map/sf,sck->fck/dot_general | solution.py:48
  530.5 0.0 all-reduce.2.cloned.1.call-update
  530.5 0.0 copy-done.1
  530.5 0.1 fusion.17
  530.6 0.3 fusion.2
  530.9 0.1 broadcast_multiply_fusion
  531.0 0.3 mul.51
  531.4 0.0 copy-done
  531.4 0.5 fusion.28
  531.9 0.2 fusion.26
  532.1 26.8 %psum.15 = f32[256]{0:T(256)S(1)} all-reduce(f32[256]{0:T(256)S(1)} %get-tuple-element.8), channel_id=1, replica_groups=mesh['fold'=4,'tile'=32] {'fold'}, use_global_device_ids=true, to_apply=%region_3.0 | all-reduce | flops 256 | bytes 2048 | tf_op jit(solution)/shard_map/psum | solution.py:49
  559.0 0.6 broadcast_subtract_fusion.1
  559.5 151.5 %all-reduce.2.cloned.1.call-done = f32[256,8192]{1,0:T(8,128)} async-done(((f32[256,8192]{1,0:T(8,128)}), f32[256,8192]{1,0:T(8,128)}) %all-reduce.2.cloned.1.call-update) | async-done | bytes 8388624 | tf_op jit(solution)/shard_map/psum | solution.py:49
  711.0 14.6 %broadcast_subtract_fusion = f32[2,256,8192]{2,0,1:T(2,128)} fusion(f32[2,256,8192]{2,0,1:T(2,128)} %get-tuple-element.7, f32[256,8192]{1,0:T(8,128)} %all-reduce.2.cloned.1.call-done), kind=kLoop, calls=%fused_computation.2 | loop fusion | flops 4194304 | bytes 41943040 | tf_op jit(solution)/shard_map/sub | solution.py:50
  725.6 2.2 add_dynamic-update-slice_fusion
  727.8 17.7 %copy.7 = f32[2,256,8192]{2,1,0:T(8,128)} copy(f32[2,256,8192]{2,0,1:T(2,128)} %add_dynamic-update-slice_fusion) | data formatting | bytes 33554432
  (2 shorter events, 0.0 us)
Async XLA Ops:
  7.2 388.4 %all-gather.2.cloned.1.call-start = ((), (), s32[]{:S(2)}) async-start(), calls=%async_computation | async-start | bytes 34603008 | tf_op jit(solution)/shard_map/all_gather | solution.py:45
  10.5 700.5 %all-reduce.2.cloned.1.call-start = ((), (), s32[]{:S(2)}) async-start(), calls=%async_computation.1 | async-start | bytes 16777216 | tf_op jit(solution)/shard_map/psum | solution.py:49
  395.6 33.6 %copy-start.2 = (s32[8]{0:T(128)S(1)}, s32[8]{0:T(128)}, u32[]{:S(2)}) copy-start(s32[8]{0:T(128)} %param.8) | copy-start | bytes 100
  429.2 101.3 %copy-start.1 = (f32[4]{0:T(128)S(1)}, f32[4]{0:T(128)}, u32[]{:S(2)}) copy-start(f32[4]{0:T(128)} %param.9) | copy-start | bytes 52
  429.2 102.2 %copy-start = (bf16[2048,256]{1,0:T(8,128)(2,1)S(1)}, bf16[2048,256]{1,0:T(8,128)(2,1)}, u32[]{:S(2)}) copy-start(bf16[2048,256]{1,0:T(8,128)(2,1)} %multiply_convert_fusion) | copy-start | bytes 3145732
Sparse Core Ops, SparseCore 0:
  10.6 384.8 all-gather.1
  530.6 180.3 all-reduce.1
where the time goes:
time: 753 us; the launch traced here: 752 us
  waiting for transfers between devices  536 us (71%)
  matrix products  136 us (18%)
  blocking collectives  26.8 us (4%)
  other arithmetic  20.8 us (3%)
  local copies, waits for them, and re-layouts  18.1 us (2%)
  between operations  14.1 us (2%)
    all_gather x1, waiting for transfers between devices, body(): piece = lax.all_gather(rooted, 'tile', axis=1, tiled=True)  385 us
    psum x1, waiting for transfers between devices, body(): lax.psum((jnp.sum(grams, axis=0), jnp.sum(rhs_fold, axis=0)), 'fold')  151 us
    dot_general x1, matrix products, body(): jnp.einsum('sf,sck->fck', member, per_slab, precision=lax.Precision.HIGHEST)  101 us
    dot_general x1, matrix products, body(): jnp.einsum('src,srk->sck', left, right, preferred_element_type=jnp.float32)  33.6 us
    psum x1, blocking collectives, body(): lax.psum((jnp.sum(grams, axis=0), jnp.sum(rhs_fold, axis=0)), 'fold')  26.8 us
    unnamed x7, local copies, waits for them, and re-layouts  17.8 us
  transfers between devices with their start and end apart: 2, of which 2 were waited for; matrix products, arithmetic and copies ran while one was open for 0% of the time, Pallas kernels for 0%

commit v1 on v0

v1 whole, which is shorter than its diff:
```python
import jax
import jax.numpy as jnp
from jax import lax
from jax.experimental import pallas as pl
from jax.experimental.pallas import tpu as pltpu
from jax.sharding import PartitionSpec as P


TERM = 64
AXES = ("fold", "tile")


def second_differences(width):
    rows = lax.broadcasted_iota(jnp.int32, (width - 2, width), 0)
    cols = lax.broadcasted_iota(jnp.int32, (width - 2, width), 1)
    diffs = (
        jnp.where(cols == rows, 1.0, 0.0)
        + jnp.where(cols == rows + 1, -2.0, 0.0)
        + jnp.where(cols == rows + 2, 1.0, 0.0)
    )
    diffs = diffs.astype(jnp.float32)
    return jnp.dot(
        diffs.T, diffs, precision=lax.Precision.HIGHEST, preferred_element_type=jnp.float32
    )


def flat(h, c, y, l, z):
    return (h * 2 + c) * 32 + y * 8 + l * 4 + z


def perm(move):
    pairs = []
    for h in range(2):
        for c in range(2):
            for y in range(4):
                for l in range(2):
                    for z in range(4):
                        pairs.append((flat(h, c, y, l, z), flat(*move(h, c, y, l, z))))
    return pairs


STEP = {
    ("y", 1): perm(lambda h, c, y, l, z: (h, c, (y + 1) % 4, l, z)),
    ("y", -1): perm(lambda h, c, y, l, z: (h, c, (y - 1) % 4, l, z)),
    ("z", 1): perm(lambda h, c, y, l, z: (h, c, y, l, (z + 1) % 4)),
    ("z", -1): perm(lambda h, c, y, l, z: (h, c, y, l, (z - 1) % 4)),
}
TURN = {
    ("y", 1): perm(lambda h, c, y, l, z: (h, c, (y + 1 - 2 * c) % 4, l, z)),
    ("y", -1): perm(lambda h, c, y, l, z: (h, c, (y - 1 + 2 * c) % 4, l, z)),
    ("z", 1): perm(lambda h, c, y, l, z: (h, c, y, l, (z + 1 - 2 * c) % 4)),
    ("z", -1): perm(lambda h, c, y, l, z: (h, c, y, l, (z - 1 + 2 * c) % 4)),
}
PARTNER = perm(lambda h, c, y, l, z: (h, c, y, 1 - l, z))
CORE = perm(lambda h, c, y, l, z: (h, 1 - c, y, l, z))
ACROSS = perm(lambda h, c, y, l, z: (1 - h, c, y, l if c == 0 else 1 - l, z))
OTHER = perm(lambda h, c, y, l, z: (1 - h, c, y, l, z))
MIB = 1 << 20
VMEM = 48 * MIB


def gram_kernel(slabs, local, r0, r1, *refs):
    xs, (g_ref, s_ref) = refs[:-2], refs[-2:]
    i = pl.program_id(0)
    size = r0.shape[1] // slabs
    g_ref[...] = jnp.zeros_like(g_ref)
    for k, x in enumerate(xs):

        @pl.when(i == k)
        def _(k=k, x=x):
            for t in range(slabs):
                part = pl.ds(t * size, size)
                for r, left in enumerate((r0, r1)[: 2 if k < 4 else 1]):
                    g_ref[2 * r + local[t]] += lax.dot_general(
                        left[:, part],
                        x[:, part],
                        (((1,), (1,)), ((), ())),
                        preferred_element_type=jnp.float32,
                    )

    for r in range(2):
        s_ref[r] = g_ref[2 * r] + g_ref[2 * r + 1]


def gram(local, rooted, partner, xs):
    rows, m = rooted.shape[1], len(xs)
    whole = pl.BlockSpec((256, rows), lambda i, f: (0, 0))
    return pl.pallas_call(
        lambda *refs: gram_kernel(local.shape[0], *refs),
        grid_spec=pltpu.PrefetchScalarGridSpec(
            num_scalar_prefetch=1,
            grid=(m,),
            in_specs=[whole] * (m + 2),
            out_specs=[
                pl.BlockSpec((4, 256, 256), lambda i, f: (0, 0, i)),
                pl.BlockSpec((2, 256, 256), lambda i, f: (0, 0, i)),
            ],
        ),
        out_shape=[
            pltpu.HBM((4, 256, 256 * m), jnp.float32),
            pltpu.HBM((2, 256, 256 * m), jnp.float32),
        ],
        compiler_params=pltpu.CompilerParams(vmem_limit_bytes=VMEM),
        cost_estimate=pl.CostEstimate(
            flops=2 * 512 * 256 * m * rows, bytes_accessed=4 * m * MIB, transcendentals=0
        ),
    )(local, rooted, partner, *xs)


def mix_kernel(r_ref, g1, s1, sr, tr, *refs):
    d_ref, u_ref = refs[-2:]
    other = s1[0]
    d_ref[0] = (g1[1] + other).astype(jnp.bfloat16)
    d_ref[1] = (g1[0] + other).astype(jnp.bfloat16)
    u_ref[...] = (sr[0] + tr[0]).astype(jnp.bfloat16)


def mix(pick, g, s, swapped, skip, u):
    extra = [] if u is None else [u]
    base = 4 * len(extra)
    width = 1024 - 256 * skip
    return pl.pallas_call(
        mix_kernel,
        grid_spec=pltpu.PrefetchScalarGridSpec(
            num_scalar_prefetch=1,
            grid=(4,),
            in_specs=[
                pl.BlockSpec((2, 256, 256), lambda i, r: (1, 0, i)),
                pl.BlockSpec((1, 256, 256), lambda i, r: (1, 0, i)),
                pl.BlockSpec((1, 256, 256), lambda i, r: (r[0], 0, i)),
                pl.BlockSpec((1, 256, 256), lambda i, r: (r[0], 0, i)),
            ]
            + [pl.BlockSpec(memory_space=pl.ANY)] * len(extra),
            out_specs=[
                pl.BlockSpec((2, 256, 256), lambda i, r: (0, 0, jnp.maximum(i - skip, 0))),
                pl.BlockSpec((256, 256), lambda i, r: (0, i + base)),
            ],
        ),
        out_shape=[
            pltpu.HBM((2, 256, width), jnp.bfloat16),
            pltpu.HBM((256, 2048), jnp.bfloat16),
        ],
        input_output_aliases={5: 1} if extra else {},
        compiler_params=pltpu.CompilerParams(vmem_limit_bytes=VMEM),
        cost_estimate=pl.CostEstimate(flops=MIB, bytes_accessed=8 * MIB, transcendentals=0),
    )(pick, g, swapped, s, swapped, *extra)


def final_kernel(first, pick, cols, g0, s0, mine, theirs, dr, *refs):
    out, buf, sems = refs[-3:]
    n = pl.program_id(0)
    slot = lax.rem(n, 2)
    swap = pick[0] == 0

    def copies(step, slot):
        return [
            pltpu.make_async_copy(
                buf.at[slot, j, :, :, pl.ds(128 * k, 128)],
                out.at[:, :, pl.ds(pl.multiple_of(cols[4 * step + 2 * k + j] * 128, 128), 128)],
                sems.at[slot, j, k],
            )
            for j in range(2)
            for k in range(2)
        ]

    @pl.when(n >= 2)
    def _():
        for copy in copies(n - 2, slot):
            copy.wait()

    a, b = mine[...].astype(jnp.float32), theirs[...].astype(jnp.float32)
    rest = s0[0] + jnp.where(swap, a, b)
    if first:
        rest = rest + jnp.where(n == 0, refs[0][...], 0.0)
    buf[slot, 0, 0] = g0[1] + rest
    buf[slot, 0, 1] = g0[0] + rest
    rest = jnp.where(swap, b, a)
    if first:

        @pl.when(n == 0)
        def _():
            gp, sp = refs[1], refs[2]
            buf[slot, 1, 0] = gp[1] + sp[0] + rest
            buf[slot, 1, 1] = gp[0] + sp[0] + rest

    @pl.when(n >= (1 if first else 0))
    def _():
        buf[slot, 1, 0] = dr[0].astype(jnp.float32) + rest
        buf[slot, 1, 1] = dr[1].astype(jnp.float32) + rest

    for copy in copies(n, slot):
        copy.start()

    @pl.when(n == 3)
    def _():
        for step in (2, 3):
            for copy in copies(step, step % 2):
                copy.wait()


def final(pick, cols, g, swapped, mine, theirs, half, dr, pen, out, total):
    first = out is None
    skip = 1 if first else 0
    base = 4 * half
    if first:
        extra = [pen, g, swapped]
        extra_specs = [
            pl.BlockSpec((256, 256), lambda n, p, c: (0, 0)),
            pl.BlockSpec((2, 256, 256), lambda n, p, c: (0, 0, 4)),
            pl.BlockSpec((1, 256, 256), lambda n, p, c: (0, 0, 4)),
        ]
    else:
        extra, extra_specs = [out], [pl.BlockSpec(memory_space=pl.ANY)]
    return pl.pallas_call(
        lambda *refs: final_kernel(first, *refs),
        grid_spec=pltpu.PrefetchScalarGridSpec(
            num_scalar_prefetch=2,
            grid=(4,),
            in_specs=[
                pl.BlockSpec((2, 256, 256), lambda n, p, c: (0, 0, n)),
                pl.BlockSpec((1, 256, 256), lambda n, p, c: (0, 0, n)),
                pl.BlockSpec((256, 256), lambda n, p, c: (0, n + base)),
                pl.BlockSpec((256, 256), lambda n, p, c: (0, n + base)),
                pl.BlockSpec((2, 256, 256), lambda n, p, c: (0, 0, jnp.maximum(n - skip, 0))),
            ]
            + extra_specs,
            out_specs=pl.BlockSpec(memory_space=pl.ANY),
            scratch_shapes=[
                pltpu.VMEM((2, 2, 2, 256, 256), jnp.float32),
                pltpu.SemaphoreType.DMA((2, 2, 2)),
            ],
        ),
        out_shape=pltpu.HBM((2, 256, total), jnp.float32),
        input_output_aliases={} if first else {7: 0},
        compiler_params=pltpu.CompilerParams(vmem_limit_bytes=VMEM),
        cost_estimate=pl.CostEstimate(flops=MIB, bytes_accessed=9 * MIB, transcendentals=0),
    )(pick, cols, g, swapped, mine, theirs, dr, *extra)


def body(design, weights, response, fold_of, smoothing):
    rows, block = design.shape
    slabs = fold_of.shape[0]
    width = block * 32
    fold, tile = lax.axis_index("fold"), lax.axis_index("tile")
    core = lax.rem(fold, 2)
    me_y, me_l, me_z = tile // 8, lax.rem(tile // 4, 2), lax.rem(tile, 4)
    pick = core.reshape(1).astype(jnp.int32)
    local = fold_of - 2 * fold

    def send(x, pairs):
        return lax.ppermute(x, AXES, pairs)

    root_w = jnp.sqrt(weights)
    rooted = (design.astype(jnp.float32) * root_w[:, None]).astype(jnp.bfloat16).T
    rooted = lax.optimization_barrier(rooted)
    partner = send(rooted, PARTNER)

    target = root_w * response
    member = jnp.repeat(local, rows // slabs)
    prod = rooted.astype(jnp.float32) * target[None, :]
    rhs = jnp.stack([jnp.sum(jnp.where(member == f, prod, 0.0), axis=1) for f in range(2)])
    chip_rhs = jnp.sum(rhs, axis=0)
    chip_rhs = chip_rhs + send(chip_rhs, CORE)
    total_rhs = chip_rhs + send(chip_rhs, OTHER)
    complement_rhs = total_rhs[None] - rhs

    near, chunks = [], ([], [], [])
    where = ([], [], [], [])
    where[0].extend([(0, 0, 0), (0, 0, 1)])
    far = []
    for colour, (p, q) in enumerate((("y", "z"), ("z", "y"))):
        at = lambda u, v, p=p, k=colour: (u, v, k) if p == "y" else (v, u, k)
        own = rooted[128 * colour : 128 * (colour + 1)]
        a = send(own, TURN[p, 1])
        b = send(own, TURN[p, -1])
        d = send(a, TURN[p, 1])
        ab = jnp.concatenate([jnp.where(core == 0, a, b), jnp.where(core == 0, b, a)], axis=0)
        ab_m, ab_p = send(ab, STEP[q, 1]), send(ab, STEP[q, -1])
        od = jnp.concatenate([own, d], axis=0)
        od_m, od_p = send(od, STEP[q, 1]), send(od, STEP[q, -1])
        ab_2 = send(ab_m, STEP[q, 1])
        od_2 = send(od_p, STEP[q, -1])
        near.append(ab)
        far.append(d)
        chunks[0].extend([ab_m, ab_p])
        chunks[1].extend([od_m, od_p])
        chunks[2].extend([ab_2, od_2])
        ab_off, od_off = (-1, 1), (0, 2)
        where[0].extend(at(o, 0) for o in ab_off)
        where[1].extend(at(o, v) for v in (-1, 1) for o in ab_off)
        where[2].extend(at(o, v) for v in (-1, 1) for o in od_off)
        where[3].extend(at(o, 2) for o in ab_off + od_off)
    where[0].extend([(2, 0, 0), (0, 2, 1)])
    work = [[rooted] + near + [jnp.concatenate(far, axis=0), partner]] + list(chunks)

    pen = jnp.kron(jnp.diag(smoothing), second_differences(TERM))

    state, mine, theirs, u = [], [], [], None
    for n, xs in enumerate(work):
        g, s = gram(local, rooted, partner, xs)
        swapped = send(s, CORE)
        give, u = mix(pick, g, s, swapped, 1 if n == 0 else 0, u)
        dr = send(give, PARTNER)
        state.append((g, swapped, dr))
        if n % 2 == 1:
            mine.append(send(u, ACROSS))
            theirs.append(send(mine[-1], CORE))
            u = None
    out = None
    for n, (g, swapped, dr) in enumerate(state):
        cols = []
        for dy, dz, colour in where[n]:
            y, z = lax.rem(me_y + dy + 4, 4), lax.rem(me_z + dz + 4, 4)
            for l in (me_l, 1 - me_l):
                cols.append((y * 8 + l * 4 + z) * 2 + colour)
        cols = jnp.stack(cols).astype(jnp.int32)
        out = final(
            pick, cols, g, swapped, mine[n // 2], theirs[n // 2], n % 2, dr, pen, out, width
        )
    return (out, complement_rhs)


def solution(mesh):
    in_specs = (P("fold", "tile"), P("fold"), P("fold"), P("fold"), P("tile"))
    out_specs = (P("fold", "tile", None), P("fold", "tile"))

    return jax.shard_map(body, mesh=mesh, in_specs=in_specs, out_specs=out_specs, check_vma=False)
```

time: 753 us -> 267 us (0.35)
  waiting for transfers between devices: 536 us -> 103 us
  matrix products: 136 us -> 0.31 us
  starting transfers between devices: 0.08 us -> 71.3 us
  Pallas kernels: 0 us -> 70.3 us
  blocking collectives: 26.8 us -> 0 us
  other arithmetic: 20.8 us -> 6.85 us
  between operations: 14.1 us -> 1.2 us
  local copies, waits for them, and re-layouts: 18.1 us -> 10.4 us
    all_gather x1 -> x0, waiting for transfers between devices: 385 us -> none  [body(): piece = lax.all_gather(rooted, 'tile', axis=1, tiled=True)]
    psum x1 -> x0, waiting for transfers between devices: 151 us -> none  [body(): lax.psum((jnp.sum(grams, axis=0), jnp.sum(rhs_fold, axis=0)), 'fold')]
    dot_general x4 -> x0, matrix products: 136 us -> none  [the longest x1 101 us: body(): jnp.einsum('sf,sck->fck', member, per_slab, precision=lax.Precision.HIGHEST)]
    ppermute x0 -> x33, waiting for transfers between devices: none -> 103 us  [send(): return lax.ppermute(x, AXES, pairs)]
    ppermute x0 -> x33, starting transfers between devices: none -> 71.3 us  [send(): return lax.ppermute(x, AXES, pairs)]
    pallas_call x0 -> x12, Pallas kernels: none -> 70.3 us  [the longest x4 31.9 us: gram(): pl.pallas_call(lambda *refs: gram_kernel(local.shape[0], *refs), grid_spe...]
    psum x1 -> x0, blocking collectives: 26.8 us -> none  [body(): lax.psum((jnp.sum(grams, axis=0), jnp.sum(rhs_fold, axis=0)), 'fold')]
    sub x2 -> x1, other arithmetic: 15.2 us -> 0.59 us  [body(): complement_rhs = total_rhs[None] - rhs]
  transfers between devices with their start and end apart: 2 -> 33, of which waited for: 2 -> 16; matrix products, arithmetic and copies ran while one was open for 0% -> 3% of each run, Pallas kernels for 0% -> 25%
where the time goes in v1:
time: 267 us; the launch traced here: 263 us
  waiting for transfers between devices  103 us (39%)
  starting transfers between devices  71.3 us (27%)
  Pallas kernels  70.3 us (26%)
  local copies, waits for them, and re-layouts  10.4 us (4%)
  other arithmetic  6.85 us (3%)
    ppermute x33, waiting for transfers between devices, send(): return lax.ppermute(x, AXES, pairs)  103 us
    ppermute x33, starting transfers between devices, send(): return lax.ppermute(x, AXES, pairs)  71.3 us
    pallas_call x4, Pallas kernels, gram(): pl.pallas_call(lambda *refs: gram_kernel(local.shape[0], *refs), grid_spe...  31.9 us
    pallas_call x4, Pallas kernels, final(): pl.pallas_call(lambda *refs: final_kernel(first, *refs), grid_spec=pltpu....  21.4 us
    pallas_call x4, Pallas kernels, mix(): pl.pallas_call(mix_kernel, grid_spec=pltpu.PrefetchScalarGridSpec(num_sca...  17 us
    unnamed x55, local copies, waits for them, and re-layouts  9.39 us
  transfers between devices with their start and end apart: 33, of which 16 were waited for; matrix products, arithmetic and copies ran while one was open for 3% of the time, Pallas kernels for 25%

profile of v1, /device:TPU:1, one launch (start us, length us, event | category | flops | bytes accessed | tf_op | source)
XLA Modules:
  0.0 263.3 jit_solution(10417996999187711000)
XLA Ops:
  2.5 4.6 %collective-permute-start.8 = (bf16[128,2048]{1,0:T(8,128)(2,1)S(1)}, bf16[128,2048]{1,0:T(8,128)(2,1)}, u32[]{:S(2)}, u32[]{:S(2)}) collective-permute-start(bf16[128,2048]{1,0:T(8,128)(2,1)S(1)} %get-tuple-element.40), channel_id=1, source_target_pairs={{0,1},{1,2},{2,3},{3,0},{4,5},{5,6},{6,7},{7,4},{8,9},{9,10},{10,1... | collective-permute-start | bytes 1572872 | tf_op jit(solution)/shard_map/ppermute | solution.py:251
  7.2 2.7 %collective-permute-start.1 = (bf16[128,2048]{1,0:T(8,128)(2,1)S(1)}, bf16[128,2048]{1,0:T(8,128)(2,1)}, u32[]{:S(2)}, u32[]{:S(2)}) collective-permute-start(bf16[128,2048]{1,0:T(8,128)(2,1)S(1)} %get-tuple-element.41), channel_id=1, source_target_pairs={{0,8},{1,9},{2,10},{3,11},{4,12},{5,13},{6,14},{7,15},{8,16},{9,17... | collective-permute-start | bytes 1572872 | tf_op jit(solution)/shard_map/ppermute | solution.py:251
  11.1 6.6 %collective-permute-done.8 = bf16[128,2048]{1,0:T(8,128)(2,1)} collective-permute-done((bf16[128,2048]{1,0:T(8,128)(2,1)S(1)}, bf16[128,2048]{1,0:T(8,128)(2,1)}, u32[]{:S(2)}, u32[]{:S(2)}) %collective-permute-start.8) | collective-permute-done | bytes 524320 | tf_op jit(solution)/shard_map/ppermute | solution.py:251
  17.7 2.9 %collective-permute-done.9 = bf16[128,2048]{1,0:T(8,128)(2,1)} collective-permute-done((bf16[128,2048]{1,0:T(8,128)(2,1)S(1)}, bf16[128,2048]{1,0:T(8,128)(2,1)}, u32[]{:S(2)}, u32[]{:S(2)}) %collective-permute-start.9) | collective-permute-done | bytes 524320 | tf_op jit(solution)/shard_map/ppermute | solution.py:251
  25.1 2.7 %collective-permute-start.12 = (bf16[128,2048]{1,0:T(8,128)(2,1)}, bf16[128,2048]{1,0:T(8,128)(2,1)S(1)}, u32[]{:S(2)}, u32[]{:S(2)}) collective-permute-start(bf16[128,2048]{1,0:T(8,128)(2,1)} %collective-permute-done.8), channel_id=1, source_target_pairs={{0,1},{1,2},{2,3},{3,0},{4,5},{5,6},{6,7},{7,4},{8,9},{9,10},{10,1... | collective-permute-start | bytes 1572872 | tf_op jit(solution)/shard_map/ppermute | solution.py:251
  29.3 4.9 %collective-permute-done.12 = bf16[128,2048]{1,0:T(8,128)(2,1)S(1)} collective-permute-done((bf16[128,2048]{1,0:T(8,128)(2,1)}, bf16[128,2048]{1,0:T(8,128)(2,1)S(1)}, u32[]{:S(2)}, u32[]{:S(2)}) %collective-permute-start.12) | collective-permute-done | bytes 524320 | tf_op jit(solution)/shard_map/ppermute | solution.py:251
  41.2 7.4 %collective-permute-done.10.refs_5_ = bf16[256,2048]{1,0:T(8,128)(2,1)} collective-permute-done((bf16[256,2048]{1,0:T(8,128)(2,1)S(1)}, bf16[256,2048]{1,0:T(8,128)(2,1)}, u32[]{:S(2)}, u32[]{:S(2)}) %collective-permute-start.10) | collective-permute-done | bytes 1048608 | tf_op jit(solution)/shard_map/ppermute | solution.py:251
  48.6 2.8 %collective-permute-done.3.refs_3_ = bf16[256,2048]{1,0:T(8,128)(2,1)} collective-permute-done((bf16[256,2048]{1,0:T(8,128)(2,1)S(1)}, bf16[256,2048]{1,0:T(8,128)(2,1)}, u32[]{:S(2)}, u32[]{:S(2)}) %collective-permute-start.3) | collective-permute-done | bytes 1048608 | tf_op jit(solution)/shard_map/ppermute | solution.py:251
  54.7 4.5 %collective-permute-done.13.refs_6_ = bf16[256,2048]{1,0:T(8,128)(2,1)} collective-permute-done((bf16[256,2048]{1,0:T(8,128)(2,1)}, bf16[256,2048]{1,0:T(8,128)(2,1)}, u32[]{:S(2)}, u32[]{:S(2)}) %collective-permute-start.13) | collective-permute-done | bytes 1048608 | tf_op jit(solution)/shard_map/ppermute | solution.py:251
  59.9 2.7 %collective-permute-done.6.refs_4_ = bf16[256,2048]{1,0:T(8,128)(2,1)} collective-permute-done((bf16[256,2048]{1,0:T(8,128)(2,1)S(1)}, bf16[256,2048]{1,0:T(8,128)(2,1)}, u32[]{:S(2)}, u32[]{:S(2)}) %collective-permute-start.6) | collective-permute-done | bytes 1048608 | tf_op jit(solution)/shard_map/ppermute | solution.py:251
  64.1 3.8 %collective-permute-done.16.refs_3_ = bf16[256,2048]{1,0:T(8,128)(2,1)S(1)} collective-permute-done((bf16[256,2048]{1,0:T(8,128)(2,1)S(1)}, bf16[256,2048]{1,0:T(8,128)(2,1)S(1)}, u32[]{:S(2)}, u32[]{:S(2)}) %collective-permute-start.16) | collective-permute-done | bytes 1048608 | tf_op jit(solution)/shard_map/ppermute | solution.py:251
  73.5 7.9 %shard_map.73 = (f32[4,256,1280]{2,1,0:T(8,128)}, f32[2,256,1280]{2,1,0:T(8,128)}) custom-call(s32[8]{0:T(128)S(1)} %get-tuple-element.37.refs_0_, bf16[256,2048]{1,0:T(8,128)(2,1)S(1)} %copy-done.7, bf16[256,2048]{1,0:T(8,128)(2,1)} %collective-permute-done.refs_2_.refs_7_, bf16[256,2048]{1,0:T(8,128)(2,1)S(1)} %copy-done.7, ...), custom_call_target="tpu_custom_call" | custom-call | flops 2684354560 | bytes 20971520 | tf_op jit(solution)/shard_map/pallas_call | solution.py:88
  81.4 35.1 %collective-permute-start.26 = (f32[2,256,1280]{2,1,0:T(8,128)}, f32[2,256,1280]{2,1,0:T(8,128)S(1)}, u32[]{:S(2)}, u32[]{:S(2)}) collective-permute-start(f32[2,256,1280]{2,1,0:T(8,128)} %get-tuple-element.29.sr), channel_id=1, source_target_pairs={{0,32},{1,33},{2,34},{3,35},{4,36},{5,37},{6,38},{7,39},{8,40},{9,... | collective-permute-start | bytes 7864328 | tf_op jit(solution)/shard_map/ppermute | solution.py:251
  116.5 7.9 %shard_map.72 = (f32[4,256,1024]{2,1,0:T(8,128)}, f32[2,256,1024]{2,1,0:T(8,128)}) custom-call(s32[8]{0:T(128)S(1)} %get-tuple-element.37.refs_0_, bf16[256,2048]{1,0:T(8,128)(2,1)S(1)} %copy-done.8, bf16[256,2048]{1,0:T(8,128)(2,1)} %collective-permute-done.refs_2_.refs_7_, bf16[256,2048]{1,0:T(8,128)(2,1)} %collective-permute-done.3.refs_3_, ...), custom_call_target="tpu_custom_call" | custom-call | flops 2147483648 | bytes 16777216 | tf_op jit(solution)/shard_map/pallas_call | solution.py:88
  124.4 7.9 %shard_map.69 = (f32[4,256,1024]{2,1,0:T(8,128)}, f32[2,256,1024]{2,1,0:T(8,128)}) custom-call(s32[8]{0:T(128)S(1)} %get-tuple-element.37.refs_0_, bf16[256,2048]{1,0:T(8,128)(2,1)S(1)} %copy-done.8, bf16[256,2048]{1,0:T(8,128)(2,1)} %collective-permute-done.refs_2_.refs_7_, bf16[256,2048]{1,0:T(8,128)(2,1)S(1)} %copy-done.21, ...), custom_call_target="tpu_custom_call" | custom-call | flops 2147483648 | bytes 16777216 | tf_op jit(solution)/shard_map/pallas_call | solution.py:88
  132.9 8.1 %shard_map.68 = (f32[4,256,1024]{2,1,0:T(8,128)}, f32[2,256,1024]{2,1,0:T(8,128)}) custom-call(s32[8]{0:T(128)S(1)} %get-tuple-element.37.refs_0_, bf16[256,2048]{1,0:T(8,128)(2,1)S(1)} %copy-done.8, bf16[256,2048]{1,0:T(8,128)(2,1)} %collective-permute-done.refs_2_.refs_7_, bf16[256,2048]{1,0:T(8,128)(2,1)} %collective-permute-done.4.refs_3_, ...), custom_call_target="tpu_custom_call" | custom-call | flops 2147483648 | bytes 16777216 | tf_op jit(solution)/shard_map/pallas_call | solution.py:88
  141.2 3.7 %shard_map.74 = (bf16[2,256,768]{2,1,0:T(8,128)(2,1)}, bf16[256,2048]{1,0:T(8,128)(2,1)}) custom-call(s32[1]{0:T(128)} %bitcast.r_ref.refs_0_, f32[4,256,1280]{2,1,0:T(8,128)} %get-tuple-element.28.g1.refs_2_.refs_8_, f32[2,256,1280]{2,1,0:T(8,128)S(1)} %collective-permute-done.26.s1.tr.refs_3_.refs_9_, f32[2,256,1280]{2,1,0:T(8,128)S(1)} %copy-done.9, ...), custom_call_target="tpu_custom_call" | custom-call | flops 1048576 | bytes 8388608 | tf_op jit(solution)/shard_map/pallas_call | solution.py:122
  144.9 4.8 %shard_map.75 = (bf16[2,256,1024]{2,1,0:T(8,128)(2,1)}, bf16[256,2048]{1,0:T(8,128)(2,1)}) custom-call(s32[1]{0:T(128)} %bitcast.r_ref.refs_0_, f32[4,256,1024]{2,1,0:T(8,128)} %get-tuple-element.26.g1.refs_2_, f32[2,256,1024]{2,1,0:T(8,128)S(1)} %collective-permute-done.25.s1.tr.refs_3_, ...), custom_call_target="tpu_custom_call", output_to_operand_aliasing={{1}: (5, {})} | custom-call | flops 1048576 | bytes 8388608 | tf_op jit(solution)/shard_map/pallas_call | solution.py:122
  149.7 2.5 collective-permute-start.27
  152.2 4.3 %shard_map.70 = (bf16[2,256,1024]{2,1,0:T(8,128)(2,1)}, bf16[256,2048]{1,0:T(8,128)(2,1)}) custom-call(s32[1]{0:T(128)} %bitcast.r_ref.refs_0_, f32[4,256,1024]{2,1,0:T(8,128)} %get-tuple-element.20.g1.refs_2_, f32[2,256,1024]{2,1,0:T(8,128)S(1)} %collective-permute-done.18.s1.tr.refs_3_, f32[2,256,1024]{2,1,0:T(8,128)S(1)} %copy-done.10, ...), custom_call_target="tpu_custom_call" | custom-call | flops 1048576 | bytes 8388608 | tf_op jit(solution)/shard_map/pallas_call | solution.py:122
  156.5 4.2 %shard_map.71 = (bf16[2,256,1024]{2,1,0:T(8,128)(2,1)}, bf16[256,2048]{1,0:T(8,128)(2,1)}) custom-call(s32[1]{0:T(128)} %bitcast.r_ref.refs_0_, f32[4,256,1024]{2,1,0:T(8,128)} %get-tuple-element.18.g1.refs_2_, f32[2,256,1024]{2,1,0:T(8,128)S(1)} %collective-permute-done.15.s1.tr.refs_3_, ...), custom_call_target="tpu_custom_call", output_to_operand_aliasing={{1}: (5, {})} | custom-call | flops 1048576 | bytes 8388608 | tf_op jit(solution)/shard_map/pallas_call | solution.py:122
  163.0 2.6 collective-permute-start.31
  166.4 2.5 collective-permute-start.32
  168.8 18.5 %collective-permute-done.27.refs_4_ = bf16[256,2048]{1,0:T(8,128)(2,1)} collective-permute-done((bf16[256,2048]{1,0:T(8,128)(2,1)}, bf16[256,2048]{1,0:T(8,128)(2,1)}, u32[]{:S(2)}, u32[]{:S(2)}) %collective-permute-start.27) | collective-permute-done | bytes 1048608 | tf_op jit(solution)/shard_map/ppermute | solution.py:251
  188.8 9.8 %collective-permute-done.19.refs_4_ = bf16[256,2048]{1,0:T(8,128)(2,1)} collective-permute-done((bf16[256,2048]{1,0:T(8,128)(2,1)}, bf16[256,2048]{1,0:T(8,128)(2,1)}, u32[]{:S(2)}, u32[]{:S(2)}) %collective-permute-start.19) | collective-permute-done | bytes 1048608 | tf_op jit(solution)/shard_map/ppermute | solution.py:251
  204.7 5.3 %shard_map.76.refs_7_ = f32[2,256,8192]{2,1,0:T(8,128)} custom-call(s32[1]{0:T(128)} %bitcast.r_ref.refs_0_, s32[16]{0:T(128)S(1)} %stack.280.refs_1_, f32[4,256,1280]{2,1,0:T(8,128)} %get-tuple-element.28.g1.refs_2_.refs_8_, f32[2,256,1280]{2,1,0:T(8,128)S(1)} %collective-permute-done.26.s1.tr.refs_3_.refs_9_, ...), custom_call_target="tpu_custom_call" | custom-call | flops 1048576 | bytes 9437184 | tf_op jit(solution)/shard_map/pallas_call | solution.py:214
  210.0 2.8 %collective-permute-done.29.refs_6_ = bf16[2,256,1024]{2,1,0:T(8,128)(2,1)} collective-permute-done((bf16[2,256,1024]{2,1,0:T(8,128)(2,1)}, bf16[2,256,1024]{2,1,0:T(8,128)(2,1)}, u32[]{:S(2)}, u32[]{:S(2)}) %collective-permute-start.29) | collective-permute-done | bytes 1048608 | tf_op jit(solution)/shard_map/ppermute | solution.py:251
  212.8 5.4 %shard_map.77.refs_7_ = f32[2,256,8192]{2,1,0:T(8,128)} custom-call(s32[1]{0:T(128)} %bitcast.r_ref.refs_0_, s32[16]{0:T(128)S(1)} %stack.263.refs_1_, f32[4,256,1024]{2,1,0:T(8,128)} %get-tuple-element.26.g1.refs_2_, f32[2,256,1024]{2,1,0:T(8,128)S(1)} %copy-done.3, ...), custom_call_target="tpu_custom_call", output_to_operand_aliasing={{}: (7, {})} | custom-call | flops 1048576 | bytes 9437184 | tf_op jit(solution)/shard_map/pallas_call | solution.py:214
  218.2 17.1 %collective-permute-done.22.refs_6_ = bf16[2,256,1024]{2,1,0:T(8,128)(2,1)} collective-permute-done((bf16[2,256,1024]{2,1,0:T(8,128)(2,1)}, bf16[2,256,1024]{2,1,0:T(8,128)(2,1)}, u32[]{:S(2)}, u32[]{:S(2)}) %collective-permute-start.22) | collective-permute-done | bytes 1048608 | tf_op jit(solution)/shard_map/ppermute | solution.py:251
  235.3 5.4 %shard_map.78.refs_7_ = f32[2,256,8192]{2,1,0:T(8,128)} custom-call(s32[1]{0:T(128)} %bitcast.r_ref.refs_0_, s32[16]{0:T(128)S(1)} %stack.246.refs_1_, f32[4,256,1024]{2,1,0:T(8,128)} %get-tuple-element.20.g1.refs_2_, f32[2,256,1024]{2,1,0:T(8,128)S(1)} %copy-done.1, ...), custom_call_target="tpu_custom_call", output_to_operand_aliasing={{}: (7, {})} | custom-call | flops 1048576 | bytes 9437184 | tf_op jit(solution)/shard_map/pallas_call | solution.py:214
  240.7 17.1 %collective-permute-done.21.refs_6_ = bf16[2,256,1024]{2,1,0:T(8,128)(2,1)} collective-permute-done((bf16[2,256,1024]{2,1,0:T(8,128)(2,1)}, bf16[2,256,1024]{2,1,0:T(8,128)(2,1)}, u32[]{:S(2)}, u32[]{:S(2)}) %collective-permute-start.21) | collective-permute-done | bytes 1048608 | tf_op jit(solution)/shard_map/ppermute | solution.py:251
  257.8 5.4 %shard_map.79 = f32[2,256,8192]{2,1,0:T(8,128)} custom-call(s32[1]{0:T(128)} %bitcast.r_ref.refs_0_, s32[16]{0:T(128)S(1)} %stack.229.refs_1_, f32[4,256,1024]{2,1,0:T(8,128)} %get-tuple-element.18.g1.refs_2_, f32[2,256,1024]{2,1,0:T(8,128)S(1)} %copy-done.5, bf16[256,2048]{1,0:T(8,128)(2,1)} %collective-permute-done.19.refs_4_, ...), custom_call_target="tpu_custom_call", output_to_operand_aliasing={{}: (7, {})} | custom-call | flops 1048576 | bytes 9437184 | tf_op jit(solution)/shard_map/pallas_call | solution.py:214
  (129 shorter events, 38.3 us)
Async XLA Ops:
  2.5 15.2 %collective-permute-start.8 = (bf16[128,2048]{1,0:T(8,128)(2,1)S(1)}, bf16[128,2048]{1,0:T(8,128)(2,1)}, u32[]{:S(2)}, u32[]{:S(2)}) collective-permute-start(bf16[128,2048]{1,0:T(8,128)(2,1)S(1)} %get-tuple-element.40), channel_id=1, source_target_pairs={{0,1},{1,2},{2,3},{3,0},{4,5},{5,6},{6,7},{7,4},{8,9},{9,10},{10,1... | collective-permute-start | bytes 1572872 | tf_op jit(solution)/shard_map/ppermute | solution.py:251
  7.2 13.4 %collective-permute-start.9 = (bf16[128,2048]{1,0:T(8,128)(2,1)S(1)}, bf16[128,2048]{1,0:T(8,128)(2,1)}, u32[]{:S(2)}, u32[]{:S(2)}) collective-permute-start(bf16[128,2048]{1,0:T(8,128)(2,1)S(1)} %get-tuple-element.40), channel_id=1, source_target_pairs={{0,3},{1,0},{2,1},{3,2},{4,7},{5,4},{6,5},{7,6},{8,11},{9,8},{10,9... | collective-permute-start | bytes 1572872 | tf_op jit(solution)/shard_map/ppermute | solution.py:251
  7.2 15.9 %collective-permute-start.1 = (bf16[128,2048]{1,0:T(8,128)(2,1)S(1)}, bf16[128,2048]{1,0:T(8,128)(2,1)}, u32[]{:S(2)}, u32[]{:S(2)}) collective-permute-start(bf16[128,2048]{1,0:T(8,128)(2,1)S(1)} %get-tuple-element.41), channel_id=1, source_target_pairs={{0,8},{1,9},{2,10},{3,11},{4,12},{5,13},{6,14},{7,15},{8,16},{9,17... | collective-permute-start | bytes 1572872 | tf_op jit(solution)/shard_map/ppermute | solution.py:251
  9.9 13.7 %collective-permute-start.2 = (bf16[128,2048]{1,0:T(8,128)(2,1)S(1)}, bf16[128,2048]{1,0:T(8,128)(2,1)}, u32[]{:S(2)}, u32[]{:S(2)}) collective-permute-start(bf16[128,2048]{1,0:T(8,128)(2,1)S(1)} %get-tuple-element.41), channel_id=1, source_target_pairs={{0,24},{1,25},{2,26},{3,27},{4,28},{5,29},{6,30},{7,31},{8,0},{9,1... | collective-permute-start | bytes 1572872 | tf_op jit(solution)/shard_map/ppermute | solution.py:251
  9.9 30.2 %collective-permute-start = (bf16[256,2048]{1,0:T(8,128)(2,1)S(1)}, bf16[256,2048]{1,0:T(8,128)(2,1)}, u32[]{:S(2)}, u32[]{:S(2)}) collective-permute-start(bf16[256,2048]{1,0:T(8,128)(2,1)S(1)} %fusion.refs_1_.refs_3_), channel_id=1, source_target_pairs={{0,4},{1,5},{2,6},{3,7},{4,0},{5,1},{6,2},{7,3},{8,12},{9,13},{10,... | collective-permute-start | bytes 3145736 | tf_op jit(solution)/shard_map/ppermute | solution.py:251
  22.0 26.6 %collective-permute-start.10 = (bf16[256,2048]{1,0:T(8,128)(2,1)S(1)}, bf16[256,2048]{1,0:T(8,128)(2,1)}, u32[]{:S(2)}, u32[]{:S(2)}) collective-permute-start(bf16[256,2048]{1,0:T(8,128)(2,1)S(1)} %pad_maximum_fusion.4.refs_5_), channel_id=1, source_target_pairs={{0,8},{1,9},{2,10},{3,11},{4,12},{5,13},{6,14},{7,15},{8,16},{9,17... | collective-permute-start | bytes 3145736 | tf_op jit(solution)/shard_map/ppermute | solution.py:251
  25.0 26.5 %collective-permute-start.3 = (bf16[256,2048]{1,0:T(8,128)(2,1)S(1)}, bf16[256,2048]{1,0:T(8,128)(2,1)}, u32[]{:S(2)}, u32[]{:S(2)}) collective-permute-start(bf16[256,2048]{1,0:T(8,128)(2,1)S(1)} %pad_maximum_fusion.2.refs_4_), channel_id=1, source_target_pairs={{0,1},{1,2},{2,3},{3,0},{4,5},{5,6},{6,7},{7,4},{8,9},{9,10},{10,1... | collective-permute-start | bytes 3145736 | tf_op jit(solution)/shard_map/ppermute | solution.py:251
  25.1 9.1 %collective-permute-start.12 = (bf16[128,2048]{1,0:T(8,128)(2,1)}, bf16[128,2048]{1,0:T(8,128)(2,1)S(1)}, u32[]{:S(2)}, u32[]{:S(2)}) collective-permute-start(bf16[128,2048]{1,0:T(8,128)(2,1)} %collective-permute-done.8), channel_id=1, source_target_pairs={{0,1},{1,2},{2,3},{3,0},{4,5},{5,6},{6,7},{7,4},{8,9},{9,10},{10,1... | collective-permute-start | bytes 1572872 | tf_op jit(solution)/shard_map/ppermute | solution.py:251
  27.8 8.6 %collective-permute-start.5 = (bf16[128,2048]{1,0:T(8,128)(2,1)}, bf16[128,2048]{1,0:T(8,128)(2,1)S(1)}, u32[]{:S(2)}, u32[]{:S(2)}) collective-permute-start(bf16[128,2048]{1,0:T(8,128)(2,1)} %collective-permute-done.1), channel_id=1, source_target_pairs={{0,8},{1,9},{2,10},{3,11},{4,12},{5,13},{6,14},{7,15},{8,16},{9,17... | collective-permute-start | bytes 1572872 | tf_op jit(solution)/shard_map/ppermute | solution.py:251
  34.2 17.3 %collective-permute-start.24 = (bf16[256,2048]{1,0:T(8,128)(2,1)S(1)}, bf16[256,2048]{1,0:T(8,128)(2,1)S(1)}, u32[]{:S(2)}, u32[]{:S(2)}) collective-permute-start(bf16[256,2048]{1,0:T(8,128)(2,1)S(1)} %pad_maximum_fusion.4.refs_5_), channel_id=1, source_target_pairs={{0,24},{1,25},{2,26},{3,27},{4,28},{5,29},{6,30},{7,31},{8,0},{9,1... | collective-permute-start | bytes 3145736 | tf_op jit(solution)/shard_map/ppermute | solution.py:251
  36.4 15.6 %collective-permute-start.23 = (bf16[256,2048]{1,0:T(8,128)(2,1)S(1)}, bf16[256,2048]{1,0:T(8,128)(2,1)S(1)}, u32[]{:S(2)}, u32[]{:S(2)}) collective-permute-start(bf16[256,2048]{1,0:T(8,128)(2,1)S(1)} %pad_maximum_fusion.2.refs_4_), channel_id=1, source_target_pairs={{0,3},{1,0},{2,1},{3,2},{4,7},{5,4},{6,5},{7,6},{8,11},{9,8},{10,9... | collective-permute-start | bytes 3145736 | tf_op jit(solution)/shard_map/ppermute | solution.py:251
  40.1 19.1 %collective-permute-start.13 = (bf16[256,2048]{1,0:T(8,128)(2,1)}, bf16[256,2048]{1,0:T(8,128)(2,1)}, u32[]{:S(2)}, u32[]{:S(2)}) collective-permute-start(bf16[256,2048]{1,0:T(8,128)(2,1)} %get-tuple-element.46), channel_id=1, source_target_pairs={{0,24},{1,25},{2,26},{3,27},{4,28},{5,29},{6,30},{7,31},{8,0},{9,1... | collective-permute-start | bytes 3145736 | tf_op jit(solution)/shard_map/ppermute | solution.py:251
  48.6 13.9 %collective-permute-start.6 = (bf16[256,2048]{1,0:T(8,128)(2,1)S(1)}, bf16[256,2048]{1,0:T(8,128)(2,1)}, u32[]{:S(2)}, u32[]{:S(2)}) collective-permute-start(bf16[256,2048]{1,0:T(8,128)(2,1)S(1)} %get-tuple-element.45), channel_id=1, source_target_pairs={{0,3},{1,0},{2,1},{3,2},{4,7},{5,4},{6,5},{7,6},{8,11},{9,8},{10,9... | collective-permute-start | bytes 3145736 | tf_op jit(solution)/shard_map/ppermute | solution.py:251
  51.5 16.5 %collective-permute-start.16 = (bf16[256,2048]{1,0:T(8,128)(2,1)S(1)}, bf16[256,2048]{1,0:T(8,128)(2,1)S(1)}, u32[]{:S(2)}, u32[]{:S(2)}) collective-permute-start(bf16[256,2048]{1,0:T(8,128)(2,1)S(1)} %get-tuple-element.45), channel_id=1, source_target_pairs={{0,1},{1,2},{2,3},{3,0},{4,5},{5,6},{6,7},{7,4},{8,9},{9,10},{10,1... | collective-permute-start | bytes 3145736 | tf_op jit(solution)/shard_map/ppermute | solution.py:251
  51.5 29.9 %collective-permute-start.17 = (bf16[256,2048]{1,0:T(8,128)(2,1)}, bf16[256,2048]{1,0:T(8,128)(2,1)}, u32[]{:S(2)}, u32[]{:S(2)}) collective-permute-start(bf16[256,2048]{1,0:T(8,128)(2,1)} %get-tuple-element.46), channel_id=1, source_target_pairs={{0,8},{1,9},{2,10},{3,11},{4,12},{5,13},{6,14},{7,15},{8,16},{9,17... | collective-permute-start | bytes 3145736 | tf_op jit(solution)/shard_map/ppermute | solution.py:251
  53.0 79.3 %collective-permute-start.11 = (bf16[256,2048]{1,0:T(8,128)(2,1)}, bf16[256,2048]{1,0:T(8,128)(2,1)}, u32[]{:S(2)}, u32[]{:S(2)}) collective-permute-start(bf16[256,2048]{1,0:T(8,128)(2,1)} %collective-permute-done.10.refs_5_), channel_id=1, source_target_pairs={{0,8},{1,9},{2,10},{3,11},{4,12},{5,13},{6,14},{7,15},{8,16},{9,17... | collective-permute-start | bytes 3145736 | tf_op jit(solution)/shard_map/ppermute | solution.py:251
  59.2 73.1 %collective-permute-start.4 = (bf16[256,2048]{1,0:T(8,128)(2,1)}, bf16[256,2048]{1,0:T(8,128)(2,1)}, u32[]{:S(2)}, u32[]{:S(2)}) collective-permute-start(bf16[256,2048]{1,0:T(8,128)(2,1)} %collective-permute-done.3.refs_3_), channel_id=1, source_target_pairs={{0,1},{1,2},{2,3},{3,0},{4,5},{5,6},{6,7},{7,4},{8,9},{9,10},{10,1... | collective-permute-start | bytes 3145736 | tf_op jit(solution)/shard_map/ppermute | solution.py:251
  62.6 70.3 %collective-permute-start.14 = (bf16[256,2048]{1,0:T(8,128)(2,1)}, bf16[256,2048]{1,0:T(8,128)(2,1)}, u32[]{:S(2)}, u32[]{:S(2)}) collective-permute-start(bf16[256,2048]{1,0:T(8,128)(2,1)} %collective-permute-done.13.refs_6_), channel_id=1, source_target_pairs={{0,24},{1,25},{2,26},{3,27},{4,28},{5,29},{6,30},{7,31},{8,0},{9,1... | collective-permute-start | bytes 3145736 | tf_op jit(solution)/shard_map/ppermute | solution.py:251
  69.0 63.9 %collective-permute-start.7 = (bf16[256,2048]{1,0:T(8,128)(2,1)}, bf16[256,2048]{1,0:T(8,128)(2,1)}, u32[]{:S(2)}, u32[]{:S(2)}) collective-permute-start(bf16[256,2048]{1,0:T(8,128)(2,1)} %collective-permute-done.6.refs_4_), channel_id=1, source_target_pairs={{0,3},{1,0},{2,1},{3,2},{4,7},{5,4},{6,5},{7,6},{8,11},{9,8},{10,9... | collective-permute-start | bytes 3145736 | tf_op jit(solution)/shard_map/ppermute | solution.py:251
  81.4 59.7 %collective-permute-start.26 = (f32[2,256,1280]{2,1,0:T(8,128)}, f32[2,256,1280]{2,1,0:T(8,128)S(1)}, u32[]{:S(2)}, u32[]{:S(2)}) collective-permute-start(f32[2,256,1280]{2,1,0:T(8,128)} %get-tuple-element.29.sr), channel_id=1, source_target_pairs={{0,32},{1,33},{2,34},{3,35},{4,36},{5,37},{6,38},{7,39},{8,40},{9,... | collective-permute-start | bytes 7864328 | tf_op jit(solution)/shard_map/ppermute | solution.py:251
  132.3 12.6 %collective-permute-start.25 = (f32[2,256,1024]{2,1,0:T(8,128)}, f32[2,256,1024]{2,1,0:T(8,128)S(1)}, u32[]{:S(2)}, u32[]{:S(2)}) collective-permute-start(f32[2,256,1024]{2,1,0:T(8,128)} %get-tuple-element.27.sr), channel_id=1, source_target_pairs={{0,32},{1,33},{2,34},{3,35},{4,36},{5,37},{6,38},{7,39},{8,40},{9,... | collective-permute-start | bytes 6291464 | tf_op jit(solution)/shard_map/ppermute | solution.py:251
  132.4 19.8 %collective-permute-start.18 = (f32[2,256,1024]{2,1,0:T(8,128)}, f32[2,256,1024]{2,1,0:T(8,128)S(1)}, u32[]{:S(2)}, u32[]{:S(2)}) collective-permute-start(f32[2,256,1024]{2,1,0:T(8,128)} %get-tuple-element.21.sr), channel_id=1, source_target_pairs={{0,32},{1,33},{2,34},{3,35},{4,36},{5,37},{6,38},{7,39},{8,40},{9,... | collective-permute-start | bytes 6291464 | tf_op jit(solution)/shard_map/ppermute | solution.py:251
  141.0 15.5 %collective-permute-start.15 = (f32[2,256,1024]{2,1,0:T(8,128)}, f32[2,256,1024]{2,1,0:T(8,128)S(1)}, u32[]{:S(2)}, u32[]{:S(2)}) collective-permute-start(f32[2,256,1024]{2,1,0:T(8,128)} %get-tuple-element.19.sr), channel_id=1, source_target_pairs={{0,32},{1,33},{2,34},{3,35},{4,36},{5,37},{6,38},{7,39},{8,40},{9,... | collective-permute-start | bytes 6291464 | tf_op jit(solution)/shard_map/ppermute | solution.py:251
  149.7 37.7 %collective-permute-start.27 = (bf16[256,2048]{1,0:T(8,128)(2,1)}, bf16[256,2048]{1,0:T(8,128)(2,1)}, u32[]{:S(2)}, u32[]{:S(2)}) collective-permute-start(bf16[256,2048]{1,0:T(8,128)(2,1)} %get-tuple-element.31), channel_id=1, source_target_pairs={{0,64},{1,65},{2,66},{3,67},{4,68},{5,69},{6,70},{7,71},{8,72},{9,... | collective-permute-start | bytes 3145736 | tf_op jit(solution)/shard_map/ppermute | solution.py:251
  160.7 37.9 %collective-permute-start.19 = (bf16[256,2048]{1,0:T(8,128)(2,1)}, bf16[256,2048]{1,0:T(8,128)(2,1)}, u32[]{:S(2)}, u32[]{:S(2)}) collective-permute-start(bf16[256,2048]{1,0:T(8,128)(2,1)} %get-tuple-element.23), channel_id=1, source_target_pairs={{0,64},{1,65},{2,66},{3,67},{4,68},{5,69},{6,70},{7,71},{8,72},{9,... | collective-permute-start | bytes 3145736 | tf_op jit(solution)/shard_map/ppermute | solution.py:251
  160.9 38.9 %collective-permute-start.30 = (bf16[2,256,768]{2,1,0:T(8,128)(2,1)}, bf16[2,256,768]{2,1,0:T(8,128)(2,1)S(1)}, u32[]{:S(2)}, u32[]{:S(2)}) collective-permute-start(bf16[2,256,768]{2,1,0:T(8,128)(2,1)} %get-tuple-element.33), channel_id=1, source_target_pairs={{0,4},{1,5},{2,6},{3,7},{4,0},{5,1},{6,2},{7,3},{8,12},{9,13},{10,... | collective-permute-start | bytes 2359304 | tf_op jit(solution)/shard_map/ppermute | solution.py:251
  166.4 21.1 %collective-permute-start.32 = (f32[256]{0:T(256)S(1)}, f32[256]{0:T(256)S(1)}, u32[]{:S(2)}, u32[]{:S(2)}) collective-permute-start(f32[256]{0:T(256)S(1)} %add.566), channel_id=1, source_target_pairs={{0,64},{1,65},{2,66},{3,67},{4,68},{5,69},{6,70},{7,71},{8,72},{9,... | collective-permute-start | bytes 3080 | tf_op jit(solution)/shard_map/ppermute | solution.py:251
  187.3 16.1 %collective-permute-start.28 = (bf16[256,2048]{1,0:T(8,128)(2,1)}, bf16[256,2048]{1,0:T(8,128)(2,1)}, u32[]{:S(2)}, u32[]{:S(2)}) collective-permute-start(bf16[256,2048]{1,0:T(8,128)(2,1)} %collective-permute-done.27.refs_4_), channel_id=1, source_target_pairs={{0,32},{1,33},{2,34},{3,35},{4,36},{5,37},{6,38},{7,39},{8,40},{9,... | collective-permute-start | bytes 3145736 | tf_op jit(solution)/shard_map/ppermute | solution.py:251
  187.3 25.5 %collective-permute-start.29 = (bf16[2,256,1024]{2,1,0:T(8,128)(2,1)}, bf16[2,256,1024]{2,1,0:T(8,128)(2,1)}, u32[]{:S(2)}, u32[]{:S(2)}) collective-permute-start(bf16[2,256,1024]{2,1,0:T(8,128)(2,1)} %get-tuple-element.32), channel_id=1, source_target_pairs={{0,4},{1,5},{2,6},{3,7},{4,0},{5,1},{6,2},{7,3},{8,12},{9,13},{10,... | collective-permute-start | bytes 3145736 | tf_op jit(solution)/shard_map/ppermute | solution.py:251
  187.5 47.8 %collective-permute-start.22 = (bf16[2,256,1024]{2,1,0:T(8,128)(2,1)}, bf16[2,256,1024]{2,1,0:T(8,128)(2,1)}, u32[]{:S(2)}, u32[]{:S(2)}) collective-permute-start(bf16[2,256,1024]{2,1,0:T(8,128)(2,1)} %get-tuple-element.25), channel_id=1, source_target_pairs={{0,4},{1,5},{2,6},{3,7},{4,0},{5,1},{6,2},{7,3},{8,12},{9,13},{10,... | collective-permute-start | bytes 3145736 | tf_op jit(solution)/shard_map/ppermute | solution.py:251
  198.6 36.7 %collective-permute-start.20 = (bf16[256,2048]{1,0:T(8,128)(2,1)}, bf16[256,2048]{1,0:T(8,128)(2,1)}, u32[]{:S(2)}, u32[]{:S(2)}) collective-permute-start(bf16[256,2048]{1,0:T(8,128)(2,1)} %collective-permute-done.19.refs_4_), channel_id=1, source_target_pairs={{0,32},{1,33},{2,34},{3,35},{4,36},{5,37},{6,38},{7,39},{8,40},{9,... | collective-permute-start | bytes 3145736 | tf_op jit(solution)/shard_map/ppermute | solution.py:251
  200.7 57.1 %collective-permute-start.21 = (bf16[2,256,1024]{2,1,0:T(8,128)(2,1)}, bf16[2,256,1024]{2,1,0:T(8,128)(2,1)}, u32[]{:S(2)}, u32[]{:S(2)}) collective-permute-start(bf16[2,256,1024]{2,1,0:T(8,128)(2,1)} %get-tuple-element.24), channel_id=1, source_target_pairs={{0,4},{1,5},{2,6},{3,7},{4,0},{5,1},{6,2},{7,3},{8,12},{9,13},{10,... | collective-permute-start | bytes 3145736 | tf_op jit(solution)/shard_map/ppermute | solution.py:251
  (28 other events, 404.2 us)

commit v2 on v1

--- a/solution.py
+++ b/solution.py
@@ -60,31 +60,37 @@
 
 
 def gram_kernel(slabs, local, r0, r1, *refs):
-    xs, (g_ref, s_ref) = refs[:-2], refs[-2:]
+    xs, (own_ref, give_ref, sum_ref, acc) = refs[:-4], refs[-4:]
     i = pl.program_id(0)
     size = r0.shape[1] // slabs
-    g_ref[...] = jnp.zeros_like(g_ref)
+    own_ref[...] = jnp.zeros_like(own_ref)
+    acc[...] = jnp.zeros_like(acc)
     for k, x in enumerate(xs):
 
         @pl.when(i == k)
         def _(k=k, x=x):
             for t in range(slabs):
                 part = pl.ds(t * size, size)
-                for r, left in enumerate((r0, r1)[: 2 if k < 4 else 1]):
-                    g_ref[2 * r + local[t]] += lax.dot_general(
+                for left, to in ((r0, own_ref), (r1, acc))[: 2 if k < 4 else 1]:
+                    to[local[t]] += lax.dot_general(
                         left[:, part],
                         x[:, part],
                         (((1,), (1,)), ((), ())),
                         preferred_element_type=jnp.float32,
                     )
 
-    for r in range(2):
-        s_ref[r] = g_ref[2 * r] + g_ref[2 * r + 1]
-
-
-def gram(local, rooted, partner, xs):
+    sum_ref[0] = own_ref[0] + own_ref[1]
+    sum_ref[1] = acc[0] + acc[1]
+
+    @pl.when(i < 4)
+    def _():
+        give_ref[...] = acc[...].astype(jnp.bfloat16)
+
+
+def gram(local, rooted, partner, xs, skip):
     rows, m = rooted.shape[1], len(xs)
     whole = pl.BlockSpec((256, rows), lambda i, f: (0, 0))
+    last = 3 - skip
     return pl.pallas_call(
         lambda *refs: gram_kernel(local.shape[0], *refs),
         grid_spec=pltpu.PrefetchScalarGridSpec(
@@ -92,61 +98,51 @@
             grid=(m,),
             in_specs=[whole] * (m + 2),
             out_specs=[
-                pl.BlockSpec((4, 256, 256), lambda i, f: (0, 0, i)),
+                pl.BlockSpec((2, 256, 256), lambda i, f: (0, 0, i)),
+                pl.BlockSpec((2, 256, 256), lambda i, f: (0, 0, jnp.clip(i - skip, 0, last))),
                 pl.BlockSpec((2, 256, 256), lambda i, f: (0, 0, i)),
             ],
+            scratch_shapes=[pltpu.VMEM((2, 256, 256), jnp.float32)],
         ),
         out_shape=[
-            pltpu.HBM((4, 256, 256 * m), jnp.float32),
+            pltpu.HBM((2, 256, 256 * m), jnp.float32),
+            pltpu.HBM((2, 256, 256 * (last + 1)), jnp.bfloat16),
             pltpu.HBM((2, 256, 256 * m), jnp.float32),
         ],
         compiler_params=pltpu.CompilerParams(vmem_limit_bytes=VMEM),
         cost_estimate=pl.CostEstimate(
-            flops=2 * 512 * 256 * m * rows, bytes_accessed=4 * m * MIB, transcendentals=0
+            flops=2 * 512 * 256 * m * rows, bytes_accessed=3 * m * MIB, transcendentals=0
         ),
     )(local, rooted, partner, *xs)
 
 
-def mix_kernel(r_ref, g1, s1, sr, tr, *refs):
-    d_ref, u_ref = refs[-2:]
-    other = s1[0]
-    d_ref[0] = (g1[1] + other).astype(jnp.bfloat16)
-    d_ref[1] = (g1[0] + other).astype(jnp.bfloat16)
-    u_ref[...] = (sr[0] + tr[0]).astype(jnp.bfloat16)
-
-
-def mix(pick, g, s, swapped, skip, u):
+def mix_kernel(r_ref, mine, theirs, *refs):
+    refs[-1][...] = (mine[0] + theirs[0]).astype(jnp.bfloat16)
+
+
+def mix(pick, s, swapped, half, parts, u):
     extra = [] if u is None else [u]
-    base = 4 * len(extra)
-    width = 1024 - 256 * skip
+    base = 2 * half
     return pl.pallas_call(
         mix_kernel,
         grid_spec=pltpu.PrefetchScalarGridSpec(
             num_scalar_prefetch=1,
-            grid=(4,),
+            grid=(2,),
             in_specs=[
-                pl.BlockSpec((2, 256, 256), lambda i, r: (1, 0, i)),
-                pl.BlockSpec((1, 256, 256), lambda i, r: (1, 0, i)),
-                pl.BlockSpec((1, 256, 256), lambda i, r: (r[0], 0, i)),
-                pl.BlockSpec((1, 256, 256), lambda i, r: (r[0], 0, i)),
+                pl.BlockSpec((1, 256, 512), lambda i, r: (r[0], 0, i)),
+                pl.BlockSpec((1, 256, 512), lambda i, r: (r[0], 0, i)),
             ]
             + [pl.BlockSpec(memory_space=pl.ANY)] * len(extra),
-            out_specs=[
-                pl.BlockSpec((2, 256, 256), lambda i, r: (0, 0, jnp.maximum(i - skip, 0))),
-                pl.BlockSpec((256, 256), lambda i, r: (0, i + base)),
-            ],
+            out_specs=pl.BlockSpec((256, 512), lambda i, r: (0, i + base)),
         ),
-        out_shape=[
-            pltpu.HBM((2, 256, width), jnp.bfloat16),
-            pltpu.HBM((256, 2048), jnp.bfloat16),
-        ],
-        input_output_aliases={5: 1} if extra else {},
+        out_shape=pltpu.HBM((256, 1024 * parts), jnp.bfloat16),
+        input_output_aliases={3: 0} if extra else {},
         compiler_params=pltpu.CompilerParams(vmem_limit_bytes=VMEM),
-        cost_estimate=pl.CostEstimate(flops=MIB, bytes_accessed=8 * MIB, transcendentals=0),
-    )(pick, g, swapped, s, swapped, *extra)
-
-
-def final_kernel(first, pick, cols, g0, s0, mine, theirs, dr, *refs):
+        cost_estimate=pl.CostEstimate(flops=MIB, bytes_accessed=3 * MIB, transcendentals=0),
+    )(pick, s, swapped, *extra)
+
+
+def final_kernel(first, pick, cols, g0, s0, mine, theirs, dr, er, *refs):
     out, buf, sems = refs[-3:]
     n = pl.program_id(0)
     slot = lax.rem(n, 2)
@@ -185,8 +181,9 @@
 
     @pl.when(n >= (1 if first else 0))
     def _():
-        buf[slot, 1, 0] = dr[0].astype(jnp.float32) + rest
-        buf[slot, 1, 1] = dr[1].astype(jnp.float32) + rest
+        other = er[0].astype(jnp.float32) + er[1].astype(jnp.float32) + rest
+        buf[slot, 1, 0] = dr[1].astype(jnp.float32) + other
+        buf[slot, 1, 1] = dr[0].astype(jnp.float32) + other
 
     for copy in copies(n, slot):
         copy.start()
@@ -198,7 +195,7 @@
                 copy.wait()
 
 
-def final(pick, cols, g, swapped, mine, theirs, half, dr, pen, out, total):
+def final(pick, cols, g, swapped, mine, theirs, half, dr, er, pen, out, total):
     first = out is None
     skip = 1 if first else 0
     base = 4 * half
@@ -221,8 +218,8 @@
                 pl.BlockSpec((1, 256, 256), lambda n, p, c: (0, 0, n)),
                 pl.BlockSpec((256, 256), lambda n, p, c: (0, n + base)),
                 pl.BlockSpec((256, 256), lambda n, p, c: (0, n + base)),
-                pl.BlockSpec((2, 256, 256), lambda n, p, c: (0, 0, jnp.maximum(n - skip, 0))),
             ]
+            + [pl.BlockSpec((2, 256, 256), lambda n, p, c: (0, 0, jnp.maximum(n - skip, 0)))] * 2
             + extra_specs,
             out_specs=pl.BlockSpec(memory_space=pl.ANY),
             scratch_shapes=[
@@ -231,10 +228,10 @@
             ],
         ),
         out_shape=pltpu.HBM((2, 256, total), jnp.float32),
-        input_output_aliases={} if first else {7: 0},
+        input_output_aliases={} if first else {8: 0},
         compiler_params=pltpu.CompilerParams(vmem_limit_bytes=VMEM),
         cost_estimate=pl.CostEstimate(flops=MIB, bytes_accessed=9 * MIB, transcendentals=0),
-    )(pick, cols, g, swapped, mine, theirs, dr, *extra)
+    )(pick, cols, g, swapped, mine, theirs, dr, er, *extra)
 
 
 def body(design, weights, response, fold_of, smoothing):
@@ -295,19 +292,23 @@
 
     pen = jnp.kron(jnp.diag(smoothing), second_differences(TERM))
 
+    places = ((0, 0, 2), (0, 1, 2), (1, 0, 1), (2, 0, 1))
     state, mine, theirs, u = [], [], [], None
     for n, xs in enumerate(work):
-        g, s = gram(local, rooted, partner, xs)
+        message, half, parts = places[n]
+        g, give, s = gram(local, rooted, partner, xs, 1 if n == 0 else 0)
         swapped = send(s, CORE)
-        give, u = mix(pick, g, s, swapped, 1 if n == 0 else 0, u)
         dr = send(give, PARTNER)
-        state.append((g, swapped, dr))
-        if n % 2 == 1:
+        er = send(dr, CORE)
+        u = mix(pick, s, swapped, half, parts, u)
+        state.append((g, swapped, dr, er))
+        if half == parts - 1:
             mine.append(send(u, ACROSS))
             theirs.append(send(mine[-1], CORE))
             u = None
     out = None
-    for n, (g, swapped, dr) in enumerate(state):
+    for n, (g, swapped, dr, er) in enumerate(state):
+        message, half, _ = places[n]
         cols = []
         for dy, dz, colour in where[n]:
             y, z = lax.rem(me_y + dy + 4, 4), lax.rem(me_z + dz + 4, 4)
@@ -315,7 +316,7 @@
                 cols.append((y * 8 + l * 4 + z) * 2 + colour)
         cols = jnp.stack(cols).astype(jnp.int32)
         out = final(
-            pick, cols, g, swapped, mine[n // 2], theirs[n // 2], n % 2, dr, pen, out, width
+            pick, cols, g, swapped, mine[message], theirs[message], half, dr, er, pen, out, width
         )
     return (out, complement_rhs)
 

time: 267 us -> 260 us (0.974); the launches traced: 263 us -> 259 us
  starting transfers between devices: 71.3 us -> 88.9 us
  waiting for transfers between devices: 103 us -> 89.3 us
  Pallas kernels: 70.3 us -> 59.6 us
  local copies, waits for them, and re-layouts: 10.4 us -> 14.1 us
    ppermute x33 -> x39, starting transfers between devices: 71.3 us -> 88.9 us  [send(): return lax.ppermute(x, AXES, pairs)]
    ppermute x33 -> x39, waiting for transfers between devices: 103 us -> 89.3 us  [send(): return lax.ppermute(x, AXES, pairs)]
    pallas_call x4, Pallas kernels: 17 us -> 6.3 us  [mix(): pl.pallas_call(mix_kernel, grid_spec=pltpu.PrefetchScalarGridSpec(num_sca...]
    unnamed x55 -> x61, local copies, waits for them, and re-layouts: 9.39 us -> 12 us
  transfers between devices with their start and end apart: 33 -> 39, of which waited for: 16 -> 12; matrix products, arithmetic and copies ran while one was open for 3% -> 3% of each run, Pallas kernels for 25% -> 21%
where the time goes in v2:
time: 260 us; the launch traced here: 259 us
  waiting for transfers between devices  89.3 us (34%)
  starting transfers between devices  88.9 us (34%)
  Pallas kernels  59.6 us (23%)
  local copies, waits for them, and re-layouts  14.1 us (5%)
  other arithmetic  5.55 us (2%)
    ppermute x39, waiting for transfers between devices, send(): return lax.ppermute(x, AXES, pairs)  89.3 us
    ppermute x39, starting transfers between devices, send(): return lax.ppermute(x, AXES, pairs)  88.9 us
    pallas_call x4, Pallas kernels, gram(): pl.pallas_call(lambda *refs: gram_kernel(local.shape[0], *refs), grid_spe...  31 us
    pallas_call x4, Pallas kernels, final(): pl.pallas_call(lambda *refs: final_kernel(first, *refs), grid_spec=pltpu....  22.3 us
    unnamed x61, local copies, waits for them, and re-layouts  12 us
    pallas_call x4, Pallas kernels, mix(): pl.pallas_call(mix_kernel, grid_spec=pltpu.PrefetchScalarGridSpec(num_sca...  6.3 us
  transfers between devices with their start and end apart: 39, of which 12 were waited for; matrix products, arithmetic and copies ran while one was open for 3% of the time, Pallas kernels for 21%

profile of v2, /device:TPU:1, one launch (start us, length us, event | category | flops | bytes accessed | tf_op | source)
XLA Modules:
  0.0 259.1 jit_solution(15250116142840896386)
XLA Ops:
  2.6 4.6 %collective-permute-start.8 = (bf16[128,2048]{1,0:T(8,128)(2,1)S(1)}, bf16[128,2048]{1,0:T(8,128)(2,1)S(1)}, u32[]{:S(2)}, u32[]{:S(2)}) collective-permute-start(bf16[128,2048]{1,0:T(8,128)(2,1)S(1)} %get-tuple-element.32), channel_id=1, source_target_pairs={{0,1},{1,2},{2,3},{3,0},{4,5},{5,6},{6,7},{7,4},{8,9},{9,10},{10,1... | collective-permute-start | bytes 1572872 | tf_op jit(solution)/shard_map/ppermute | solution.py:248
  7.2 2.7 %collective-permute-start.1 = (bf16[128,2048]{1,0:T(8,128)(2,1)S(1)}, bf16[128,2048]{1,0:T(8,128)(2,1)}, u32[]{:S(2)}, u32[]{:S(2)}) collective-permute-start(bf16[128,2048]{1,0:T(8,128)(2,1)S(1)} %get-tuple-element.33), channel_id=1, source_target_pairs={{0,8},{1,9},{2,10},{3,11},{4,12},{5,13},{6,14},{7,15},{8,16},{9,17... | collective-permute-start | bytes 1572872 | tf_op jit(solution)/shard_map/ppermute | solution.py:248
  11.2 6.6 %collective-permute-done.8 = bf16[128,2048]{1,0:T(8,128)(2,1)S(1)} collective-permute-done((bf16[128,2048]{1,0:T(8,128)(2,1)S(1)}, bf16[128,2048]{1,0:T(8,128)(2,1)S(1)}, u32[]{:S(2)}, u32[]{:S(2)}) %collective-permute-start.8) | collective-permute-done | bytes 524320 | tf_op jit(solution)/shard_map/ppermute | solution.py:248
  17.7 2.9 %collective-permute-done.9 = bf16[128,2048]{1,0:T(8,128)(2,1)S(1)} collective-permute-done((bf16[128,2048]{1,0:T(8,128)(2,1)S(1)}, bf16[128,2048]{1,0:T(8,128)(2,1)S(1)}, u32[]{:S(2)}, u32[]{:S(2)}) %collective-permute-start.9) | collective-permute-done | bytes 524320 | tf_op jit(solution)/shard_map/ppermute | solution.py:248
  26.7 3.8 %collective-permute-done.12 = bf16[128,2048]{1,0:T(8,128)(2,1)S(1)} collective-permute-done((bf16[128,2048]{1,0:T(8,128)(2,1)}, bf16[128,2048]{1,0:T(8,128)(2,1)S(1)}, u32[]{:S(2)}, u32[]{:S(2)}) %collective-permute-start.12) | collective-permute-done | bytes 524320 | tf_op jit(solution)/shard_map/ppermute | solution.py:248
  38.3 9.0 %collective-permute-done.10.refs_5_ = bf16[256,2048]{1,0:T(8,128)(2,1)} collective-permute-done((bf16[256,2048]{1,0:T(8,128)(2,1)S(1)}, bf16[256,2048]{1,0:T(8,128)(2,1)}, u32[]{:S(2)}, u32[]{:S(2)}) %collective-permute-start.10) | collective-permute-done | bytes 1048608 | tf_op jit(solution)/shard_map/ppermute | solution.py:248
  47.6 5.3 %collective-permute-done.3.refs_3_ = bf16[256,2048]{1,0:T(8,128)(2,1)S(1)} collective-permute-done((bf16[256,2048]{1,0:T(8,128)(2,1)S(1)}, bf16[256,2048]{1,0:T(8,128)(2,1)S(1)}, u32[]{:S(2)}, u32[]{:S(2)}) %collective-permute-start.3) | collective-permute-done | bytes 1048608 | tf_op jit(solution)/shard_map/ppermute | solution.py:248
  56.5 7.7 %shard_map.73 = (f32[2,256,1280]{2,1,0:T(8,128)}, bf16[2,256,768]{2,1,0:T(8,128)(2,1)}, f32[2,256,1280]{2,1,0:T(8,128)}) custom-call(s32[8]{0:T(128)S(1)} %get-tuple-element.29.refs_0_, bf16[256,2048]{1,0:T(8,128)(2,1)S(1)} %fusion.refs_1_.refs_3_, bf16[256,2048]{1,0:T(8,128)(2,1)} %collective-permute-done.refs_2_.refs_7_, ...), custom_call_target="tpu_custom_call" | custom-call | flops 2684354560 | bytes 15728640 | tf_op jit(solution)/shard_map/pallas_call | solution.py:94
  64.2 9.8 %collective-permute-done.13.refs_6_ = bf16[256,2048]{1,0:T(8,128)(2,1)} collective-permute-done((bf16[256,2048]{1,0:T(8,128)(2,1)}, bf16[256,2048]{1,0:T(8,128)(2,1)}, u32[]{:S(2)}, u32[]{:S(2)}) %collective-permute-start.13) | collective-permute-done | bytes 1048608 | tf_op jit(solution)/shard_map/ppermute | solution.py:248
  74.0 9.1 %collective-permute-start.30 = (f32[2,256,1280]{2,1,0:T(8,128)}, f32[2,256,1280]{2,1,0:T(8,128)S(1)}, u32[]{:S(2)}, u32[]{:S(2)}) collective-permute-start(f32[2,256,1280]{2,1,0:T(8,128)} %get-tuple-element.22.mine), channel_id=1, source_target_pairs={{0,32},{1,33},{2,34},{3,35},{4,36},{5,37},{6,38},{7,39},{8,40},{9,... | collective-permute-start | bytes 7864328 | tf_op jit(solution)/shard_map/ppermute | solution.py:248
  83.1 3.0 %collective-permute-start.14 = (bf16[256,2048]{1,0:T(8,128)(2,1)}, bf16[256,2048]{1,0:T(8,128)(2,1)S(1)}, u32[]{:S(2)}, u32[]{:S(2)}) collective-permute-start(bf16[256,2048]{1,0:T(8,128)(2,1)} %collective-permute-done.13.refs_6_), channel_id=1, source_target_pairs={{0,24},{1,25},{2,26},{3,27},{4,28},{5,29},{6,30},{7,31},{8,0},{9,1... | collective-permute-start | bytes 3145736 | tf_op jit(solution)/shard_map/ppermute | solution.py:248
  86.1 2.6 %collective-permute-start.7 = (bf16[256,2048]{1,0:T(8,128)(2,1)}, bf16[256,2048]{1,0:T(8,128)(2,1)S(1)}, u32[]{:S(2)}, u32[]{:S(2)}) collective-permute-start(bf16[256,2048]{1,0:T(8,128)(2,1)} %collective-permute-done.6.refs_4_), channel_id=1, source_target_pairs={{0,3},{1,0},{2,1},{3,2},{4,7},{5,4},{6,5},{7,6},{8,11},{9,8},{10,9... | collective-permute-start | bytes 3145736 | tf_op jit(solution)/shard_map/ppermute | solution.py:248
  89.9 7.6 %shard_map.72 = (f32[2,256,1024]{2,1,0:T(8,128)}, bf16[2,256,1024]{2,1,0:T(8,128)(2,1)}, f32[2,256,1024]{2,1,0:T(8,128)}) custom-call(s32[8]{0:T(128)S(1)} %get-tuple-element.29.refs_0_, bf16[256,2048]{1,0:T(8,128)(2,1)S(1)} %copy-done.2, bf16[256,2048]{1,0:T(8,128)(2,1)} %collective-permute-done.refs_2_.refs_7_, bf16[256,2048]{1,0:T(8,128)(2,1)S(1)} %copy-done.16, ...), custom_call_target="tpu_custom_call" | custom-call | flops 2147483648 | bytes 12582912 | tf_op jit(solution)/shard_map/pallas_call | solution.py:94
  97.5 5.0 %collective-permute-start.29 = (f32[2,256,1024]{2,1,0:T(8,128)}, f32[2,256,1024]{2,1,0:T(8,128)S(1)}, u32[]{:S(2)}, u32[]{:S(2)}) collective-permute-start(f32[2,256,1024]{2,1,0:T(8,128)} %get-tuple-element.21.mine), channel_id=1, source_target_pairs={{0,32},{1,33},{2,34},{3,35},{4,36},{5,37},{6,38},{7,39},{8,40},{9,... | collective-permute-start | bytes 6291464 | tf_op jit(solution)/shard_map/ppermute | solution.py:248
  102.6 8.2 %shard_map.70 = (f32[2,256,1024]{2,1,0:T(8,128)}, bf16[2,256,1024]{2,1,0:T(8,128)(2,1)}, f32[2,256,1024]{2,1,0:T(8,128)}) custom-call(s32[8]{0:T(128)S(1)} %get-tuple-element.29.refs_0_, bf16[256,2048]{1,0:T(8,128)(2,1)S(1)} %copy-done.2, bf16[256,2048]{1,0:T(8,128)(2,1)} %collective-permute-done.refs_2_.refs_7_, ...), custom_call_target="tpu_custom_call" | custom-call | flops 2147483648 | bytes 12582912 | tf_op jit(solution)/shard_map/pallas_call | solution.py:94
  113.0 7.5 %shard_map.68 = (f32[2,256,1024]{2,1,0:T(8,128)}, bf16[2,256,1024]{2,1,0:T(8,128)(2,1)}, f32[2,256,1024]{2,1,0:T(8,128)}) custom-call(s32[8]{0:T(128)S(1)} %get-tuple-element.29.refs_0_, bf16[256,2048]{1,0:T(8,128)(2,1)S(1)} %copy-done.2, bf16[256,2048]{1,0:T(8,128)(2,1)} %collective-permute-done.refs_2_.refs_7_, ...), custom_call_target="tpu_custom_call" | custom-call | flops 2147483648 | bytes 12582912 | tf_op jit(solution)/shard_map/pallas_call | solution.py:94
  121.3 9.3 %collective-permute-done.35.refs_6_ = bf16[2,256,768]{2,1,0:T(8,128)(2,1)S(1)} collective-permute-done((bf16[2,256,768]{2,1,0:T(8,128)(2,1)}, bf16[2,256,768]{2,1,0:T(8,128)(2,1)S(1)}, u32[]{:S(2)}, u32[]{:S(2)}) %collective-permute-start.35) | collective-permute-done | bytes 786464 | tf_op jit(solution)/shard_map/ppermute | solution.py:248
  136.2 2.5 collective-permute-start.31
  141.4 4.0 %collective-permute-done.38 = f32[256]{0:T(256)S(1)} collective-permute-done((f32[256]{0:T(256)S(1)}, f32[256]{0:T(256)S(1)}, u32[]{:S(2)}, u32[]{:S(2)}) %collective-permute-start.38) | collective-permute-done | bytes 1056 | tf_op jit(solution)/shard_map/ppermute | solution.py:248
  147.2 15.4 %collective-permute-done.31.refs_4_ = bf16[256,2048]{1,0:T(8,128)(2,1)S(1)} collective-permute-done((bf16[256,2048]{1,0:T(8,128)(2,1)}, bf16[256,2048]{1,0:T(8,128)(2,1)S(1)}, u32[]{:S(2)}, u32[]{:S(2)}) %collective-permute-start.31) | collective-permute-done | bytes 1048608 | tf_op jit(solution)/shard_map/ppermute | solution.py:248
  164.1 2.2 shard_map.71
  166.3 2.5 collective-permute-start.23
  171.0 18.0 %collective-permute-done.25.refs_6_ = bf16[2,256,1024]{2,1,0:T(8,128)(2,1)} collective-permute-done((bf16[2,256,1024]{2,1,0:T(8,128)(2,1)}, bf16[2,256,1024]{2,1,0:T(8,128)(2,1)}, u32[]{:S(2)}, u32[]{:S(2)}) %collective-permute-start.25) | collective-permute-done | bytes 1048608 | tf_op jit(solution)/shard_map/ppermute | solution.py:248
  189.0 18.0 %collective-permute-start.34 = (bf16[2,256,1024]{2,1,0:T(8,128)(2,1)}, bf16[2,256,1024]{2,1,0:T(8,128)(2,1)}, u32[]{:S(2)}, u32[]{:S(2)}) collective-permute-start(bf16[2,256,1024]{2,1,0:T(8,128)(2,1)} %collective-permute-done.33.refs_6_), channel_id=1, source_target_pairs={{0,32},{1,33},{2,34},{3,35},{4,36},{5,37},{6,38},{7,39},{8,40},{9,... | collective-permute-start | bytes 3145736 | tf_op jit(solution)/shard_map/ppermute | solution.py:248
  207.0 4.3 %collective-permute-done.18.refs_6_ = bf16[2,256,1024]{2,1,0:T(8,128)(2,1)S(1)} collective-permute-done((bf16[2,256,1024]{2,1,0:T(8,128)(2,1)}, bf16[2,256,1024]{2,1,0:T(8,128)(2,1)S(1)}, u32[]{:S(2)}, u32[]{:S(2)}) %collective-permute-start.18) | collective-permute-done | bytes 1048608 | tf_op jit(solution)/shard_map/ppermute | solution.py:248
  211.4 9.2 %collective-permute-start.26 = (bf16[2,256,1024]{2,1,0:T(8,128)(2,1)}, bf16[2,256,1024]{2,1,0:T(8,128)(2,1)}, u32[]{:S(2)}, u32[]{:S(2)}) collective-permute-start(bf16[2,256,1024]{2,1,0:T(8,128)(2,1)} %collective-permute-done.25.refs_6_), channel_id=1, source_target_pairs={{0,32},{1,33},{2,34},{3,35},{4,36},{5,37},{6,38},{7,39},{8,40},{9,... | collective-permute-start | bytes 3145736 | tf_op jit(solution)/shard_map/ppermute | solution.py:248
  220.6 5.7 %collective-permute-start.19 = (bf16[2,256,1024]{2,1,0:T(8,128)(2,1)S(1)}, bf16[2,256,1024]{2,1,0:T(8,128)(2,1)}, u32[]{:S(2)}, u32[]{:S(2)}) collective-permute-start(bf16[2,256,1024]{2,1,0:T(8,128)(2,1)S(1)} %collective-permute-done.18.refs_6_), channel_id=1, source_target_pairs={{0,32},{1,33},{2,34},{3,35},{4,36},{5,37},{6,38},{7,39},{8,40},{9,... | collective-permute-start | bytes 3145736 | tf_op jit(solution)/shard_map/ppermute | solution.py:248
  226.6 5.3 %collective-permute-start.24 = (bf16[256,1024]{1,0:T(8,128)(2,1)}, bf16[256,1024]{1,0:T(8,128)(2,1)}, u32[]{:S(2)}, u32[]{:S(2)}) collective-permute-start(bf16[256,1024]{1,0:T(8,128)(2,1)} %collective-permute-done.23.refs_4_), channel_id=1, source_target_pairs={{0,32},{1,33},{2,34},{3,35},{4,36},{5,37},{6,38},{7,39},{8,40},{9,... | collective-permute-start | bytes 1572872 | tf_op jit(solution)/shard_map/ppermute | solution.py:248
  236.5 5.7 %shard_map.76.refs_8_ = f32[2,256,8192]{2,1,0:T(8,128)} custom-call(s32[1]{0:T(128)} %bitcast.r_ref.refs_0_, s32[16]{0:T(128)S(1)} %stack.280.refs_1_, f32[2,256,1280]{2,1,0:T(8,128)} %get-tuple-element.24.refs_2_.refs_9_, f32[2,256,1280]{2,1,0:T(8,128)} %copy-done, bf16[256,2048]{1,0:T(8,128)(2,1)S(1)} %collective-permute-done.31.refs_4_, ...), custom_call_target="tpu_custom_call" | custom-call | flops 1048576 | bytes 9437184 | tf_op jit(solution)/shard_map/pallas_call | solution.py:211
  242.2 5.7 %shard_map.77.refs_8_ = f32[2,256,8192]{2,1,0:T(8,128)} custom-call(s32[1]{0:T(128)} %bitcast.r_ref.refs_0_, s32[16]{0:T(128)S(1)} %stack.263.refs_1_, f32[2,256,1024]{2,1,0:T(8,128)} %get-tuple-element.20.refs_2_, f32[2,256,1024]{2,1,0:T(8,128)} %copy-done.4, bf16[256,2048]{1,0:T(8,128)(2,1)S(1)} %collective-permute-done.31.refs_4_, ...), custom_call_target="tpu_custom_call", output_to_operand_aliasing={{}: (8, {})} | custom-call | flops 1048576 | bytes 9437184 | tf_op jit(solution)/shard_map/pallas_call | solution.py:211
  247.9 5.6 %shard_map.78.refs_8_ = f32[2,256,8192]{2,1,0:T(8,128)} custom-call(s32[1]{0:T(128)} %bitcast.r_ref.refs_0_, s32[16]{0:T(128)S(1)} %stack.246.refs_1_, f32[2,256,1024]{2,1,0:T(8,128)S(1)} %copy-done.6, f32[2,256,1024]{2,1,0:T(8,128)} %collective-permute-done.22.theirs.refs_3_, ...), custom_call_target="tpu_custom_call", output_to_operand_aliasing={{}: (8, {})} | custom-call | flops 1048576 | bytes 9437184 | tf_op jit(solution)/shard_map/pallas_call | solution.py:211
  253.5 5.3 %shard_map.79 = f32[2,256,8192]{2,1,0:T(8,128)} custom-call(s32[1]{0:T(128)} %bitcast.r_ref.refs_0_, s32[16]{0:T(128)S(1)} %stack.229.refs_1_, f32[2,256,1024]{2,1,0:T(8,128)S(1)} %copy-done.7, f32[2,256,1024]{2,1,0:T(8,128)} %collective-permute-done.15.theirs.refs_3_, ...), custom_call_target="tpu_custom_call", output_to_operand_aliasing={{}: (8, {})} | custom-call | flops 1048576 | bytes 9437184 | tf_op jit(solution)/shard_map/pallas_call | solution.py:211
  (147 shorter events, 43.6 us)
Async XLA Ops:
  2.6 15.2 %collective-permute-start.8 = (bf16[128,2048]{1,0:T(8,128)(2,1)S(1)}, bf16[128,2048]{1,0:T(8,128)(2,1)S(1)}, u32[]{:S(2)}, u32[]{:S(2)}) collective-permute-start(bf16[128,2048]{1,0:T(8,128)(2,1)S(1)} %get-tuple-element.32), channel_id=1, source_target_pairs={{0,1},{1,2},{2,3},{3,0},{4,5},{5,6},{6,7},{7,4},{8,9},{9,10},{10,1... | collective-permute-start | bytes 1572872 | tf_op jit(solution)/shard_map/ppermute | solution.py:248
  7.2 16.2 %collective-permute-start.1 = (bf16[128,2048]{1,0:T(8,128)(2,1)S(1)}, bf16[128,2048]{1,0:T(8,128)(2,1)}, u32[]{:S(2)}, u32[]{:S(2)}) collective-permute-start(bf16[128,2048]{1,0:T(8,128)(2,1)S(1)} %get-tuple-element.33), channel_id=1, source_target_pairs={{0,8},{1,9},{2,10},{3,11},{4,12},{5,13},{6,14},{7,15},{8,16},{9,17... | collective-permute-start | bytes 1572872 | tf_op jit(solution)/shard_map/ppermute | solution.py:248
  9.9 26.3 %collective-permute-start = (bf16[256,2048]{1,0:T(8,128)(2,1)S(1)}, bf16[256,2048]{1,0:T(8,128)(2,1)}, u32[]{:S(2)}, u32[]{:S(2)}) collective-permute-start(bf16[256,2048]{1,0:T(8,128)(2,1)S(1)} %fusion.refs_1_.refs_3_), channel_id=1, source_target_pairs={{0,4},{1,5},{2,6},{3,7},{4,0},{5,1},{6,2},{7,3},{8,12},{9,13},{10,... | collective-permute-start | bytes 3145736 | tf_op jit(solution)/shard_map/ppermute | solution.py:248
  20.8 26.5 %collective-permute-start.10 = (bf16[256,2048]{1,0:T(8,128)(2,1)S(1)}, bf16[256,2048]{1,0:T(8,128)(2,1)}, u32[]{:S(2)}, u32[]{:S(2)}) collective-permute-start(bf16[256,2048]{1,0:T(8,128)(2,1)S(1)} %pad_maximum_fusion.4.refs_5_), channel_id=1, source_target_pairs={{0,8},{1,9},{2,10},{3,11},{4,12},{5,13},{6,14},{7,15},{8,16},{9,17... | collective-permute-start | bytes 3145736 | tf_op jit(solution)/shard_map/ppermute | solution.py:248
  26.4 26.5 %collective-permute-start.3 = (bf16[256,2048]{1,0:T(8,128)(2,1)S(1)}, bf16[256,2048]{1,0:T(8,128)(2,1)S(1)}, u32[]{:S(2)}, u32[]{:S(2)}) collective-permute-start(bf16[256,2048]{1,0:T(8,128)(2,1)S(1)} %pad_maximum_fusion.2.refs_4_), channel_id=1, source_target_pairs={{0,1},{1,2},{2,3},{3,0},{4,5},{5,6},{6,7},{7,4},{8,9},{9,10},{10,1... | collective-permute-start | bytes 3145736 | tf_op jit(solution)/shard_map/ppermute | solution.py:248
  30.4 22.5 %collective-permute-start.28 = (bf16[256,2048]{1,0:T(8,128)(2,1)S(1)}, bf16[256,2048]{1,0:T(8,128)(2,1)S(1)}, u32[]{:S(2)}, u32[]{:S(2)}) collective-permute-start(bf16[256,2048]{1,0:T(8,128)(2,1)S(1)} %pad_maximum_fusion.4.refs_5_), channel_id=1, source_target_pairs={{0,24},{1,25},{2,26},{3,27},{4,28},{5,29},{6,30},{7,31},{8,0},{9,1... | collective-permute-start | bytes 3145736 | tf_op jit(solution)/shard_map/ppermute | solution.py:248
  32.4 20.6 %collective-permute-start.27 = (bf16[256,2048]{1,0:T(8,128)(2,1)S(1)}, bf16[256,2048]{1,0:T(8,128)(2,1)S(1)}, u32[]{:S(2)}, u32[]{:S(2)}) collective-permute-start(bf16[256,2048]{1,0:T(8,128)(2,1)S(1)} %pad_maximum_fusion.2.refs_4_), channel_id=1, source_target_pairs={{0,3},{1,0},{2,1},{3,2},{4,7},{5,4},{6,5},{7,6},{8,11},{9,8},{10,9... | collective-permute-start | bytes 3145736 | tf_op jit(solution)/shard_map/ppermute | solution.py:248
  36.2 37.7 %collective-permute-start.13 = (bf16[256,2048]{1,0:T(8,128)(2,1)}, bf16[256,2048]{1,0:T(8,128)(2,1)}, u32[]{:S(2)}, u32[]{:S(2)}) collective-permute-start(bf16[256,2048]{1,0:T(8,128)(2,1)} %get-tuple-element.38), channel_id=1, source_target_pairs={{0,24},{1,25},{2,26},{3,27},{4,28},{5,29},{6,30},{7,31},{8,0},{9,1... | collective-permute-start | bytes 3145736 | tf_op jit(solution)/shard_map/ppermute | solution.py:248
  47.4 35.7 %collective-permute-start.6 = (bf16[256,2048]{1,0:T(8,128)(2,1)}, bf16[256,2048]{1,0:T(8,128)(2,1)}, u32[]{:S(2)}, u32[]{:S(2)}) collective-permute-start(bf16[256,2048]{1,0:T(8,128)(2,1)} %get-tuple-element.37), channel_id=1, source_target_pairs={{0,3},{1,0},{2,1},{3,2},{4,7},{5,4},{6,5},{7,6},{8,11},{9,8},{10,9... | collective-permute-start | bytes 3145736 | tf_op jit(solution)/shard_map/ppermute | solution.py:248
  52.9 30.2 %collective-permute-start.20 = (bf16[256,2048]{1,0:T(8,128)(2,1)}, bf16[256,2048]{1,0:T(8,128)(2,1)}, u32[]{:S(2)}, u32[]{:S(2)}) collective-permute-start(bf16[256,2048]{1,0:T(8,128)(2,1)} %get-tuple-element.37), channel_id=1, source_target_pairs={{0,1},{1,2},{2,3},{3,0},{4,5},{5,6},{6,7},{7,4},{8,9},{9,10},{10,1... | collective-permute-start | bytes 3145736 | tf_op jit(solution)/shard_map/ppermute | solution.py:248
  52.9 33.2 %collective-permute-start.21 = (bf16[256,2048]{1,0:T(8,128)(2,1)}, bf16[256,2048]{1,0:T(8,128)(2,1)}, u32[]{:S(2)}, u32[]{:S(2)}) collective-permute-start(bf16[256,2048]{1,0:T(8,128)(2,1)} %get-tuple-element.38), channel_id=1, source_target_pairs={{0,8},{1,9},{2,10},{3,11},{4,12},{5,13},{6,14},{7,15},{8,16},{9,17... | collective-permute-start | bytes 3145736 | tf_op jit(solution)/shard_map/ppermute | solution.py:248
  55.2 42.3 %collective-permute-start.11 = (bf16[256,2048]{1,0:T(8,128)(2,1)}, bf16[256,2048]{1,0:T(8,128)(2,1)}, u32[]{:S(2)}, u32[]{:S(2)}) collective-permute-start(bf16[256,2048]{1,0:T(8,128)(2,1)} %collective-permute-done.10.refs_5_), channel_id=1, source_target_pairs={{0,8},{1,9},{2,10},{3,11},{4,12},{5,13},{6,14},{7,15},{8,16},{9,17... | collective-permute-start | bytes 3145736 | tf_op jit(solution)/shard_map/ppermute | solution.py:248
  74.0 58.0 %collective-permute-start.30 = (f32[2,256,1280]{2,1,0:T(8,128)}, f32[2,256,1280]{2,1,0:T(8,128)S(1)}, u32[]{:S(2)}, u32[]{:S(2)}) collective-permute-start(f32[2,256,1280]{2,1,0:T(8,128)} %get-tuple-element.22.mine), channel_id=1, source_target_pairs={{0,32},{1,33},{2,34},{3,35},{4,36},{5,37},{6,38},{7,39},{8,40},{9,... | collective-permute-start | bytes 7864328 | tf_op jit(solution)/shard_map/ppermute | solution.py:248
  83.1 27.7 %collective-permute-start.4 = (bf16[256,2048]{1,0:T(8,128)(2,1)S(1)}, bf16[256,2048]{1,0:T(8,128)(2,1)S(1)}, u32[]{:S(2)}, u32[]{:S(2)}) collective-permute-start(bf16[256,2048]{1,0:T(8,128)(2,1)S(1)} %copy-done.16), channel_id=1, source_target_pairs={{0,1},{1,2},{2,3},{3,0},{4,5},{5,6},{6,7},{7,4},{8,9},{9,10},{10,1... | collective-permute-start | bytes 3145736 | tf_op jit(solution)/shard_map/ppermute | solution.py:248
  83.1 27.7 %collective-permute-start.14 = (bf16[256,2048]{1,0:T(8,128)(2,1)}, bf16[256,2048]{1,0:T(8,128)(2,1)S(1)}, u32[]{:S(2)}, u32[]{:S(2)}) collective-permute-start(bf16[256,2048]{1,0:T(8,128)(2,1)} %collective-permute-done.13.refs_6_), channel_id=1, source_target_pairs={{0,24},{1,25},{2,26},{3,27},{4,28},{5,29},{6,30},{7,31},{8,0},{9,1... | collective-permute-start | bytes 3145736 | tf_op jit(solution)/shard_map/ppermute | solution.py:248
  86.1 26.9 %collective-permute-start.7 = (bf16[256,2048]{1,0:T(8,128)(2,1)}, bf16[256,2048]{1,0:T(8,128)(2,1)S(1)}, u32[]{:S(2)}, u32[]{:S(2)}) collective-permute-start(bf16[256,2048]{1,0:T(8,128)(2,1)} %collective-permute-done.6.refs_4_), channel_id=1, source_target_pairs={{0,3},{1,0},{2,1},{3,2},{4,7},{5,4},{6,5},{7,6},{8,11},{9,8},{10,9... | collective-permute-start | bytes 3145736 | tf_op jit(solution)/shard_map/ppermute | solution.py:248
  97.5 36.1 %collective-permute-start.29 = (f32[2,256,1024]{2,1,0:T(8,128)}, f32[2,256,1024]{2,1,0:T(8,128)S(1)}, u32[]{:S(2)}, u32[]{:S(2)}) collective-permute-start(f32[2,256,1024]{2,1,0:T(8,128)} %get-tuple-element.21.mine), channel_id=1, source_target_pairs={{0,32},{1,33},{2,34},{3,35},{4,36},{5,37},{6,38},{7,39},{8,40},{9,... | collective-permute-start | bytes 6291464 | tf_op jit(solution)/shard_map/ppermute | solution.py:248
  110.8 36.1 %collective-permute-start.22 = (f32[2,256,1024]{2,1,0:T(8,128)}, f32[2,256,1024]{2,1,0:T(8,128)}, u32[]{:S(2)}, u32[]{:S(2)}) collective-permute-start(f32[2,256,1024]{2,1,0:T(8,128)} %get-tuple-element.18.mine), channel_id=1, source_target_pairs={{0,32},{1,33},{2,34},{3,35},{4,36},{5,37},{6,38},{7,39},{8,40},{9,... | collective-permute-start | bytes 6291464 | tf_op jit(solution)/shard_map/ppermute | solution.py:248
  111.8 18.8 %collective-permute-start.35 = (bf16[2,256,768]{2,1,0:T(8,128)(2,1)}, bf16[2,256,768]{2,1,0:T(8,128)(2,1)S(1)}, u32[]{:S(2)}, u32[]{:S(2)}) collective-permute-start(bf16[2,256,768]{2,1,0:T(8,128)(2,1)} %get-tuple-element.25), channel_id=1, source_target_pairs={{0,4},{1,5},{2,6},{3,7},{4,0},{5,1},{6,2},{7,3},{8,12},{9,13},{10,... | collective-permute-start | bytes 2359304 | tf_op jit(solution)/shard_map/ppermute | solution.py:248
  120.5 45.8 %collective-permute-start.15 = (f32[2,256,1024]{2,1,0:T(8,128)}, f32[2,256,1024]{2,1,0:T(8,128)}, u32[]{:S(2)}, u32[]{:S(2)}) collective-permute-start(f32[2,256,1024]{2,1,0:T(8,128)} %get-tuple-element.15.mine), channel_id=1, source_target_pairs={{0,32},{1,33},{2,34},{3,35},{4,36},{5,37},{6,38},{7,39},{8,40},{9,... | collective-permute-start | bytes 6291464 | tf_op jit(solution)/shard_map/ppermute | solution.py:248
  136.2 26.3 %collective-permute-start.31 = (bf16[256,2048]{1,0:T(8,128)(2,1)}, bf16[256,2048]{1,0:T(8,128)(2,1)S(1)}, u32[]{:S(2)}, u32[]{:S(2)}) collective-permute-start(bf16[256,2048]{1,0:T(8,128)(2,1)} %shard_map.75), channel_id=1, source_target_pairs={{0,64},{1,65},{2,66},{3,67},{4,68},{5,69},{6,70},{7,71},{8,72},{9,... | collective-permute-start | bytes 3145736 | tf_op jit(solution)/shard_map/ppermute | solution.py:248
  145.4 25.4 %collective-permute-start.33 = (bf16[2,256,1024]{2,1,0:T(8,128)(2,1)}, bf16[2,256,1024]{2,1,0:T(8,128)(2,1)}, u32[]{:S(2)}, u32[]{:S(2)}) collective-permute-start(bf16[2,256,1024]{2,1,0:T(8,128)(2,1)} %get-tuple-element.23), channel_id=1, source_target_pairs={{0,4},{1,5},{2,6},{3,7},{4,0},{5,1},{6,2},{7,3},{8,12},{9,13},{10,... | collective-permute-start | bytes 3145736 | tf_op jit(solution)/shard_map/ppermute | solution.py:248
  145.7 43.3 %collective-permute-start.25 = (bf16[2,256,1024]{2,1,0:T(8,128)(2,1)}, bf16[2,256,1024]{2,1,0:T(8,128)(2,1)}, u32[]{:S(2)}, u32[]{:S(2)}) collective-permute-start(bf16[2,256,1024]{2,1,0:T(8,128)(2,1)} %get-tuple-element.19), channel_id=1, source_target_pairs={{0,4},{1,5},{2,6},{3,7},{4,0},{5,1},{6,2},{7,3},{8,12},{9,13},{10,... | collective-permute-start | bytes 3145736 | tf_op jit(solution)/shard_map/ppermute | solution.py:248
  146.9 64.5 %collective-permute-start.18 = (bf16[2,256,1024]{2,1,0:T(8,128)(2,1)}, bf16[2,256,1024]{2,1,0:T(8,128)(2,1)S(1)}, u32[]{:S(2)}, u32[]{:S(2)}) collective-permute-start(bf16[2,256,1024]{2,1,0:T(8,128)(2,1)} %get-tuple-element.16), channel_id=1, source_target_pairs={{0,4},{1,5},{2,6},{3,7},{4,0},{5,1},{6,2},{7,3},{8,12},{9,13},{10,... | collective-permute-start | bytes 3145736 | tf_op jit(solution)/shard_map/ppermute | solution.py:248
  162.6 69.3 %collective-permute-start.32 = (bf16[256,2048]{1,0:T(8,128)(2,1)S(1)}, bf16[256,2048]{1,0:T(8,128)(2,1)S(1)}, u32[]{:S(2)}, u32[]{:S(2)}) collective-permute-start(bf16[256,2048]{1,0:T(8,128)(2,1)S(1)} %collective-permute-done.31.refs_4_), channel_id=1, source_target_pairs={{0,32},{1,33},{2,34},{3,35},{4,36},{5,37},{6,38},{7,39},{8,40},{9,... | collective-permute-start | bytes 3145736 | tf_op jit(solution)/shard_map/ppermute | solution.py:248
  166.3 54.3 %collective-permute-start.23 = (bf16[256,1024]{1,0:T(8,128)(2,1)}, bf16[256,1024]{1,0:T(8,128)(2,1)}, u32[]{:S(2)}, u32[]{:S(2)}) collective-permute-start(bf16[256,1024]{1,0:T(8,128)(2,1)} %shard_map.71), channel_id=1, source_target_pairs={{0,64},{1,65},{2,66},{3,67},{4,68},{5,69},{6,70},{7,71},{8,72},{9,... | collective-permute-start | bytes 1572872 | tf_op jit(solution)/shard_map/ppermute | solution.py:248
  170.8 55.8 %collective-permute-start.16 = (bf16[256,1024]{1,0:T(8,128)(2,1)}, bf16[256,1024]{1,0:T(8,128)(2,1)}, u32[]{:S(2)}, u32[]{:S(2)}) collective-permute-start(bf16[256,1024]{1,0:T(8,128)(2,1)} %shard_map.69), channel_id=1, source_target_pairs={{0,64},{1,65},{2,66},{3,67},{4,68},{5,69},{6,70},{7,71},{8,72},{9,... | collective-permute-start | bytes 1572872 | tf_op jit(solution)/shard_map/ppermute | solution.py:248
  189.0 53.2 %collective-permute-start.34 = (bf16[2,256,1024]{2,1,0:T(8,128)(2,1)}, bf16[2,256,1024]{2,1,0:T(8,128)(2,1)}, u32[]{:S(2)}, u32[]{:S(2)}) collective-permute-start(bf16[2,256,1024]{2,1,0:T(8,128)(2,1)} %collective-permute-done.33.refs_6_), channel_id=1, source_target_pairs={{0,32},{1,33},{2,34},{3,35},{4,36},{5,37},{6,38},{7,39},{8,40},{9,... | collective-permute-start | bytes 3145736 | tf_op jit(solution)/shard_map/ppermute | solution.py:248
  211.4 36.6 %collective-permute-start.26 = (bf16[2,256,1024]{2,1,0:T(8,128)(2,1)}, bf16[2,256,1024]{2,1,0:T(8,128)(2,1)}, u32[]{:S(2)}, u32[]{:S(2)}) collective-permute-start(bf16[2,256,1024]{2,1,0:T(8,128)(2,1)} %collective-permute-done.25.refs_6_), channel_id=1, source_target_pairs={{0,32},{1,33},{2,34},{3,35},{4,36},{5,37},{6,38},{7,39},{8,40},{9,... | collective-permute-start | bytes 3145736 | tf_op jit(solution)/shard_map/ppermute | solution.py:248
  220.6 32.9 %collective-permute-start.19 = (bf16[2,256,1024]{2,1,0:T(8,128)(2,1)S(1)}, bf16[2,256,1024]{2,1,0:T(8,128)(2,1)}, u32[]{:S(2)}, u32[]{:S(2)}) collective-permute-start(bf16[2,256,1024]{2,1,0:T(8,128)(2,1)S(1)} %collective-permute-done.18.refs_6_), channel_id=1, source_target_pairs={{0,32},{1,33},{2,34},{3,35},{4,36},{5,37},{6,38},{7,39},{8,40},{9,... | collective-permute-start | bytes 3145736 | tf_op jit(solution)/shard_map/ppermute | solution.py:248
  226.6 21.4 %collective-permute-start.24 = (bf16[256,1024]{1,0:T(8,128)(2,1)}, bf16[256,1024]{1,0:T(8,128)(2,1)}, u32[]{:S(2)}, u32[]{:S(2)}) collective-permute-start(bf16[256,1024]{1,0:T(8,128)(2,1)} %collective-permute-done.23.refs_4_), channel_id=1, source_target_pairs={{0,32},{1,33},{2,34},{3,35},{4,36},{5,37},{6,38},{7,39},{8,40},{9,... | collective-permute-start | bytes 1572872 | tf_op jit(solution)/shard_map/ppermute | solution.py:248
  231.9 21.7 %collective-permute-start.17 = (bf16[256,1024]{1,0:T(8,128)(2,1)}, bf16[256,1024]{1,0:T(8,128)(2,1)}, u32[]{:S(2)}, u32[]{:S(2)}) collective-permute-start(bf16[256,1024]{1,0:T(8,128)(2,1)} %collective-permute-done.16.refs_4_), channel_id=1, source_target_pairs={{0,32},{1,33},{2,34},{3,35},{4,36},{5,37},{6,38},{7,39},{8,40},{9,... | collective-permute-start | bytes 1572872 | tf_op jit(solution)/shard_map/ppermute | solution.py:248
  (37 other events, 409.2 us)

commit v3 on v2

--- a/solution.py
+++ b/solution.py
@@ -56,64 +56,84 @@
 ACROSS = perm(lambda h, c, y, l, z: (1 - h, c, y, l if c == 0 else 1 - l, z))
 OTHER = perm(lambda h, c, y, l, z: (1 - h, c, y, l, z))
 MIB = 1 << 20
-VMEM = 48 * MIB
-
-
-def gram_kernel(slabs, local, r0, r1, *refs):
-    xs, (own_ref, give_ref, sum_ref, acc) = refs[:-4], refs[-4:]
+
+
+def gram_kernel(slabs, layout, skip, gives, count, local, r0, r1, *refs):
+    xs, refs = refs[:count], refs[count:]
+    own_ref, sum_ref = refs[0], refs[1]
     i = pl.program_id(0)
     size = r0.shape[1] // slabs
     own_ref[...] = jnp.zeros_like(own_ref)
-    acc[...] = jnp.zeros_like(acc)
-    for k, x in enumerate(xs):
+    targets = [(r0, own_ref)]
+    if gives:
+        give_ref, acc = refs[2], refs[3]
+        acc[...] = jnp.zeros_like(acc)
+        targets.append((r1, acc))
+    for k, ((a, ha), (b, hb)) in enumerate(layout):
 
         @pl.when(i == k)
-        def _(k=k, x=x):
+        def _(k=k, a=xs[a], ha=ha, b=xs[b], hb=hb):
             for t in range(slabs):
                 part = pl.ds(t * size, size)
-                for left, to in ((r0, own_ref), (r1, acc))[: 2 if k < 4 else 1]:
+                x = jnp.concatenate(
+                    [a[pl.ds(128 * ha, 128), part], b[pl.ds(128 * hb, 128), part]], axis=0
+                )
+                for left, to in targets if k < 4 else targets[:1]:
                     to[local[t]] += lax.dot_general(
                         left[:, part],
-                        x[:, part],
+                        x,
                         (((1,), (1,)), ((), ())),
                         preferred_element_type=jnp.float32,
                     )
 
     sum_ref[0] = own_ref[0] + own_ref[1]
-    sum_ref[1] = acc[0] + acc[1]
-
-    @pl.when(i < 4)
-    def _():
-        give_ref[...] = acc[...].astype(jnp.bfloat16)
-
-
-def gram(local, rooted, partner, xs, skip):
-    rows, m = rooted.shape[1], len(xs)
-    whole = pl.BlockSpec((256, rows), lambda i, f: (0, 0))
+    if gives:
+        sum_ref[1] = acc[0] + acc[1]
+
+        @pl.when((i >= skip) & (i < 4))
+        def _():
+            give_ref[...] = acc[...].astype(jnp.bfloat16)
+
+
+def gram(local, rooted, partner, xs, layout, skip, gives):
+    rows, m = rooted.shape[1], len(layout)
+    whole = lambda x: pl.BlockSpec(
+        x.shape, lambda i, f: (0, 0), pipeline_mode=pl.Buffered(1)
+    )
     last = 3 - skip
+    rank = 2 if gives else 1
+    out_specs = [
+        pl.BlockSpec((2, 256, 256), lambda i, f: (0, 0, i)),
+        pl.BlockSpec((rank, 256, 256), lambda i, f: (0, 0, i)),
+    ]
+    out_shape = [
+        pltpu.HBM((2, 256, 256 * m), jnp.float32),
+        pltpu.HBM((rank, 256, 256 * m), jnp.float32),
+    ]
+    if gives:
+        out_specs.append(
+            pl.BlockSpec((2, 256, 256), lambda i, f: (0, 0, jnp.clip(i - skip, 0, last)))
+        )
+        out_shape.append(pltpu.HBM((2, 256, 256 * (last + 1)), jnp.bfloat16))
     return pl.pallas_call(
-        lambda *refs: gram_kernel(local.shape[0], *refs),
+        lambda *refs: gram_kernel(local.shape[0], layout, skip, gives, len(xs), *refs),
         grid_spec=pltpu.PrefetchScalarGridSpec(
             num_scalar_prefetch=1,
             grid=(m,),
-            in_specs=[whole] * (m + 2),
-            out_specs=[
-                pl.BlockSpec((2, 256, 256), lambda i, f: (0, 0, i)),
-                pl.BlockSpec((2, 256, 256), lambda i, f: (0, 0, jnp.clip(i - skip, 0, last))),
-                pl.BlockSpec((2, 256, 256), lambda i, f: (0, 0, i)),
-            ],
-            scratch_shapes=[pltpu.VMEM((2, 256, 256), jnp.float32)],
+            in_specs=[whole(x) for x in (rooted, partner, *xs)],
+            out_specs=out_specs,
+            scratch_shapes=[pltpu.VMEM((2, 256, 256), jnp.float32)] if gives else [],
         ),
-        out_shape=[
-            pltpu.HBM((2, 256, 256 * m), jnp.float32),
-            pltpu.HBM((2, 256, 256 * (last + 1)), jnp.bfloat16),
-            pltpu.HBM((2, 256, 256 * m), jnp.float32),
-        ],
-        compiler_params=pltpu.CompilerParams(vmem_limit_bytes=VMEM),
+        out_shape=out_shape,
+        compiler_params=pltpu.CompilerParams(vmem_limit_bytes=20 * MIB),
         cost_estimate=pl.CostEstimate(
             flops=2 * 512 * 256 * m * rows, bytes_accessed=3 * m * MIB, transcendentals=0
         ),
     )(local, rooted, partner, *xs)
+
+
+def stay(x):
+    return pltpu.with_memory_space_constraint(x, pltpu.HBM)
 
 
 def mix_kernel(r_ref, mine, theirs, *refs):
@@ -137,12 +157,12 @@
         ),
         out_shape=pltpu.HBM((256, 1024 * parts), jnp.bfloat16),
         input_output_aliases={3: 0} if extra else {},
-        compiler_params=pltpu.CompilerParams(vmem_limit_bytes=VMEM),
+        compiler_params=pltpu.CompilerParams(vmem_limit_bytes=8 * MIB),
         cost_estimate=pl.CostEstimate(flops=MIB, bytes_accessed=3 * MIB, transcendentals=0),
-    )(pick, s, swapped, *extra)
-
-
-def final_kernel(first, pick, cols, g0, s0, mine, theirs, dr, er, *refs):
+    )(pick, stay(s), swapped, *extra)
+
+
+def final_kernel(diagonal, skip, pick, cols, g0, s0, mine, theirs, dr, er, *refs):
     out, buf, sems = refs[-3:]
     n = pl.program_id(0)
     slot = lax.rem(n, 2)
@@ -166,20 +186,20 @@
 
     a, b = mine[...].astype(jnp.float32), theirs[...].astype(jnp.float32)
     rest = s0[0] + jnp.where(swap, a, b)
-    if first:
-        rest = rest + jnp.where(n == 0, refs[0][...], 0.0)
+    if diagonal:
+        rest = rest + jnp.where(n == 0, refs[2][...], 0.0)
     buf[slot, 0, 0] = g0[1] + rest
     buf[slot, 0, 1] = g0[0] + rest
     rest = jnp.where(swap, b, a)
-    if first:
-
-        @pl.when(n == 0)
+    if skip:
+
+        @pl.when(n < skip)
         def _():
-            gp, sp = refs[1], refs[2]
+            gp, sp = refs[0], refs[1]
             buf[slot, 1, 0] = gp[1] + sp[0] + rest
             buf[slot, 1, 1] = gp[0] + sp[0] + rest
 
-    @pl.when(n >= (1 if first else 0))
+    @pl.when(n >= skip)
     def _():
         other = er[0].astype(jnp.float32) + er[1].astype(jnp.float32) + rest
         buf[slot, 1, 0] = dr[1].astype(jnp.float32) + other
@@ -195,21 +215,25 @@
                 copy.wait()
 
 
-def final(pick, cols, g, swapped, mine, theirs, half, dr, er, pen, out, total):
-    first = out is None
-    skip = 1 if first else 0
+def final(pick, cols, g, swapped, mine, theirs, half, dr, er, skip, known, pen, out, total):
     base = 4 * half
-    if first:
-        extra = [pen, g, swapped]
-        extra_specs = [
-            pl.BlockSpec((256, 256), lambda n, p, c: (0, 0)),
-            pl.BlockSpec((2, 256, 256), lambda n, p, c: (0, 0, 4)),
-            pl.BlockSpec((1, 256, 256), lambda n, p, c: (0, 0, 4)),
+    extra, extra_specs, alias = [], [], {}
+    if skip:
+        gp, sp, at = known
+        extra += [stay(gp), sp]
+        extra_specs += [
+            pl.BlockSpec((2, 256, 256), lambda n, p, c: (0, 0, at + jnp.minimum(n, skip - 1))),
+            pl.BlockSpec((1, 256, 256), lambda n, p, c: (0, 0, at + jnp.minimum(n, skip - 1))),
         ]
+    if out is None:
+        extra.append(pen)
+        extra_specs.append(pl.BlockSpec((256, 256), lambda n, p, c: (0, 0)))
     else:
-        extra, extra_specs = [out], [pl.BlockSpec(memory_space=pl.ANY)]
+        alias = {8 + len(extra): 0}
+        extra.append(out)
+        extra_specs.append(pl.BlockSpec(memory_space=pl.ANY))
     return pl.pallas_call(
-        lambda *refs: final_kernel(first, *refs),
+        lambda *refs: final_kernel(out is None, skip, *refs),
         grid_spec=pltpu.PrefetchScalarGridSpec(
             num_scalar_prefetch=2,
             grid=(4,),
@@ -228,10 +252,10 @@
             ],
         ),
         out_shape=pltpu.HBM((2, 256, total), jnp.float32),
-        input_output_aliases={} if first else {8: 0},
-        compiler_params=pltpu.CompilerParams(vmem_limit_bytes=VMEM),
+        input_output_aliases=alias,
+        compiler_params=pltpu.CompilerParams(vmem_limit_bytes=12 * MIB),
         cost_estimate=pl.CostEstimate(flops=MIB, bytes_accessed=9 * MIB, transcendentals=0),
-    )(pick, cols, g, swapped, mine, theirs, dr, er, *extra)
+    )(pick, cols, stay(g), swapped, mine, theirs, dr, er, *extra)
 
 
 def body(design, weights, response, fold_of, smoothing):
@@ -261,9 +285,8 @@
     total_rhs = chip_rhs + send(chip_rhs, OTHER)
     complement_rhs = total_rhs[None] - rhs
 
-    near, chunks = [], ([], [], [])
-    where = ([], [], [], [])
-    where[0].extend([(0, 0, 0), (0, 0, 1)])
+    blocks = ([rooted], [], [], [])
+    where = ([(0, 0, 0), (0, 0, 1)], [], [], [])
     far = []
     for colour, (p, q) in enumerate((("y", "z"), ("z", "y"))):
         at = lambda u, v, p=p, k=colour: (u, v, k) if p == "y" else (v, u, k)
@@ -277,26 +300,36 @@
         od_m, od_p = send(od, STEP[q, 1]), send(od, STEP[q, -1])
         ab_2 = send(ab_m, STEP[q, 1])
         od_2 = send(od_p, STEP[q, -1])
-        near.append(ab)
+        blocks[0].append(ab)
         far.append(d)
-        chunks[0].extend([ab_m, ab_p])
-        chunks[1].extend([od_m, od_p])
-        chunks[2].extend([ab_2, od_2])
-        ab_off, od_off = (-1, 1), (0, 2)
-        where[0].extend(at(o, 0) for o in ab_off)
-        where[1].extend(at(o, v) for v in (-1, 1) for o in ab_off)
-        where[2].extend(at(o, v) for v in (-1, 1) for o in od_off)
-        where[3].extend(at(o, 2) for o in ab_off + od_off)
+        blocks[1].extend([ab_m, ab_p])
+        blocks[2].extend([od_m, od_p])
+        blocks[3].extend([ab_2, od_2])
+        where[0].extend(at(o, 0) for o in (-1, 1))
+        where[1].extend(at(o, v) for v in (-1, 1) for o in (-1, 1))
+        where[2].extend(at(0, v) for v in (-1, 1))
+        where[3].extend(at(o, 2) for o in (-1, 1, 0, 2))
     where[0].extend([(2, 0, 0), (0, 2, 1)])
-    work = [[rooted] + near + [jnp.concatenate(far, axis=0), partner]] + list(chunks)
+    where[2].extend([(2, -1, 0), (2, 1, 0), (-1, 2, 1), (1, 2, 1)])
+    blocks[0].extend(far + [partner])
+    both = lambda k: ((k, 0), (k, 1))
+    layouts = (
+        (both(0), both(1), both(2), ((3, 0), (4, 0)), both(5)),
+        tuple(both(k) for k in range(4)),
+        tuple(((k, half), (k + 1, half)) for half in range(2) for k in (0, 2)),
+        tuple(both(k) for k in range(4)),
+    )
+    skips = (1, 0, 2, 0)
 
     pen = jnp.kron(jnp.diag(smoothing), second_differences(TERM))
-
-    places = ((0, 0, 2), (0, 1, 2), (1, 0, 1), (2, 0, 1))
+    halves = (partner[:128], partner[128:])
+    local, pen, halves = lax.optimization_barrier((local, pen, halves))
+
+    places = ((0, 0, 1), (1, 0, 1), (2, 0, 1), (3, 0, 1))
     state, mine, theirs, u = [], [], [], None
-    for n, xs in enumerate(work):
+    for n, xs in enumerate(blocks):
         message, half, parts = places[n]
-        g, give, s = gram(local, rooted, partner, xs, 1 if n == 0 else 0)
+        g, s, give = gram(local, rooted, partner, xs, layouts[n], skips[n], True)
         swapped = send(s, CORE)
         dr = send(give, PARTNER)
         er = send(dr, CORE)
@@ -306,6 +339,14 @@
             mine.append(send(u, ACROSS))
             theirs.append(send(mine[-1], CORE))
             u = None
+    known = []
+    for colour, q in enumerate("zy"):
+        known.append(send(halves[colour], STEP[q, 1]))
+        known.append(send(halves[colour], STEP[q, -1]))
+    pair = lambda k: ((k, 0), (k + 1, 0))
+    g_known, s = gram(local, rooted, partner, known, (pair(0), pair(2)), 0, False)
+    s_known = send(s, CORE)
+    raw = {0: (state[0][0], state[0][1], 4), 2: (g_known, s_known, 0)}
     out = None
     for n, (g, swapped, dr, er) in enumerate(state):
         message, half, _ = places[n]
@@ -315,8 +356,9 @@
             for l in (me_l, 1 - me_l):
                 cols.append((y * 8 + l * 4 + z) * 2 + colour)
         cols = jnp.stack(cols).astype(jnp.int32)
+        v0, v1 = mine[message], theirs[message]
         out = final(
-            pick, cols, g, swapped, mine[message], theirs[message], half, dr, er, pen, out, width
+            pick, cols, g, swapped, v0, v1, half, dr, er, skips[n], raw.get(n), pen, out, width
         )
     return (out, complement_rhs)
 

time: 260 us -> 277 us (1.065)
  waiting for transfers between devices: 89.3 us -> 119 us
  starting transfers between devices: 88.9 us -> 75.8 us
    ppermute x39 -> x46, waiting for transfers between devices: 89.3 us -> 119 us  [send(): return lax.ppermute(x, AXES, pairs)]
    ppermute x39 -> x46, starting transfers between devices: 88.9 us -> 75.8 us  [send(): return lax.ppermute(x, AXES, pairs)]
    pallas_call x8 -> x9, Pallas kernels: 53.3 us -> 50.9 us  [the longest x5 29.3 us: gram(): pl.pallas_call(lambda *refs: gram_kernel(local.shape[0], layout, skip, gi...]
    unnamed x61 -> x73, local copies, waits for them, and re-layouts: 12 us -> 10.9 us
  transfers between devices with their start and end apart: 39 -> 46, of which waited for: 12 -> 12; matrix products, arithmetic and copies ran while one was open for 3% -> 3% of each run, Pallas kernels for 21% -> 19%
where the time goes in v3:
time: 277 us; the launch traced here: 276 us
  waiting for transfers between devices  119 us (43%)
  starting transfers between devices  75.8 us (27%)
  Pallas kernels  58.9 us (21%)
  local copies, waits for them, and re-layouts  12.9 us (5%)
  other arithmetic  7.45 us (3%)
    ppermute x46, waiting for transfers between devices, send(): return lax.ppermute(x, AXES, pairs)  119 us
    ppermute x46, starting transfers between devices, send(): return lax.ppermute(x, AXES, pairs)  75.8 us
    pallas_call x5, Pallas kernels, gram(): pl.pallas_call(lambda *refs: gram_kernel(local.shape[0], layout, skip, gi...  29.3 us
    pallas_call x4, Pallas kernels, final(): pl.pallas_call(lambda *refs: final_kernel(out is None, skip, *refs), grid...  21.6 us
    unnamed x73, local copies, waits for them, and re-layouts  10.9 us
    pallas_call x4, Pallas kernels, mix(): pl.pallas_call(mix_kernel, grid_spec=pltpu.PrefetchScalarGridSpec(num_sca...  7.98 us
  transfers between devices with their start and end apart: 46, of which 12 were waited for; matrix products, arithmetic and copies ran while one was open for 3% of the time, Pallas kernels for 19%

profile of v3, /device:TPU:1, one launch (start us, length us, event | category | flops | bytes accessed | tf_op | source)
XLA Modules:
  0.0 275.7 jit_solution(13850783074726397468)
XLA Ops:
  3.4 4.6 %collective-permute-start.8 = (bf16[128,2048]{1,0:T(8,128)(2,1)S(1)}, bf16[128,2048]{1,0:T(8,128)(2,1)}, u32[]{:S(2)}, u32[]{:S(2)}) collective-permute-start(bf16[128,2048]{1,0:T(8,128)(2,1)S(1)} %get-tuple-element.44), channel_id=1, source_target_pairs={{0,1},{1,2},{2,3},{3,0},{4,5},{5,6},{6,7},{7,4},{8,9},{9,10},{10,1... | collective-permute-start | bytes 1572872 | tf_op jit(solution)/shard_map/ppermute | solution.py:272
  8.0 2.7 collective-permute-start.1
  13.0 5.6 %collective-permute-done.8 = bf16[128,2048]{1,0:T(8,128)(2,1)} collective-permute-done((bf16[128,2048]{1,0:T(8,128)(2,1)S(1)}, bf16[128,2048]{1,0:T(8,128)(2,1)}, u32[]{:S(2)}, u32[]{:S(2)}) %collective-permute-start.8) | collective-permute-done | bytes 524320 | tf_op jit(solution)/shard_map/ppermute | solution.py:272
  28.7 2.8 %collective-permute-start.45 = (f32[256]{0:T(256)S(1)}, f32[256]{0:T(256)S(1)}, u32[]{:S(2)}, u32[]{:S(2)}) collective-permute-start(f32[256]{0:T(256)S(1)} %add.566), channel_id=1, source_target_pairs={{0,64},{1,65},{2,66},{3,67},{4,68},{5,69},{6,70},{7,71},{8,72},{9,... | collective-permute-start | bytes 3080 | tf_op jit(solution)/shard_map/ppermute | solution.py:272
  31.9 4.0 %collective-permute-done.45 = f32[256]{0:T(256)S(1)} collective-permute-done((f32[256]{0:T(256)S(1)}, f32[256]{0:T(256)S(1)}, u32[]{:S(2)}, u32[]{:S(2)}) %collective-permute-start.45) | collective-permute-done | bytes 1056 | tf_op jit(solution)/shard_map/ppermute | solution.py:272
  35.9 3.8 %collective-permute-start.33 = (bf16[256,2048]{1,0:T(8,128)(2,1)}, bf16[256,2048]{1,0:T(8,128)(2,1)S(1)}, u32[]{:S(2)}, u32[]{:S(2)}) collective-permute-start(bf16[256,2048]{1,0:T(8,128)(2,1)} %pad_maximum_fusion.2.refs_5_), channel_id=1, source_target_pairs={{0,24},{1,25},{2,26},{3,27},{4,28},{5,29},{6,30},{7,31},{8,0},{9,1... | collective-permute-start | bytes 3145736 | tf_op jit(solution)/shard_map/ppermute | solution.py:272
  39.7 3.4 %collective-permute-start.32 = (bf16[256,2048]{1,0:T(8,128)(2,1)}, bf16[256,2048]{1,0:T(8,128)(2,1)S(1)}, u32[]{:S(2)}, u32[]{:S(2)}) collective-permute-start(bf16[256,2048]{1,0:T(8,128)(2,1)} %pad_maximum_fusion.refs_4_), channel_id=1, source_target_pairs={{0,3},{1,0},{2,1},{3,2},{4,7},{5,4},{6,5},{7,6},{8,11},{9,8},{10,9... | collective-permute-start | bytes 3145736 | tf_op jit(solution)/shard_map/ppermute | solution.py:272
  43.4 29.0 %collective-permute-done.5.refs_6_ = bf16[128,2048]{1,0:T(8,128)(2,1)S(1)} collective-permute-done((bf16[128,2048]{1,0:T(8,128)(2,1)}, bf16[128,2048]{1,0:T(8,128)(2,1)S(1)}, u32[]{:S(2)}, u32[]{:S(2)}) %collective-permute-start.5) | collective-permute-done | bytes 524320 | tf_op jit(solution)/shard_map/ppermute | solution.py:272
  72.4 4.5 %collective-permute-start.28 = (bf16[128,2048]{1,0:T(8,128)(2,1)S(1)}, bf16[128,2048]{1,0:T(8,128)(2,1)S(1)}, u32[]{:S(2)}, u32[]{:S(2)}) collective-permute-start(bf16[128,2048]{1,0:T(8,128)(2,1)S(1)} %get-tuple-element.27), channel_id=1, source_target_pairs={{0,3},{1,0},{2,1},{3,2},{4,7},{5,4},{6,5},{7,6},{8,11},{9,8},{10,9... | collective-permute-start | bytes 1572872 | tf_op jit(solution)/shard_map/ppermute | solution.py:272
  76.8 3.3 %collective-permute-start.13 = (bf16[256,2048]{1,0:T(8,128)(2,1)S(1)}, bf16[256,2048]{1,0:T(8,128)(2,1)S(1)}, u32[]{:S(2)}, u32[]{:S(2)}) collective-permute-start(bf16[256,2048]{1,0:T(8,128)(2,1)S(1)} %pad_maximum_fusion.3), channel_id=1, source_target_pairs={{0,24},{1,25},{2,26},{3,27},{4,28},{5,29},{6,30},{7,31},{8,0},{9,1... | collective-permute-start | bytes 3145736 | tf_op jit(solution)/shard_map/ppermute | solution.py:272
  81.3 7.7 %shard_map.75 = (f32[2,256,1280]{2,1,0:T(8,128)}, f32[2,256,1280]{2,1,0:T(8,128)}, bf16[2,256,768]{2,1,0:T(8,128)(2,1)}) custom-call(s32[8]{0:T(128)S(1)} %get-tuple-element.20.refs_0_, bf16[256,2048]{1,0:T(8,128)(2,1)S(1)} %fusion.refs_1_.refs_3_, bf16[256,2048]{1,0:T(8,128)(2,1)S(1)} %collective-permute-done.refs_2_.refs_8_, ...), custom_call_target="tpu_custom_call" | custom-call | flops 2684354560 | bytes 15728640 | tf_op jit(solution)/shard_map/pallas_call | solution.py:118
  90.6 2.7 collective-permute-start.30
  93.3 11.6 %collective-permute-done.29.refs_5_ = bf16[128,2048]{1,0:T(8,128)(2,1)S(1)} collective-permute-done((bf16[128,2048]{1,0:T(8,128)(2,1)S(1)}, bf16[128,2048]{1,0:T(8,128)(2,1)S(1)}, u32[]{:S(2)}, u32[]{:S(2)}) %collective-permute-start.29) | collective-permute-done | bytes 524320 | tf_op jit(solution)/shard_map/ppermute | solution.py:272
  105.2 24.7 %collective-permute-done.20.refs_3_ = bf16[256,2048]{1,0:T(8,128)(2,1)S(1)} collective-permute-done((bf16[256,2048]{1,0:T(8,128)(2,1)S(1)}, bf16[256,2048]{1,0:T(8,128)(2,1)S(1)}, u32[]{:S(2)}, u32[]{:S(2)}) %collective-permute-start.20) | collective-permute-done | bytes 1048608 | tf_op jit(solution)/shard_map/ppermute | solution.py:272
  131.2 2.4 collective-permute-start.7
  136.1 7.5 %shard_map.73 = (f32[2,256,1024]{2,1,0:T(8,128)}, f32[2,256,1024]{2,1,0:T(8,128)}, bf16[2,256,1024]{2,1,0:T(8,128)(2,1)}) custom-call(s32[8]{0:T(128)S(1)} %get-tuple-element.20.refs_0_, bf16[256,2048]{1,0:T(8,128)(2,1)S(1)} %copy-done.1, bf16[256,2048]{1,0:T(8,128)(2,1)S(1)} %copy-done.9, bf16[256,2048]{1,0:T(8,128)(2,1)} %collective-permute-done.3.refs_3_, ...), custom_call_target="tpu_custom_call" | custom-call | flops 2147483648 | bytes 12582912 | tf_op jit(solution)/shard_map/pallas_call | solution.py:118
  145.3 5.6 %shard_map.70 = (f32[2,256,1024]{2,1,0:T(8,128)}, f32[2,256,1024]{2,1,0:T(8,128)}, bf16[2,256,512]{2,1,0:T(8,128)(2,1)}) custom-call(s32[8]{0:T(128)S(1)} %get-tuple-element.20.refs_0_, bf16[256,2048]{1,0:T(8,128)(2,1)S(1)} %copy-done.1, bf16[256,2048]{1,0:T(8,128)(2,1)S(1)} %copy-done.9, bf16[256,2048]{1,0:T(8,128)(2,1)S(1)} %collective-permute-done.20.refs_3_, ...), custom_call_target="tpu_custom_call" | custom-call | flops 2147483648 | bytes 12582912 | tf_op jit(solution)/shard_map/pallas_call | solution.py:118
  152.7 5.7 %shard_map.68 = (f32[2,256,1024]{2,1,0:T(8,128)}, f32[2,256,1024]{2,1,0:T(8,128)}, bf16[2,256,1024]{2,1,0:T(8,128)(2,1)}) custom-call(s32[8]{0:T(128)S(1)} %get-tuple-element.20.refs_0_, bf16[256,2048]{1,0:T(8,128)(2,1)S(1)} %copy-done.1, bf16[256,2048]{1,0:T(8,128)(2,1)S(1)} %copy-done.9, bf16[256,2048]{1,0:T(8,128)(2,1)S(1)} %collective-permute-done.4.refs_3_, ...), custom_call_target="tpu_custom_call" | custom-call | flops 2147483648 | bytes 12582912 | tf_op jit(solution)/shard_map/pallas_call | solution.py:118
  158.9 2.1 shard_map.76
  161.0 14.6 %collective-permute-done.37.refs_6_ = bf16[2,256,1024]{2,1,0:T(8,128)(2,1)S(1)} collective-permute-done((bf16[2,256,1024]{2,1,0:T(8,128)(2,1)S(1)}, bf16[2,256,1024]{2,1,0:T(8,128)(2,1)S(1)}, u32[]{:S(2)}, u32[]{:S(2)}) %collective-permute-start.37) | collective-permute-done | bytes 1048608 | tf_op jit(solution)/shard_map/ppermute | solution.py:272
  176.3 10.5 %collective-permute-done.25.refs_6_ = bf16[2,256,512]{2,1,0:T(8,128)(2,1)S(1)} collective-permute-done((bf16[2,256,512]{2,1,0:T(8,128)(2,1)S(1)}, bf16[2,256,512]{2,1,0:T(8,128)(2,1)S(1)}, u32[]{:S(2)}, u32[]{:S(2)}) %collective-permute-start.25) | collective-permute-done | bytes 524320 | tf_op jit(solution)/shard_map/ppermute | solution.py:272
  191.7 8.3 %collective-permute-start.41 = (bf16[256,1024]{1,0:T(8,128)(2,1)S(1)}, bf16[256,1024]{1,0:T(8,128)(2,1)S(1)}, u32[]{:S(2)}, u32[]{:S(2)}) collective-permute-start(bf16[256,1024]{1,0:T(8,128)(2,1)S(1)} %collective-permute-done.40.refs_4_), channel_id=1, source_target_pairs={{0,32},{1,33},{2,34},{3,35},{4,36},{5,37},{6,38},{7,39},{8,40},{9,... | collective-permute-start | bytes 1572872 | tf_op jit(solution)/shard_map/ppermute | solution.py:272
  200.0 2.0 shard_map.71
  202.0 19.9 %collective-permute-start.36 = (bf16[256,1024]{1,0:T(8,128)(2,1)S(1)}, bf16[256,1024]{1,0:T(8,128)(2,1)S(1)}, u32[]{:S(2)}, u32[]{:S(2)}) collective-permute-start(bf16[256,1024]{1,0:T(8,128)(2,1)S(1)} %collective-permute-done.35.refs_4_), channel_id=1, source_target_pairs={{0,32},{1,33},{2,34},{3,35},{4,36},{5,37},{6,38},{7,39},{8,40},{9,... | collective-permute-start | bytes 1572872 | tf_op jit(solution)/shard_map/ppermute | solution.py:272
  223.9 2.0 shard_map.69
  228.0 2.7 shard_map.72
  233.2 9.5 %collective-permute-done.23.refs_4_ = bf16[256,1024]{1,0:T(8,128)(2,1)} collective-permute-done((bf16[256,1024]{1,0:T(8,128)(2,1)}, bf16[256,1024]{1,0:T(8,128)(2,1)}, u32[]{:S(2)}, u32[]{:S(2)}) %collective-permute-start.23) | collective-permute-done | bytes 524320 | tf_op jit(solution)/shard_map/ppermute | solution.py:272
  242.7 5.6 %collective-permute-done.16.refs_4_ = bf16[256,1024]{1,0:T(8,128)(2,1)} collective-permute-done((bf16[256,1024]{1,0:T(8,128)(2,1)}, bf16[256,1024]{1,0:T(8,128)(2,1)}, u32[]{:S(2)}, u32[]{:S(2)}) %collective-permute-start.16) | collective-permute-done | bytes 524320 | tf_op jit(solution)/shard_map/ppermute | solution.py:272
  253.7 5.4 %shard_map.77.refs_8_ = f32[2,256,8192]{2,1,0:T(8,128)} custom-call(s32[1]{0:T(128)} %bitcast.r_ref.refs_0_, s32[16]{0:T(128)S(1)} %stack.280.refs_1_, f32[2,256,1280]{2,1,0:T(8,128)} %get-tuple-element.34.refs_2_.refs_8_, f32[2,256,1280]{2,1,0:T(8,128)S(1)} %collective-permute-done.39.theirs.refs_3_.refs_9_, bf16[256,1024]{1,0:T(8,128)(2,1)S(1)} %copy-done.20, ...), custom_call_target="tpu_custom_call" | custom-call | flops 1048576 | bytes 9437184 | tf_op jit(solution)/shard_map/pallas_call | solution.py:235
  259.2 5.0 %shard_map.78.refs_10_ = f32[2,256,8192]{2,1,0:T(8,128)} custom-call(s32[1]{0:T(128)} %bitcast.r_ref.refs_0_, s32[16]{0:T(128)S(1)} %stack.263.refs_1_, f32[2,256,1024]{2,1,0:T(8,128)} %get-tuple-element.31.refs_2_, f32[2,256,1024]{2,1,0:T(8,128)S(1)} %copy-done.3, bf16[256,1024]{1,0:T(8,128)(2,1)S(1)} %copy-done.22, ...), custom_call_target="tpu_custom_call", output_to_operand_aliasing={{}: (8, {})} | custom-call | flops 1048576 | bytes 9437184 | tf_op jit(solution)/shard_map/pallas_call | solution.py:235
  264.2 5.6 %shard_map.79.refs_8_ = f32[2,256,8192]{2,1,0:T(8,128)} custom-call(s32[1]{0:T(128)} %bitcast.r_ref.refs_0_, s32[16]{0:T(128)S(1)} %stack.246.refs_1_, f32[2,256,1024]{2,1,0:T(8,128)} %get-tuple-element.24.refs_2_, f32[2,256,1024]{2,1,0:T(8,128)S(1)} %copy-done.7, ...), custom_call_target="tpu_custom_call", output_to_operand_aliasing={{}: (10, {})} | custom-call | flops 1048576 | bytes 9437184 | tf_op jit(solution)/shard_map/pallas_call | solution.py:235
  269.9 5.6 %shard_map.80 = f32[2,256,8192]{2,1,0:T(8,128)} custom-call(s32[1]{0:T(128)} %bitcast.r_ref.refs_0_, s32[16]{0:T(128)S(1)} %stack.229.refs_1_, f32[2,256,1024]{2,1,0:T(8,128)} %get-tuple-element.21.refs_2_, f32[2,256,1024]{2,1,0:T(8,128)S(1)} %copy-done.5, bf16[256,1024]{1,0:T(8,128)(2,1)} %collective-permute-done.16.refs_4_, ...), custom_call_target="tpu_custom_call", output_to_operand_aliasing={{}: (8, {})} | custom-call | flops 1048576 | bytes 9437184 | tf_op jit(solution)/shard_map/pallas_call | solution.py:235
  (176 shorter events, 44.1 us)
Async XLA Ops:
  10.7 29.0 %collective-permute-start = (bf16[256,2048]{1,0:T(8,128)(2,1)S(1)}, bf16[256,2048]{1,0:T(8,128)(2,1)S(1)}, u32[]{:S(2)}, u32[]{:S(2)}) collective-permute-start(bf16[256,2048]{1,0:T(8,128)(2,1)S(1)} %fusion.refs_1_.refs_3_), channel_id=1, source_target_pairs={{0,4},{1,5},{2,6},{3,7},{4,0},{5,1},{6,2},{7,3},{8,12},{9,13},{10,... | collective-permute-start | bytes 3145736 | tf_op jit(solution)/shard_map/ppermute | solution.py:272
  23.8 48.6 %collective-permute-start.10 = (bf16[256,2048]{1,0:T(8,128)(2,1)}, bf16[256,2048]{1,0:T(8,128)(2,1)}, u32[]{:S(2)}, u32[]{:S(2)}) collective-permute-start(bf16[256,2048]{1,0:T(8,128)(2,1)} %pad_maximum_fusion.2.refs_5_), channel_id=1, source_target_pairs={{0,8},{1,9},{2,10},{3,11},{4,12},{5,13},{6,14},{7,15},{8,16},{9,17... | collective-permute-start | bytes 3145736 | tf_op jit(solution)/shard_map/ppermute | solution.py:272
  24.8 18.4 %collective-permute-start.12 = (bf16[128,2048]{1,0:T(8,128)(2,1)}, bf16[128,2048]{1,0:T(8,128)(2,1)S(1)}, u32[]{:S(2)}, u32[]{:S(2)}) collective-permute-start(bf16[128,2048]{1,0:T(8,128)(2,1)} %collective-permute-done.8), channel_id=1, source_target_pairs={{0,1},{1,2},{2,3},{3,0},{4,5},{5,6},{6,7},{7,4},{8,9},{9,10},{10,1... | collective-permute-start | bytes 1572872 | tf_op jit(solution)/shard_map/ppermute | solution.py:272
  28.6 48.3 %collective-permute-start.3 = (bf16[256,2048]{1,0:T(8,128)(2,1)}, bf16[256,2048]{1,0:T(8,128)(2,1)}, u32[]{:S(2)}, u32[]{:S(2)}) collective-permute-start(bf16[256,2048]{1,0:T(8,128)(2,1)} %pad_maximum_fusion.refs_4_), channel_id=1, source_target_pairs={{0,1},{1,2},{2,3},{3,0},{4,5},{5,6},{6,7},{7,4},{8,9},{9,10},{10,1... | collective-permute-start | bytes 3145736 | tf_op jit(solution)/shard_map/ppermute | solution.py:272
  35.9 53.1 %collective-permute-start.33 = (bf16[256,2048]{1,0:T(8,128)(2,1)}, bf16[256,2048]{1,0:T(8,128)(2,1)S(1)}, u32[]{:S(2)}, u32[]{:S(2)}) collective-permute-start(bf16[256,2048]{1,0:T(8,128)(2,1)} %pad_maximum_fusion.2.refs_5_), channel_id=1, source_target_pairs={{0,24},{1,25},{2,26},{3,27},{4,28},{5,29},{6,30},{7,31},{8,0},{9,1... | collective-permute-start | bytes 3145736 | tf_op jit(solution)/shard_map/ppermute | solution.py:272
  39.7 50.8 %collective-permute-start.32 = (bf16[256,2048]{1,0:T(8,128)(2,1)}, bf16[256,2048]{1,0:T(8,128)(2,1)S(1)}, u32[]{:S(2)}, u32[]{:S(2)}) collective-permute-start(bf16[256,2048]{1,0:T(8,128)(2,1)} %pad_maximum_fusion.refs_4_), channel_id=1, source_target_pairs={{0,3},{1,0},{2,1},{3,2},{4,7},{5,4},{6,5},{7,6},{8,11},{9,8},{10,9... | collective-permute-start | bytes 3145736 | tf_op jit(solution)/shard_map/ppermute | solution.py:272
  43.2 29.2 %collective-permute-start.5 = (bf16[128,2048]{1,0:T(8,128)(2,1)}, bf16[128,2048]{1,0:T(8,128)(2,1)S(1)}, u32[]{:S(2)}, u32[]{:S(2)}) collective-permute-start(bf16[128,2048]{1,0:T(8,128)(2,1)} %collective-permute-done.1), channel_id=1, source_target_pairs={{0,8},{1,9},{2,10},{3,11},{4,12},{5,13},{6,14},{7,15},{8,16},{9,17... | collective-permute-start | bytes 1572872 | tf_op jit(solution)/shard_map/ppermute | solution.py:272
  72.4 18.2 %collective-permute-start.28 = (bf16[128,2048]{1,0:T(8,128)(2,1)S(1)}, bf16[128,2048]{1,0:T(8,128)(2,1)S(1)}, u32[]{:S(2)}, u32[]{:S(2)}) collective-permute-start(bf16[128,2048]{1,0:T(8,128)(2,1)S(1)} %get-tuple-element.27), channel_id=1, source_target_pairs={{0,3},{1,0},{2,1},{3,2},{4,7},{5,4},{6,5},{7,6},{8,11},{9,8},{10,9... | collective-permute-start | bytes 1572872 | tf_op jit(solution)/shard_map/ppermute | solution.py:272
  76.8 28.1 %collective-permute-start.13 = (bf16[256,2048]{1,0:T(8,128)(2,1)S(1)}, bf16[256,2048]{1,0:T(8,128)(2,1)S(1)}, u32[]{:S(2)}, u32[]{:S(2)}) collective-permute-start(bf16[256,2048]{1,0:T(8,128)(2,1)S(1)} %pad_maximum_fusion.3), channel_id=1, source_target_pairs={{0,24},{1,25},{2,26},{3,27},{4,28},{5,29},{6,30},{7,31},{8,0},{9,1... | collective-permute-start | bytes 3145736 | tf_op jit(solution)/shard_map/ppermute | solution.py:272
  104.8 25.0 %collective-permute-start.20 = (bf16[256,2048]{1,0:T(8,128)(2,1)S(1)}, bf16[256,2048]{1,0:T(8,128)(2,1)S(1)}, u32[]{:S(2)}, u32[]{:S(2)}) collective-permute-start(bf16[256,2048]{1,0:T(8,128)(2,1)S(1)} %pad_maximum_fusion.1), channel_id=1, source_target_pairs={{0,1},{1,2},{2,3},{3,0},{4,5},{5,6},{6,7},{7,4},{8,9},{9,10},{10,1... | collective-permute-start | bytes 3145736 | tf_op jit(solution)/shard_map/ppermute | solution.py:272
  104.8 26.4 %collective-permute-start.21 = (bf16[256,2048]{1,0:T(8,128)(2,1)S(1)}, bf16[256,2048]{1,0:T(8,128)(2,1)S(1)}, u32[]{:S(2)}, u32[]{:S(2)}) collective-permute-start(bf16[256,2048]{1,0:T(8,128)(2,1)S(1)} %pad_maximum_fusion.3), channel_id=1, source_target_pairs={{0,8},{1,9},{2,10},{3,11},{4,12},{5,13},{6,14},{7,15},{8,16},{9,17... | collective-permute-start | bytes 3145736 | tf_op jit(solution)/shard_map/ppermute | solution.py:272
  104.9 53.7 %collective-permute-start.39 = (f32[2,256,1280]{2,1,0:T(8,128)}, f32[2,256,1280]{2,1,0:T(8,128)S(1)}, u32[]{:S(2)}, u32[]{:S(2)}) collective-permute-start(f32[2,256,1280]{2,1,0:T(8,128)} %get-tuple-element.35.mine), channel_id=1, source_target_pairs={{0,32},{1,33},{2,34},{3,35},{4,36},{5,37},{6,38},{7,39},{8,40},{9,... | collective-permute-start | bytes 7864328 | tf_op jit(solution)/shard_map/ppermute | solution.py:272
  105.0 39.8 %collective-permute-start.11 = (bf16[256,2048]{1,0:T(8,128)(2,1)}, bf16[256,2048]{1,0:T(8,128)(2,1)S(1)}, u32[]{:S(2)}, u32[]{:S(2)}) collective-permute-start(bf16[256,2048]{1,0:T(8,128)(2,1)} %collective-permute-done.10.refs_5_), channel_id=1, source_target_pairs={{0,8},{1,9},{2,10},{3,11},{4,12},{5,13},{6,14},{7,15},{8,16},{9,17... | collective-permute-start | bytes 3145736 | tf_op jit(solution)/shard_map/ppermute | solution.py:272
  105.1 39.7 %collective-permute-start.4 = (bf16[256,2048]{1,0:T(8,128)(2,1)}, bf16[256,2048]{1,0:T(8,128)(2,1)S(1)}, u32[]{:S(2)}, u32[]{:S(2)}) collective-permute-start(bf16[256,2048]{1,0:T(8,128)(2,1)} %collective-permute-done.3.refs_3_), channel_id=1, source_target_pairs={{0,1},{1,2},{2,3},{3,0},{4,5},{5,6},{6,7},{7,4},{8,9},{9,10},{10,1... | collective-permute-start | bytes 3145736 | tf_op jit(solution)/shard_map/ppermute | solution.py:272
  129.8 21.0 %collective-permute-start.14 = (bf16[256,2048]{1,0:T(8,128)(2,1)S(1)}, bf16[256,2048]{1,0:T(8,128)(2,1)S(1)}, u32[]{:S(2)}, u32[]{:S(2)}) collective-permute-start(bf16[256,2048]{1,0:T(8,128)(2,1)S(1)} %collective-permute-done.13.refs_6_), channel_id=1, source_target_pairs={{0,24},{1,25},{2,26},{3,27},{4,28},{5,29},{6,30},{7,31},{8,0},{9,1... | collective-permute-start | bytes 3145736 | tf_op jit(solution)/shard_map/ppermute | solution.py:272
  131.2 21.1 %collective-permute-start.7 = (bf16[256,2048]{1,0:T(8,128)(2,1)S(1)}, bf16[256,2048]{1,0:T(8,128)(2,1)S(1)}, u32[]{:S(2)}, u32[]{:S(2)}) collective-permute-start(bf16[256,2048]{1,0:T(8,128)(2,1)S(1)} %collective-permute-done.6.refs_4_), channel_id=1, source_target_pairs={{0,3},{1,0},{2,1},{3,2},{4,7},{5,4},{6,5},{7,6},{8,11},{9,8},{10,9... | collective-permute-start | bytes 3145736 | tf_op jit(solution)/shard_map/ppermute | solution.py:272
  144.8 43.5 %collective-permute-start.34 = (f32[2,256,1024]{2,1,0:T(8,128)}, f32[2,256,1024]{2,1,0:T(8,128)S(1)}, u32[]{:S(2)}, u32[]{:S(2)}) collective-permute-start(f32[2,256,1024]{2,1,0:T(8,128)} %get-tuple-element.32.mine), channel_id=1, source_target_pairs={{0,32},{1,33},{2,34},{3,35},{4,36},{5,37},{6,38},{7,39},{8,40},{9,... | collective-permute-start | bytes 6291464 | tf_op jit(solution)/shard_map/ppermute | solution.py:272
  150.9 24.7 %collective-permute-start.37 = (bf16[2,256,1024]{2,1,0:T(8,128)(2,1)S(1)}, bf16[2,256,1024]{2,1,0:T(8,128)(2,1)S(1)}, u32[]{:S(2)}, u32[]{:S(2)}) collective-permute-start(bf16[2,256,1024]{2,1,0:T(8,128)(2,1)S(1)} %copy-done.34), channel_id=1, source_target_pairs={{0,4},{1,5},{2,6},{3,7},{4,0},{5,1},{6,2},{7,3},{8,12},{9,13},{10,... | collective-permute-start | bytes 3145736 | tf_op jit(solution)/shard_map/ppermute | solution.py:272
  152.4 39.4 %collective-permute-start.22 = (f32[2,256,1024]{2,1,0:T(8,128)}, f32[2,256,1024]{2,1,0:T(8,128)S(1)}, u32[]{:S(2)}, u32[]{:S(2)}) collective-permute-start(f32[2,256,1024]{2,1,0:T(8,128)} %get-tuple-element.25.mine), channel_id=1, source_target_pairs={{0,32},{1,33},{2,34},{3,35},{4,36},{5,37},{6,38},{7,39},{8,40},{9,... | collective-permute-start | bytes 6291464 | tf_op jit(solution)/shard_map/ppermute | solution.py:272
  158.4 63.5 %collective-permute-start.15 = (f32[2,256,1024]{2,1,0:T(8,128)}, f32[2,256,1024]{2,1,0:T(8,128)S(1)}, u32[]{:S(2)}, u32[]{:S(2)}) collective-permute-start(f32[2,256,1024]{2,1,0:T(8,128)} %get-tuple-element.22.mine), channel_id=1, source_target_pairs={{0,32},{1,33},{2,34},{3,35},{4,36},{5,37},{6,38},{7,39},{8,40},{9,... | collective-permute-start | bytes 6291464 | tf_op jit(solution)/shard_map/ppermute | solution.py:272
  158.6 28.2 %collective-permute-start.25 = (bf16[2,256,512]{2,1,0:T(8,128)(2,1)S(1)}, bf16[2,256,512]{2,1,0:T(8,128)(2,1)S(1)}, u32[]{:S(2)}, u32[]{:S(2)}) collective-permute-start(bf16[2,256,512]{2,1,0:T(8,128)(2,1)S(1)} %copy-done.35), channel_id=1, source_target_pairs={{0,4},{1,5},{2,6},{3,7},{4,0},{5,1},{6,2},{7,3},{8,12},{9,13},{10,... | collective-permute-start | bytes 1572872 | tf_op jit(solution)/shard_map/ppermute | solution.py:272
  186.8 39.0 %collective-permute-start.18 = (bf16[2,256,1024]{2,1,0:T(8,128)(2,1)S(1)}, bf16[2,256,1024]{2,1,0:T(8,128)(2,1)}, u32[]{:S(2)}, u32[]{:S(2)}) collective-permute-start(bf16[2,256,1024]{2,1,0:T(8,128)(2,1)S(1)} %copy-done.33), channel_id=1, source_target_pairs={{0,4},{1,5},{2,6},{3,7},{4,0},{5,1},{6,2},{7,3},{8,12},{9,13},{10,... | collective-permute-start | bytes 3145736 | tf_op jit(solution)/shard_map/ppermute | solution.py:272
  188.2 38.6 %collective-permute-start.38 = (bf16[2,256,1024]{2,1,0:T(8,128)(2,1)S(1)}, bf16[2,256,1024]{2,1,0:T(8,128)(2,1)S(1)}, u32[]{:S(2)}, u32[]{:S(2)}) collective-permute-start(bf16[2,256,1024]{2,1,0:T(8,128)(2,1)S(1)} %collective-permute-done.37.refs_6_), channel_id=1, source_target_pairs={{0,32},{1,33},{2,34},{3,35},{4,36},{5,37},{6,38},{7,39},{8,40},{9,... | collective-permute-start | bytes 3145736 | tf_op jit(solution)/shard_map/ppermute | solution.py:272
  191.7 39.0 %collective-permute-start.41 = (bf16[256,1024]{1,0:T(8,128)(2,1)S(1)}, bf16[256,1024]{1,0:T(8,128)(2,1)S(1)}, u32[]{:S(2)}, u32[]{:S(2)}) collective-permute-start(bf16[256,1024]{1,0:T(8,128)(2,1)S(1)} %collective-permute-done.40.refs_4_), channel_id=1, source_target_pairs={{0,32},{1,33},{2,34},{3,35},{4,36},{5,37},{6,38},{7,39},{8,40},{9,... | collective-permute-start | bytes 1572872 | tf_op jit(solution)/shard_map/ppermute | solution.py:272
  202.0 30.4 %collective-permute-start.36 = (bf16[256,1024]{1,0:T(8,128)(2,1)S(1)}, bf16[256,1024]{1,0:T(8,128)(2,1)S(1)}, u32[]{:S(2)}, u32[]{:S(2)}) collective-permute-start(bf16[256,1024]{1,0:T(8,128)(2,1)S(1)} %collective-permute-done.35.refs_4_), channel_id=1, source_target_pairs={{0,32},{1,33},{2,34},{3,35},{4,36},{5,37},{6,38},{7,39},{8,40},{9,... | collective-permute-start | bytes 1572872 | tf_op jit(solution)/shard_map/ppermute | solution.py:272
  221.9 20.8 %collective-permute-start.23 = (bf16[256,1024]{1,0:T(8,128)(2,1)}, bf16[256,1024]{1,0:T(8,128)(2,1)}, u32[]{:S(2)}, u32[]{:S(2)}) collective-permute-start(bf16[256,1024]{1,0:T(8,128)(2,1)} %shard_map.71), channel_id=1, source_target_pairs={{0,64},{1,65},{2,66},{3,67},{4,68},{5,69},{6,70},{7,71},{8,72},{9,... | collective-permute-start | bytes 1572872 | tf_op jit(solution)/shard_map/ppermute | solution.py:272
  225.9 44.0 %collective-permute-start.19 = (bf16[2,256,1024]{2,1,0:T(8,128)(2,1)}, bf16[2,256,1024]{2,1,0:T(8,128)(2,1)}, u32[]{:S(2)}, u32[]{:S(2)}) collective-permute-start(bf16[2,256,1024]{2,1,0:T(8,128)(2,1)} %collective-permute-done.18.refs_6_), channel_id=1, source_target_pairs={{0,32},{1,33},{2,34},{3,35},{4,36},{5,37},{6,38},{7,39},{8,40},{9,... | collective-permute-start | bytes 3145736 | tf_op jit(solution)/shard_map/ppermute | solution.py:272
  227.8 20.6 %collective-permute-start.16 = (bf16[256,1024]{1,0:T(8,128)(2,1)}, bf16[256,1024]{1,0:T(8,128)(2,1)}, u32[]{:S(2)}, u32[]{:S(2)}) collective-permute-start(bf16[256,1024]{1,0:T(8,128)(2,1)} %shard_map.69), channel_id=1, source_target_pairs={{0,64},{1,65},{2,66},{3,67},{4,68},{5,69},{6,70},{7,71},{8,72},{9,... | collective-permute-start | bytes 1572872 | tf_op jit(solution)/shard_map/ppermute | solution.py:272
  231.4 32.7 %collective-permute-start.31 = (f32[1,256,512]{2,1,0:T(8,128)}, f32[1,256,512]{2,1,0:T(8,128)}, u32[]{:S(2)}, u32[]{:S(2)}) collective-permute-start(f32[1,256,512]{2,1,0:T(8,128)} %get-tuple-element.30), channel_id=1, source_target_pairs={{0,32},{1,33},{2,34},{3,35},{4,36},{5,37},{6,38},{7,39},{8,40},{9,... | collective-permute-start | bytes 1572872 | tf_op jit(solution)/shard_map/ppermute | solution.py:272
  233.2 30.9 %collective-permute-start.26 = (bf16[2,256,512]{2,1,0:T(8,128)(2,1)S(1)}, bf16[2,256,512]{2,1,0:T(8,128)(2,1)}, u32[]{:S(2)}, u32[]{:S(2)}) collective-permute-start(bf16[2,256,512]{2,1,0:T(8,128)(2,1)S(1)} %collective-permute-done.25.refs_6_), channel_id=1, source_target_pairs={{0,32},{1,33},{2,34},{3,35},{4,36},{5,37},{6,38},{7,39},{8,40},{9,... | collective-permute-start | bytes 1572872 | tf_op jit(solution)/shard_map/ppermute | solution.py:272
  242.7 21.5 %collective-permute-start.24 = (bf16[256,1024]{1,0:T(8,128)(2,1)}, bf16[256,1024]{1,0:T(8,128)(2,1)}, u32[]{:S(2)}, u32[]{:S(2)}) collective-permute-start(bf16[256,1024]{1,0:T(8,128)(2,1)} %collective-permute-done.23.refs_4_), channel_id=1, source_target_pairs={{0,32},{1,33},{2,34},{3,35},{4,36},{5,37},{6,38},{7,39},{8,40},{9,... | collective-permute-start | bytes 1572872 | tf_op jit(solution)/shard_map/ppermute | solution.py:272
  248.3 21.5 %collective-permute-start.17 = (bf16[256,1024]{1,0:T(8,128)(2,1)}, bf16[256,1024]{1,0:T(8,128)(2,1)}, u32[]{:S(2)}, u32[]{:S(2)}) collective-permute-start(bf16[256,1024]{1,0:T(8,128)(2,1)} %collective-permute-done.16.refs_4_), channel_id=1, source_target_pairs={{0,32},{1,33},{2,34},{3,35},{4,36},{5,37},{6,38},{7,39},{8,40},{9,... | collective-permute-start | bytes 1572872 | tf_op jit(solution)/shard_map/ppermute | solution.py:272
  (50 other events, 585.1 us)

commit v4 on v3

--- a/solution.py
+++ b/solution.py
@@ -59,20 +59,33 @@
 
 
 def gram_kernel(slabs, layout, skip, gives, count, local, r0, r1, *refs):
-    xs, refs = refs[:count], refs[count:]
-    own_ref, sum_ref = refs[0], refs[1]
+    sources, refs = refs[:count], refs[count:]
+    own_ref, sum_ref, refs = refs[0], refs[1], refs[2:]
+    targets = [(r0, own_ref)]
+    if gives:
+        give_ref, acc, refs = refs[0], refs[1], refs[2:]
+        targets.append((r1, acc))
+        acc[...] = jnp.zeros_like(acc)
+    xs, sems = refs[:-1], refs[-1]
     i = pl.program_id(0)
     size = r0.shape[1] // slabs
+    loads = [pltpu.make_async_copy(sources[n], xs[n], sems.at[n]) for n in range(count)]
+
+    @pl.when(i == 0)
+    def _():
+        for load in loads:
+            load.start()
+
     own_ref[...] = jnp.zeros_like(own_ref)
-    targets = [(r0, own_ref)]
-    if gives:
-        give_ref, acc = refs[2], refs[3]
-        acc[...] = jnp.zeros_like(acc)
-        targets.append((r1, acc))
+    seen = set()
     for k, ((a, ha), (b, hb)) in enumerate(layout):
+        fresh = sorted({a, b} - seen)
+        seen.update(fresh)
 
         @pl.when(i == k)
-        def _(k=k, a=xs[a], ha=ha, b=xs[b], hb=hb):
+        def _(k=k, fresh=fresh, a=xs[a], ha=ha, b=xs[b], hb=hb):
+            for n in fresh:
+                loads[n].wait()
             for t in range(slabs):
                 part = pl.ds(t * size, size)
                 x = jnp.concatenate(
@@ -120,9 +133,12 @@
         grid_spec=pltpu.PrefetchScalarGridSpec(
             num_scalar_prefetch=1,
             grid=(m,),
-            in_specs=[whole(x) for x in (rooted, partner, *xs)],
+            in_specs=[whole(rooted), whole(partner)]
+            + [pl.BlockSpec(memory_space=pl.ANY)] * len(xs),
             out_specs=out_specs,
-            scratch_shapes=[pltpu.VMEM((2, 256, 256), jnp.float32)] if gives else [],
+            scratch_shapes=([pltpu.VMEM((2, 256, 256), jnp.float32)] if gives else [])
+            + [pltpu.VMEM(x.shape, x.dtype) for x in xs]
+            + [pltpu.SemaphoreType.DMA((len(xs),))],
         ),
         out_shape=out_shape,
         compiler_params=pltpu.CompilerParams(vmem_limit_bytes=20 * MIB),
@@ -328,6 +344,8 @@
     places = ((0, 0, 1), (1, 0, 1), (2, 0, 1), (3, 0, 1))
     state, mine, theirs, u = [], [], [], None
     for n, xs in enumerate(blocks):
+        if n == 2:
+            local, complement_rhs = lax.optimization_barrier((local, complement_rhs))
         message, half, parts = places[n]
         g, s, give = gram(local, rooted, partner, xs, layouts[n], skips[n], True)
         swapped = send(s, CORE)

time: 277 us -> 276 us (level)
  no operation moved by 1% of the time
where the time goes in v4:
time: 276 us; the launch traced here: 275 us
  waiting for transfers between devices  117 us (42%)
  starting transfers between devices  77.9 us (28%)
  Pallas kernels  58.6 us (21%)
  local copies, waits for them, and re-layouts  12.9 us (5%)
  other arithmetic  7.45 us (3%)
    ppermute x46, waiting for transfers between devices, send(): return lax.ppermute(x, AXES, pairs)  117 us
    ppermute x46, starting transfers between devices, send(): return lax.ppermute(x, AXES, pairs)  77.9 us
    pallas_call x5, Pallas kernels, gram(): pl.pallas_call(lambda *refs: gram_kernel(local.shape[0], layout, skip, gi...  29 us
    pallas_call x4, Pallas kernels, final(): pl.pallas_call(lambda *refs: final_kernel(out is None, skip, *refs), grid...  21.6 us
    unnamed x73, local copies, waits for them, and re-layouts  10.9 us
    pallas_call x4, Pallas kernels, mix(): pl.pallas_call(mix_kernel, grid_spec=pltpu.PrefetchScalarGridSpec(num_sca...  7.98 us
  transfers between devices with their start and end apart: 46, of which 12 were waited for; matrix products, arithmetic and copies ran while one was open for 3% of the time, Pallas kernels for 19%

profile of v4, /device:TPU:1, one launch (start us, length us, event | category | flops | bytes accessed | tf_op | source)
XLA Modules:
  0.0 275.2 jit_solution(6045489336116173209)
XLA Ops:
  3.4 4.6 %collective-permute-start.10 = (bf16[128,2048]{1,0:T(8,128)(2,1)S(1)}, bf16[128,2048]{1,0:T(8,128)(2,1)}, u32[]{:S(2)}, u32[]{:S(2)}) collective-permute-start(bf16[128,2048]{1,0:T(8,128)(2,1)S(1)} %get-tuple-element.48), channel_id=1, source_target_pairs={{0,1},{1,2},{2,3},{3,0},{4,5},{5,6},{6,7},{7,4},{8,9},{9,10},{10,1... | collective-permute-start | bytes 1572872 | tf_op jit(solution)/shard_map/ppermute | solution.py:288
  8.0 2.7 collective-permute-start.3
  13.0 5.6 %collective-permute-done.10 = bf16[128,2048]{1,0:T(8,128)(2,1)} collective-permute-done((bf16[128,2048]{1,0:T(8,128)(2,1)S(1)}, bf16[128,2048]{1,0:T(8,128)(2,1)}, u32[]{:S(2)}, u32[]{:S(2)}) %collective-permute-start.10) | collective-permute-done | bytes 524320 | tf_op jit(solution)/shard_map/ppermute | solution.py:288
  28.7 2.8 %collective-permute-start.2 = (f32[256]{0:T(256)S(1)}, f32[256]{0:T(256)S(1)}, u32[]{:S(2)}, u32[]{:S(2)}) collective-permute-start(f32[256]{0:T(256)S(1)} %add.244), channel_id=1, source_target_pairs={{0,64},{1,65},{2,66},{3,67},{4,68},{5,69},{6,70},{7,71},{8,72},{9,... | collective-permute-start | bytes 3080 | tf_op jit(solution)/shard_map/ppermute | solution.py:288
  31.9 4.0 %collective-permute-done.2 = f32[256]{0:T(256)S(1)} collective-permute-done((f32[256]{0:T(256)S(1)}, f32[256]{0:T(256)S(1)}, u32[]{:S(2)}, u32[]{:S(2)}) %collective-permute-start.2) | collective-permute-done | bytes 1056 | tf_op jit(solution)/shard_map/ppermute | solution.py:288
  35.9 3.8 %collective-permute-start.35 = (bf16[256,2048]{1,0:T(8,128)(2,1)}, bf16[256,2048]{1,0:T(8,128)(2,1)S(1)}, u32[]{:S(2)}, u32[]{:S(2)}) collective-permute-start(bf16[256,2048]{1,0:T(8,128)(2,1)} %pad_maximum_fusion.2.refs_5_), channel_id=1, source_target_pairs={{0,24},{1,25},{2,26},{3,27},{4,28},{5,29},{6,30},{7,31},{8,0},{9,1... | collective-permute-start | bytes 3145736 | tf_op jit(solution)/shard_map/ppermute | solution.py:288
  39.7 3.4 %collective-permute-start.34 = (bf16[256,2048]{1,0:T(8,128)(2,1)}, bf16[256,2048]{1,0:T(8,128)(2,1)S(1)}, u32[]{:S(2)}, u32[]{:S(2)}) collective-permute-start(bf16[256,2048]{1,0:T(8,128)(2,1)} %pad_maximum_fusion.refs_4_), channel_id=1, source_target_pairs={{0,3},{1,0},{2,1},{3,2},{4,7},{5,4},{6,5},{7,6},{8,11},{9,8},{10,9... | collective-permute-start | bytes 3145736 | tf_op jit(solution)/shard_map/ppermute | solution.py:288
  43.4 29.0 %collective-permute-done.7.refs_6_ = bf16[128,2048]{1,0:T(8,128)(2,1)S(1)} collective-permute-done((bf16[128,2048]{1,0:T(8,128)(2,1)}, bf16[128,2048]{1,0:T(8,128)(2,1)S(1)}, u32[]{:S(2)}, u32[]{:S(2)}) %collective-permute-start.7) | collective-permute-done | bytes 524320 | tf_op jit(solution)/shard_map/ppermute | solution.py:288
  72.4 4.5 %collective-permute-start.30 = (bf16[128,2048]{1,0:T(8,128)(2,1)S(1)}, bf16[128,2048]{1,0:T(8,128)(2,1)S(1)}, u32[]{:S(2)}, u32[]{:S(2)}) collective-permute-start(bf16[128,2048]{1,0:T(8,128)(2,1)S(1)} %get-tuple-element.30), channel_id=1, source_target_pairs={{0,3},{1,0},{2,1},{3,2},{4,7},{5,4},{6,5},{7,6},{8,11},{9,8},{10,9... | collective-permute-start | bytes 1572872 | tf_op jit(solution)/shard_map/ppermute | solution.py:288
  76.8 3.3 %collective-permute-start.15 = (bf16[256,2048]{1,0:T(8,128)(2,1)S(1)}, bf16[256,2048]{1,0:T(8,128)(2,1)S(1)}, u32[]{:S(2)}, u32[]{:S(2)}) collective-permute-start(bf16[256,2048]{1,0:T(8,128)(2,1)S(1)} %pad_maximum_fusion.3), channel_id=1, source_target_pairs={{0,24},{1,25},{2,26},{3,27},{4,28},{5,29},{6,30},{7,31},{8,0},{9,1... | collective-permute-start | bytes 3145736 | tf_op jit(solution)/shard_map/ppermute | solution.py:288
  81.3 6.6 %shard_map.75 = (f32[2,256,1280]{2,1,0:T(8,128)}, f32[2,256,1280]{2,1,0:T(8,128)}, bf16[2,256,768]{2,1,0:T(8,128)(2,1)}) custom-call(s32[8]{0:T(128)S(1)} %get-tuple-element.23.refs_0_, bf16[256,2048]{1,0:T(8,128)(2,1)S(1)} %fusion.refs_1_.refs_3_, bf16[256,2048]{1,0:T(8,128)(2,1)S(1)} %collective-permute-done.refs_2_.refs_8_, ...), custom_call_target="tpu_custom_call" | custom-call | flops 2684354560 | bytes 15728640 | tf_op jit(solution)/shard_map/pallas_call | solution.py:131
  89.5 2.7 collective-permute-start.32
  92.2 10.5 %collective-permute-done.31.refs_5_ = bf16[128,2048]{1,0:T(8,128)(2,1)S(1)} collective-permute-done((bf16[128,2048]{1,0:T(8,128)(2,1)S(1)}, bf16[128,2048]{1,0:T(8,128)(2,1)S(1)}, u32[]{:S(2)}, u32[]{:S(2)}) %collective-permute-start.31) | collective-permute-done | bytes 524320 | tf_op jit(solution)/shard_map/ppermute | solution.py:288
  104.0 22.1 %collective-permute-done.22.refs_3_ = bf16[256,2048]{1,0:T(8,128)(2,1)S(1)} collective-permute-done((bf16[256,2048]{1,0:T(8,128)(2,1)S(1)}, bf16[256,2048]{1,0:T(8,128)(2,1)S(1)}, u32[]{:S(2)}, u32[]{:S(2)}) %collective-permute-start.22) | collective-permute-done | bytes 1048608 | tf_op jit(solution)/shard_map/ppermute | solution.py:288
  126.0 3.1 %collective-permute-done.23.refs_5_ = bf16[256,2048]{1,0:T(8,128)(2,1)S(1)} collective-permute-done((bf16[256,2048]{1,0:T(8,128)(2,1)S(1)}, bf16[256,2048]{1,0:T(8,128)(2,1)S(1)}, u32[]{:S(2)}, u32[]{:S(2)}) %collective-permute-start.23) | collective-permute-done | bytes 1048608 | tf_op jit(solution)/shard_map/ppermute | solution.py:288
  129.1 3.4 %collective-permute-start.9 = (bf16[256,2048]{1,0:T(8,128)(2,1)S(1)}, bf16[256,2048]{1,0:T(8,128)(2,1)S(1)}, u32[]{:S(2)}, u32[]{:S(2)}) collective-permute-start(bf16[256,2048]{1,0:T(8,128)(2,1)S(1)} %collective-permute-done.8.refs_4_), channel_id=1, source_target_pairs={{0,3},{1,0},{2,1},{3,2},{4,7},{5,4},{6,5},{7,6},{8,11},{9,8},{10,9... | collective-permute-start | bytes 3145736 | tf_op jit(solution)/shard_map/ppermute | solution.py:288
  134.9 7.3 %shard_map.73 = (f32[2,256,1024]{2,1,0:T(8,128)}, f32[2,256,1024]{2,1,0:T(8,128)}, bf16[2,256,1024]{2,1,0:T(8,128)(2,1)}) custom-call(s32[8]{0:T(128)S(1)} %get-tuple-element.23.refs_0_, bf16[256,2048]{1,0:T(8,128)(2,1)S(1)} %copy-done.1, bf16[256,2048]{1,0:T(8,128)(2,1)S(1)} %copy-done.9, bf16[256,2048]{1,0:T(8,128)(2,1)} %collective-permute-done.5.refs_3_, ...), custom_call_target="tpu_custom_call" | custom-call | flops 2147483648 | bytes 12582912 | tf_op jit(solution)/shard_map/pallas_call | solution.py:131
  144.8 6.1 %shard_map.70 = (f32[2,256,1024]{2,1,0:T(8,128)}, f32[2,256,1024]{2,1,0:T(8,128)}, bf16[2,256,512]{2,1,0:T(8,128)(2,1)}) custom-call(s32[8]{0:T(128)S(1)} %get-tuple-element.23.refs_0_, bf16[256,2048]{1,0:T(8,128)(2,1)S(1)} %copy-done.1, bf16[256,2048]{1,0:T(8,128)(2,1)S(1)} %copy-done.9, bf16[256,2048]{1,0:T(8,128)(2,1)S(1)} %collective-permute-done.22.refs_3_, ...), custom_call_target="tpu_custom_call" | custom-call | flops 2147483648 | bytes 12582912 | tf_op jit(solution)/shard_map/pallas_call | solution.py:131
  152.8 6.2 %shard_map.68 = (f32[2,256,1024]{2,1,0:T(8,128)}, f32[2,256,1024]{2,1,0:T(8,128)}, bf16[2,256,1024]{2,1,0:T(8,128)(2,1)}) custom-call(s32[8]{0:T(128)S(1)} %get-tuple-element.23.refs_0_, bf16[256,2048]{1,0:T(8,128)(2,1)S(1)} %copy-done.1, bf16[256,2048]{1,0:T(8,128)(2,1)S(1)} %copy-done.9, bf16[256,2048]{1,0:T(8,128)(2,1)S(1)} %collective-permute-done.6.refs_3_, ...), custom_call_target="tpu_custom_call" | custom-call | flops 2147483648 | bytes 12582912 | tf_op jit(solution)/shard_map/pallas_call | solution.py:131
  159.6 2.1 shard_map.76
  161.6 14.0 %collective-permute-done.39.refs_6_ = bf16[2,256,1024]{2,1,0:T(8,128)(2,1)S(1)} collective-permute-done((bf16[2,256,1024]{2,1,0:T(8,128)(2,1)S(1)}, bf16[2,256,1024]{2,1,0:T(8,128)(2,1)S(1)}, u32[]{:S(2)}, u32[]{:S(2)}) %collective-permute-start.39) | collective-permute-done | bytes 1048608 | tf_op jit(solution)/shard_map/ppermute | solution.py:288
  176.4 10.5 %collective-permute-done.27.refs_6_ = bf16[2,256,512]{2,1,0:T(8,128)(2,1)S(1)} collective-permute-done((bf16[2,256,512]{2,1,0:T(8,128)(2,1)S(1)}, bf16[2,256,512]{2,1,0:T(8,128)(2,1)S(1)}, u32[]{:S(2)}, u32[]{:S(2)}) %collective-permute-start.27) | collective-permute-done | bytes 524320 | tf_op jit(solution)/shard_map/ppermute | solution.py:288
  191.8 8.3 %collective-permute-start.43 = (bf16[256,1024]{1,0:T(8,128)(2,1)S(1)}, bf16[256,1024]{1,0:T(8,128)(2,1)S(1)}, u32[]{:S(2)}, u32[]{:S(2)}) collective-permute-start(bf16[256,1024]{1,0:T(8,128)(2,1)S(1)} %collective-permute-done.42.refs_4_), channel_id=1, source_target_pairs={{0,32},{1,33},{2,34},{3,35},{4,36},{5,37},{6,38},{7,39},{8,40},{9,... | collective-permute-start | bytes 1572872 | tf_op jit(solution)/shard_map/ppermute | solution.py:288
  200.1 2.0 shard_map.71
  202.1 19.9 %collective-permute-start.38 = (bf16[256,1024]{1,0:T(8,128)(2,1)S(1)}, bf16[256,1024]{1,0:T(8,128)(2,1)S(1)}, u32[]{:S(2)}, u32[]{:S(2)}) collective-permute-start(bf16[256,1024]{1,0:T(8,128)(2,1)S(1)} %collective-permute-done.37.refs_4_), channel_id=1, source_target_pairs={{0,32},{1,33},{2,34},{3,35},{4,36},{5,37},{6,38},{7,39},{8,40},{9,... | collective-permute-start | bytes 1572872 | tf_op jit(solution)/shard_map/ppermute | solution.py:288
  228.1 2.9 %shard_map.72 = (f32[2,256,512]{2,1,0:T(8,128)}, f32[1,256,512]{2,1,0:T(8,128)}) custom-call(s32[8]{0:T(128)S(1)} %get-tuple-element.23.refs_0_, bf16[256,2048]{1,0:T(8,128)(2,1)S(1)} %copy-done.1, bf16[256,2048]{1,0:T(8,128)(2,1)S(1)} %copy-done.10, bf16[128,2048]{1,0:T(8,128)(2,1)S(1)} %collective-permute-done.29.refs_3_, ...), custom_call_target="tpu_custom_call" | custom-call | flops 1073741824 | bytes 6291456 | tf_op jit(solution)/shard_map/pallas_call | solution.py:131
  233.5 9.3 %collective-permute-done.25.refs_4_ = bf16[256,1024]{1,0:T(8,128)(2,1)} collective-permute-done((bf16[256,1024]{1,0:T(8,128)(2,1)}, bf16[256,1024]{1,0:T(8,128)(2,1)}, u32[]{:S(2)}, u32[]{:S(2)}) %collective-permute-start.25) | collective-permute-done | bytes 524320 | tf_op jit(solution)/shard_map/ppermute | solution.py:288
  242.8 5.6 %collective-permute-done.18.refs_4_ = bf16[256,1024]{1,0:T(8,128)(2,1)} collective-permute-done((bf16[256,1024]{1,0:T(8,128)(2,1)}, bf16[256,1024]{1,0:T(8,128)(2,1)}, u32[]{:S(2)}, u32[]{:S(2)}) %collective-permute-start.18) | collective-permute-done | bytes 524320 | tf_op jit(solution)/shard_map/ppermute | solution.py:288
  253.2 5.4 %shard_map.77.refs_8_ = f32[2,256,8192]{2,1,0:T(8,128)} custom-call(s32[1]{0:T(128)} %bitcast.r_ref.refs_0_, s32[16]{0:T(128)S(1)} %stack.283.refs_1_, f32[2,256,1280]{2,1,0:T(8,128)} %get-tuple-element.37.refs_2_.refs_8_, f32[2,256,1280]{2,1,0:T(8,128)S(1)} %collective-permute-done.41.theirs.refs_3_.refs_9_, bf16[256,1024]{1,0:T(8,128)(2,1)S(1)} %copy-done.20, ...), custom_call_target="tpu_custom_call" | custom-call | flops 1048576 | bytes 9437184 | tf_op jit(solution)/shard_map/pallas_call | solution.py:251
  258.7 5.0 %shard_map.78.refs_10_ = f32[2,256,8192]{2,1,0:T(8,128)} custom-call(s32[1]{0:T(128)} %bitcast.r_ref.refs_0_, s32[16]{0:T(128)S(1)} %stack.266.refs_1_, f32[2,256,1024]{2,1,0:T(8,128)} %get-tuple-element.34.refs_2_, f32[2,256,1024]{2,1,0:T(8,128)S(1)} %copy-done.3, bf16[256,1024]{1,0:T(8,128)(2,1)S(1)} %copy-done.22, ...), custom_call_target="tpu_custom_call", output_to_operand_aliasing={{}: (8, {})} | custom-call | flops 1048576 | bytes 9437184 | tf_op jit(solution)/shard_map/pallas_call | solution.py:251
  263.7 5.6 %shard_map.79.refs_8_ = f32[2,256,8192]{2,1,0:T(8,128)} custom-call(s32[1]{0:T(128)} %bitcast.r_ref.refs_0_, s32[16]{0:T(128)S(1)} %stack.249.refs_1_, f32[2,256,1024]{2,1,0:T(8,128)} %get-tuple-element.27.refs_2_, f32[2,256,1024]{2,1,0:T(8,128)S(1)} %copy-done.7, ...), custom_call_target="tpu_custom_call", output_to_operand_aliasing={{}: (10, {})} | custom-call | flops 1048576 | bytes 9437184 | tf_op jit(solution)/shard_map/pallas_call | solution.py:251
  269.4 5.6 %shard_map.80 = f32[2,256,8192]{2,1,0:T(8,128)} custom-call(s32[1]{0:T(128)} %bitcast.r_ref.refs_0_, s32[16]{0:T(128)S(1)} %stack.229.refs_1_, f32[2,256,1024]{2,1,0:T(8,128)} %get-tuple-element.24.refs_2_, f32[2,256,1024]{2,1,0:T(8,128)S(1)} %copy-done.5, bf16[256,1024]{1,0:T(8,128)(2,1)} %collective-permute-done.18.refs_4_, ...), custom_call_target="tpu_custom_call", output_to_operand_aliasing={{}: (8, {})} | custom-call | flops 1048576 | bytes 9437184 | tf_op jit(solution)/shard_map/pallas_call | solution.py:251
  (176 shorter events, 46.1 us)
Async XLA Ops:
  10.7 29.0 %collective-permute-start = (bf16[256,2048]{1,0:T(8,128)(2,1)S(1)}, bf16[256,2048]{1,0:T(8,128)(2,1)S(1)}, u32[]{:S(2)}, u32[]{:S(2)}) collective-permute-start(bf16[256,2048]{1,0:T(8,128)(2,1)S(1)} %fusion.refs_1_.refs_3_), channel_id=1, source_target_pairs={{0,4},{1,5},{2,6},{3,7},{4,0},{5,1},{6,2},{7,3},{8,12},{9,13},{10,... | collective-permute-start | bytes 3145736 | tf_op jit(solution)/shard_map/ppermute | solution.py:288
  23.8 48.6 %collective-permute-start.12 = (bf16[256,2048]{1,0:T(8,128)(2,1)}, bf16[256,2048]{1,0:T(8,128)(2,1)}, u32[]{:S(2)}, u32[]{:S(2)}) collective-permute-start(bf16[256,2048]{1,0:T(8,128)(2,1)} %pad_maximum_fusion.2.refs_5_), channel_id=1, source_target_pairs={{0,8},{1,9},{2,10},{3,11},{4,12},{5,13},{6,14},{7,15},{8,16},{9,17... | collective-permute-start | bytes 3145736 | tf_op jit(solution)/shard_map/ppermute | solution.py:288
  24.8 18.4 %collective-permute-start.14 = (bf16[128,2048]{1,0:T(8,128)(2,1)}, bf16[128,2048]{1,0:T(8,128)(2,1)S(1)}, u32[]{:S(2)}, u32[]{:S(2)}) collective-permute-start(bf16[128,2048]{1,0:T(8,128)(2,1)} %collective-permute-done.10), channel_id=1, source_target_pairs={{0,1},{1,2},{2,3},{3,0},{4,5},{5,6},{6,7},{7,4},{8,9},{9,10},{10,1... | collective-permute-start | bytes 1572872 | tf_op jit(solution)/shard_map/ppermute | solution.py:288
  28.6 48.3 %collective-permute-start.5 = (bf16[256,2048]{1,0:T(8,128)(2,1)}, bf16[256,2048]{1,0:T(8,128)(2,1)}, u32[]{:S(2)}, u32[]{:S(2)}) collective-permute-start(bf16[256,2048]{1,0:T(8,128)(2,1)} %pad_maximum_fusion.refs_4_), channel_id=1, source_target_pairs={{0,1},{1,2},{2,3},{3,0},{4,5},{5,6},{6,7},{7,4},{8,9},{9,10},{10,1... | collective-permute-start | bytes 3145736 | tf_op jit(solution)/shard_map/ppermute | solution.py:288
  35.9 52.0 %collective-permute-start.35 = (bf16[256,2048]{1,0:T(8,128)(2,1)}, bf16[256,2048]{1,0:T(8,128)(2,1)S(1)}, u32[]{:S(2)}, u32[]{:S(2)}) collective-permute-start(bf16[256,2048]{1,0:T(8,128)(2,1)} %pad_maximum_fusion.2.refs_5_), channel_id=1, source_target_pairs={{0,24},{1,25},{2,26},{3,27},{4,28},{5,29},{6,30},{7,31},{8,0},{9,1... | collective-permute-start | bytes 3145736 | tf_op jit(solution)/shard_map/ppermute | solution.py:288
  39.7 49.7 %collective-permute-start.34 = (bf16[256,2048]{1,0:T(8,128)(2,1)}, bf16[256,2048]{1,0:T(8,128)(2,1)S(1)}, u32[]{:S(2)}, u32[]{:S(2)}) collective-permute-start(bf16[256,2048]{1,0:T(8,128)(2,1)} %pad_maximum_fusion.refs_4_), channel_id=1, source_target_pairs={{0,3},{1,0},{2,1},{3,2},{4,7},{5,4},{6,5},{7,6},{8,11},{9,8},{10,9... | collective-permute-start | bytes 3145736 | tf_op jit(solution)/shard_map/ppermute | solution.py:288
  43.2 29.2 %collective-permute-start.7 = (bf16[128,2048]{1,0:T(8,128)(2,1)}, bf16[128,2048]{1,0:T(8,128)(2,1)S(1)}, u32[]{:S(2)}, u32[]{:S(2)}) collective-permute-start(bf16[128,2048]{1,0:T(8,128)(2,1)} %collective-permute-done.3), channel_id=1, source_target_pairs={{0,8},{1,9},{2,10},{3,11},{4,12},{5,13},{6,14},{7,15},{8,16},{9,17... | collective-permute-start | bytes 1572872 | tf_op jit(solution)/shard_map/ppermute | solution.py:288
  72.4 17.2 %collective-permute-start.30 = (bf16[128,2048]{1,0:T(8,128)(2,1)S(1)}, bf16[128,2048]{1,0:T(8,128)(2,1)S(1)}, u32[]{:S(2)}, u32[]{:S(2)}) collective-permute-start(bf16[128,2048]{1,0:T(8,128)(2,1)S(1)} %get-tuple-element.30), channel_id=1, source_target_pairs={{0,3},{1,0},{2,1},{3,2},{4,7},{5,4},{6,5},{7,6},{8,11},{9,8},{10,9... | collective-permute-start | bytes 1572872 | tf_op jit(solution)/shard_map/ppermute | solution.py:288
  76.8 26.0 %collective-permute-start.15 = (bf16[256,2048]{1,0:T(8,128)(2,1)S(1)}, bf16[256,2048]{1,0:T(8,128)(2,1)S(1)}, u32[]{:S(2)}, u32[]{:S(2)}) collective-permute-start(bf16[256,2048]{1,0:T(8,128)(2,1)S(1)} %pad_maximum_fusion.3), channel_id=1, source_target_pairs={{0,24},{1,25},{2,26},{3,27},{4,28},{5,29},{6,30},{7,31},{8,0},{9,1... | collective-permute-start | bytes 3145736 | tf_op jit(solution)/shard_map/ppermute | solution.py:288
  102.7 23.3 %collective-permute-start.22 = (bf16[256,2048]{1,0:T(8,128)(2,1)S(1)}, bf16[256,2048]{1,0:T(8,128)(2,1)S(1)}, u32[]{:S(2)}, u32[]{:S(2)}) collective-permute-start(bf16[256,2048]{1,0:T(8,128)(2,1)S(1)} %pad_maximum_fusion.1), channel_id=1, source_target_pairs={{0,1},{1,2},{2,3},{3,0},{4,5},{5,6},{6,7},{7,4},{8,9},{9,10},{10,1... | collective-permute-start | bytes 3145736 | tf_op jit(solution)/shard_map/ppermute | solution.py:288
  102.7 26.4 %collective-permute-start.23 = (bf16[256,2048]{1,0:T(8,128)(2,1)S(1)}, bf16[256,2048]{1,0:T(8,128)(2,1)S(1)}, u32[]{:S(2)}, u32[]{:S(2)}) collective-permute-start(bf16[256,2048]{1,0:T(8,128)(2,1)S(1)} %pad_maximum_fusion.3), channel_id=1, source_target_pairs={{0,8},{1,9},{2,10},{3,11},{4,12},{5,13},{6,14},{7,15},{8,16},{9,17... | collective-permute-start | bytes 3145736 | tf_op jit(solution)/shard_map/ppermute | solution.py:288
  102.7 56.5 %collective-permute-start.41 = (f32[2,256,1280]{2,1,0:T(8,128)}, f32[2,256,1280]{2,1,0:T(8,128)S(1)}, u32[]{:S(2)}, u32[]{:S(2)}) collective-permute-start(f32[2,256,1280]{2,1,0:T(8,128)} %get-tuple-element.38.mine), channel_id=1, source_target_pairs={{0,32},{1,33},{2,34},{3,35},{4,36},{5,37},{6,38},{7,39},{8,40},{9,... | collective-permute-start | bytes 7864328 | tf_op jit(solution)/shard_map/ppermute | solution.py:288
  102.8 40.9 %collective-permute-start.13 = (bf16[256,2048]{1,0:T(8,128)(2,1)}, bf16[256,2048]{1,0:T(8,128)(2,1)S(1)}, u32[]{:S(2)}, u32[]{:S(2)}) collective-permute-start(bf16[256,2048]{1,0:T(8,128)(2,1)} %collective-permute-done.12.refs_5_), channel_id=1, source_target_pairs={{0,8},{1,9},{2,10},{3,11},{4,12},{5,13},{6,14},{7,15},{8,16},{9,17... | collective-permute-start | bytes 3145736 | tf_op jit(solution)/shard_map/ppermute | solution.py:288
  103.9 39.8 %collective-permute-start.6 = (bf16[256,2048]{1,0:T(8,128)(2,1)}, bf16[256,2048]{1,0:T(8,128)(2,1)S(1)}, u32[]{:S(2)}, u32[]{:S(2)}) collective-permute-start(bf16[256,2048]{1,0:T(8,128)(2,1)} %collective-permute-done.5.refs_3_), channel_id=1, source_target_pairs={{0,1},{1,2},{2,3},{3,0},{4,5},{5,6},{6,7},{7,4},{8,9},{9,10},{10,1... | collective-permute-start | bytes 3145736 | tf_op jit(solution)/shard_map/ppermute | solution.py:288
  126.0 24.9 %collective-permute-start.16 = (bf16[256,2048]{1,0:T(8,128)(2,1)S(1)}, bf16[256,2048]{1,0:T(8,128)(2,1)S(1)}, u32[]{:S(2)}, u32[]{:S(2)}) collective-permute-start(bf16[256,2048]{1,0:T(8,128)(2,1)S(1)} %collective-permute-done.15.refs_6_), channel_id=1, source_target_pairs={{0,24},{1,25},{2,26},{3,27},{4,28},{5,29},{6,30},{7,31},{8,0},{9,1... | collective-permute-start | bytes 3145736 | tf_op jit(solution)/shard_map/ppermute | solution.py:288
  129.1 23.3 %collective-permute-start.9 = (bf16[256,2048]{1,0:T(8,128)(2,1)S(1)}, bf16[256,2048]{1,0:T(8,128)(2,1)S(1)}, u32[]{:S(2)}, u32[]{:S(2)}) collective-permute-start(bf16[256,2048]{1,0:T(8,128)(2,1)S(1)} %collective-permute-done.8.refs_4_), channel_id=1, source_target_pairs={{0,3},{1,0},{2,1},{3,2},{4,7},{5,4},{6,5},{7,6},{8,11},{9,8},{10,9... | collective-permute-start | bytes 3145736 | tf_op jit(solution)/shard_map/ppermute | solution.py:288
  143.7 44.6 %collective-permute-start.36 = (f32[2,256,1024]{2,1,0:T(8,128)}, f32[2,256,1024]{2,1,0:T(8,128)S(1)}, u32[]{:S(2)}, u32[]{:S(2)}) collective-permute-start(f32[2,256,1024]{2,1,0:T(8,128)} %get-tuple-element.35.mine), channel_id=1, source_target_pairs={{0,32},{1,33},{2,34},{3,35},{4,36},{5,37},{6,38},{7,39},{8,40},{9,... | collective-permute-start | bytes 6291464 | tf_op jit(solution)/shard_map/ppermute | solution.py:288
  151.0 24.7 %collective-permute-start.39 = (bf16[2,256,1024]{2,1,0:T(8,128)(2,1)S(1)}, bf16[2,256,1024]{2,1,0:T(8,128)(2,1)S(1)}, u32[]{:S(2)}, u32[]{:S(2)}) collective-permute-start(bf16[2,256,1024]{2,1,0:T(8,128)(2,1)S(1)} %copy-done.34), channel_id=1, source_target_pairs={{0,4},{1,5},{2,6},{3,7},{4,0},{5,1},{6,2},{7,3},{8,12},{9,13},{10,... | collective-permute-start | bytes 3145736 | tf_op jit(solution)/shard_map/ppermute | solution.py:288
  152.4 39.4 %collective-permute-start.24 = (f32[2,256,1024]{2,1,0:T(8,128)}, f32[2,256,1024]{2,1,0:T(8,128)S(1)}, u32[]{:S(2)}, u32[]{:S(2)}) collective-permute-start(f32[2,256,1024]{2,1,0:T(8,128)} %get-tuple-element.28.mine), channel_id=1, source_target_pairs={{0,32},{1,33},{2,34},{3,35},{4,36},{5,37},{6,38},{7,39},{8,40},{9,... | collective-permute-start | bytes 6291464 | tf_op jit(solution)/shard_map/ppermute | solution.py:288
  159.0 63.0 %collective-permute-start.17 = (f32[2,256,1024]{2,1,0:T(8,128)}, f32[2,256,1024]{2,1,0:T(8,128)S(1)}, u32[]{:S(2)}, u32[]{:S(2)}) collective-permute-start(f32[2,256,1024]{2,1,0:T(8,128)} %get-tuple-element.25.mine), channel_id=1, source_target_pairs={{0,32},{1,33},{2,34},{3,35},{4,36},{5,37},{6,38},{7,39},{8,40},{9,... | collective-permute-start | bytes 6291464 | tf_op jit(solution)/shard_map/ppermute | solution.py:288
  159.2 27.7 %collective-permute-start.27 = (bf16[2,256,512]{2,1,0:T(8,128)(2,1)S(1)}, bf16[2,256,512]{2,1,0:T(8,128)(2,1)S(1)}, u32[]{:S(2)}, u32[]{:S(2)}) collective-permute-start(bf16[2,256,512]{2,1,0:T(8,128)(2,1)S(1)} %copy-done.35), channel_id=1, source_target_pairs={{0,4},{1,5},{2,6},{3,7},{4,0},{5,1},{6,2},{7,3},{8,12},{9,13},{10,... | collective-permute-start | bytes 1572872 | tf_op jit(solution)/shard_map/ppermute | solution.py:288
  186.9 39.0 %collective-permute-start.20 = (bf16[2,256,1024]{2,1,0:T(8,128)(2,1)S(1)}, bf16[2,256,1024]{2,1,0:T(8,128)(2,1)}, u32[]{:S(2)}, u32[]{:S(2)}) collective-permute-start(bf16[2,256,1024]{2,1,0:T(8,128)(2,1)S(1)} %copy-done.33), channel_id=1, source_target_pairs={{0,4},{1,5},{2,6},{3,7},{4,0},{5,1},{6,2},{7,3},{8,12},{9,13},{10,... | collective-permute-start | bytes 3145736 | tf_op jit(solution)/shard_map/ppermute | solution.py:288
  188.3 38.6 %collective-permute-start.40 = (bf16[2,256,1024]{2,1,0:T(8,128)(2,1)S(1)}, bf16[2,256,1024]{2,1,0:T(8,128)(2,1)S(1)}, u32[]{:S(2)}, u32[]{:S(2)}) collective-permute-start(bf16[2,256,1024]{2,1,0:T(8,128)(2,1)S(1)} %collective-permute-done.39.refs_6_), channel_id=1, source_target_pairs={{0,32},{1,33},{2,34},{3,35},{4,36},{5,37},{6,38},{7,39},{8,40},{9,... | collective-permute-start | bytes 3145736 | tf_op jit(solution)/shard_map/ppermute | solution.py:288
  191.8 39.2 %collective-permute-start.43 = (bf16[256,1024]{1,0:T(8,128)(2,1)S(1)}, bf16[256,1024]{1,0:T(8,128)(2,1)S(1)}, u32[]{:S(2)}, u32[]{:S(2)}) collective-permute-start(bf16[256,1024]{1,0:T(8,128)(2,1)S(1)} %collective-permute-done.42.refs_4_), channel_id=1, source_target_pairs={{0,32},{1,33},{2,34},{3,35},{4,36},{5,37},{6,38},{7,39},{8,40},{9,... | collective-permute-start | bytes 1572872 | tf_op jit(solution)/shard_map/ppermute | solution.py:288
  202.1 30.6 %collective-permute-start.38 = (bf16[256,1024]{1,0:T(8,128)(2,1)S(1)}, bf16[256,1024]{1,0:T(8,128)(2,1)S(1)}, u32[]{:S(2)}, u32[]{:S(2)}) collective-permute-start(bf16[256,1024]{1,0:T(8,128)(2,1)S(1)} %collective-permute-done.37.refs_4_), channel_id=1, source_target_pairs={{0,32},{1,33},{2,34},{3,35},{4,36},{5,37},{6,38},{7,39},{8,40},{9,... | collective-permute-start | bytes 1572872 | tf_op jit(solution)/shard_map/ppermute | solution.py:288
  222.0 20.8 %collective-permute-start.25 = (bf16[256,1024]{1,0:T(8,128)(2,1)}, bf16[256,1024]{1,0:T(8,128)(2,1)}, u32[]{:S(2)}, u32[]{:S(2)}) collective-permute-start(bf16[256,1024]{1,0:T(8,128)(2,1)} %shard_map.71), channel_id=1, source_target_pairs={{0,64},{1,65},{2,66},{3,67},{4,68},{5,69},{6,70},{7,71},{8,72},{9,... | collective-permute-start | bytes 1572872 | tf_op jit(solution)/shard_map/ppermute | solution.py:288
  225.9 43.4 %collective-permute-start.21 = (bf16[2,256,1024]{2,1,0:T(8,128)(2,1)}, bf16[2,256,1024]{2,1,0:T(8,128)(2,1)}, u32[]{:S(2)}, u32[]{:S(2)}) collective-permute-start(bf16[2,256,1024]{2,1,0:T(8,128)(2,1)} %collective-permute-done.20.refs_6_), channel_id=1, source_target_pairs={{0,32},{1,33},{2,34},{3,35},{4,36},{5,37},{6,38},{7,39},{8,40},{9,... | collective-permute-start | bytes 3145736 | tf_op jit(solution)/shard_map/ppermute | solution.py:288
  227.8 20.6 %collective-permute-start.18 = (bf16[256,1024]{1,0:T(8,128)(2,1)}, bf16[256,1024]{1,0:T(8,128)(2,1)}, u32[]{:S(2)}, u32[]{:S(2)}) collective-permute-start(bf16[256,1024]{1,0:T(8,128)(2,1)} %shard_map.69), channel_id=1, source_target_pairs={{0,64},{1,65},{2,66},{3,67},{4,68},{5,69},{6,70},{7,71},{8,72},{9,... | collective-permute-start | bytes 1572872 | tf_op jit(solution)/shard_map/ppermute | solution.py:288
  231.7 31.9 %collective-permute-start.33 = (f32[1,256,512]{2,1,0:T(8,128)}, f32[1,256,512]{2,1,0:T(8,128)}, u32[]{:S(2)}, u32[]{:S(2)}) collective-permute-start(f32[1,256,512]{2,1,0:T(8,128)} %get-tuple-element.33), channel_id=1, source_target_pairs={{0,32},{1,33},{2,34},{3,35},{4,36},{5,37},{6,38},{7,39},{8,40},{9,... | collective-permute-start | bytes 1572872 | tf_op jit(solution)/shard_map/ppermute | solution.py:288
  233.5 30.1 %collective-permute-start.28 = (bf16[2,256,512]{2,1,0:T(8,128)(2,1)S(1)}, bf16[2,256,512]{2,1,0:T(8,128)(2,1)}, u32[]{:S(2)}, u32[]{:S(2)}) collective-permute-start(bf16[2,256,512]{2,1,0:T(8,128)(2,1)S(1)} %collective-permute-done.27.refs_6_), channel_id=1, source_target_pairs={{0,32},{1,33},{2,34},{3,35},{4,36},{5,37},{6,38},{7,39},{8,40},{9,... | collective-permute-start | bytes 1572872 | tf_op jit(solution)/shard_map/ppermute | solution.py:288
  242.8 20.9 %collective-permute-start.26 = (bf16[256,1024]{1,0:T(8,128)(2,1)}, bf16[256,1024]{1,0:T(8,128)(2,1)}, u32[]{:S(2)}, u32[]{:S(2)}) collective-permute-start(bf16[256,1024]{1,0:T(8,128)(2,1)} %collective-permute-done.25.refs_4_), channel_id=1, source_target_pairs={{0,32},{1,33},{2,34},{3,35},{4,36},{5,37},{6,38},{7,39},{8,40},{9,... | collective-permute-start | bytes 1572872 | tf_op jit(solution)/shard_map/ppermute | solution.py:288
  248.4 20.9 %collective-permute-start.19 = (bf16[256,1024]{1,0:T(8,128)(2,1)}, bf16[256,1024]{1,0:T(8,128)(2,1)}, u32[]{:S(2)}, u32[]{:S(2)}) collective-permute-start(bf16[256,1024]{1,0:T(8,128)(2,1)} %collective-permute-done.18.refs_4_), channel_id=1, source_target_pairs={{0,32},{1,33},{2,34},{3,35},{4,36},{5,37},{6,38},{7,39},{8,40},{9,... | collective-permute-start | bytes 1572872 | tf_op jit(solution)/shard_map/ppermute | solution.py:288
  (50 other events, 583.6 us)

commit v5 on v4

--- a/solution.py
+++ b/solution.py
@@ -39,11 +39,19 @@
     return pairs
 
 
+def even(v):
+    return v + 1 - 2 * (v % 2)
+
+
+def odd(v):
+    return (v - 1 + 2 * (v % 2)) % 4
+
+
 STEP = {
-    ("y", 1): perm(lambda h, c, y, l, z: (h, c, (y + 1) % 4, l, z)),
-    ("y", -1): perm(lambda h, c, y, l, z: (h, c, (y - 1) % 4, l, z)),
-    ("z", 1): perm(lambda h, c, y, l, z: (h, c, y, l, (z + 1) % 4)),
-    ("z", -1): perm(lambda h, c, y, l, z: (h, c, y, l, (z - 1) % 4)),
+    ("y", 1): perm(lambda h, c, y, l, z: (h, c, even(y), l, z)),
+    ("y", -1): perm(lambda h, c, y, l, z: (h, c, odd(y), l, z)),
+    ("z", 1): perm(lambda h, c, y, l, z: (h, c, y, l, even(z))),
+    ("z", -1): perm(lambda h, c, y, l, z: (h, c, y, l, odd(z))),
 }
 TURN = {
     ("y", 1): perm(lambda h, c, y, l, z: (h, c, (y + 1 - 2 * c) % 4, l, z)),
@@ -314,19 +322,19 @@
         ab_m, ab_p = send(ab, STEP[q, 1]), send(ab, STEP[q, -1])
         od = jnp.concatenate([own, d], axis=0)
         od_m, od_p = send(od, STEP[q, 1]), send(od, STEP[q, -1])
-        ab_2 = send(ab_m, STEP[q, 1])
-        od_2 = send(od_p, STEP[q, -1])
+        ab_2 = send(ab_m, STEP[q, -1])
+        od_2 = send(od_p, STEP[q, 1])
         blocks[0].append(ab)
         far.append(d)
         blocks[1].extend([ab_m, ab_p])
         blocks[2].extend([od_m, od_p])
         blocks[3].extend([ab_2, od_2])
         where[0].extend(at(o, 0) for o in (-1, 1))
-        where[1].extend(at(o, v) for v in (-1, 1) for o in (-1, 1))
-        where[2].extend(at(0, v) for v in (-1, 1))
+        where[1].extend(at(o, v) for v in (1, -1) for o in (-1, 1))
+        where[2].extend(at(0, v) for v in (1, -1))
         where[3].extend(at(o, 2) for o in (-1, 1, 0, 2))
     where[0].extend([(2, 0, 0), (0, 2, 1)])
-    where[2].extend([(2, -1, 0), (2, 1, 0), (-1, 2, 1), (1, 2, 1)])
+    where[2].extend([(2, 1, 0), (2, -1, 0), (1, 2, 1), (-1, 2, 1)])
     blocks[0].extend(far + [partner])
     both = lambda k: ((k, 0), (k, 1))
     layouts = (
@@ -365,11 +373,16 @@
     g_known, s = gram(local, rooted, partner, known, (pair(0), pair(2)), 0, False)
     s_known = send(s, CORE)
     raw = {0: (state[0][0], state[0][1], 4), 2: (g_known, s_known, 0)}
+    turn_y, turn_z = 1 - 2 * lax.rem(me_y, 2), 1 - 2 * lax.rem(me_z, 2)
     out = None
     for n, (g, swapped, dr, er) in enumerate(state):
         message, half, _ = places[n]
         cols = []
         for dy, dz, colour in where[n]:
+            if colour == 0:
+                dz = dz * turn_z
+            else:
+                dy = dy * turn_y
             y, z = lax.rem(me_y + dy + 4, 4), lax.rem(me_z + dz + 4, 4)
             for l in (me_l, 1 - me_l):
                 cols.append((y * 8 + l * 4 + z) * 2 + colour)

time: 276 us -> 279 us (1.011)
  starting transfers between devices: 77.9 us -> 82.2 us
    ppermute x46, starting transfers between devices: 77.9 us -> 82.2 us  [send(): return lax.ppermute(x, AXES, pairs)]
  transfers between devices with their start and end apart: 46 -> 46, of which waited for: 12 -> 13; matrix products, arithmetic and copies ran while one was open for 3% -> 3% of each run, Pallas kernels for 19% -> 19%
where the time goes in v5:
time: 279 us; the launch traced here: 278 us
  waiting for transfers between devices  115 us (41%)
  starting transfers between devices  82.2 us (29%)
  Pallas kernels  58.6 us (21%)
  local copies, waits for them, and re-layouts  12.9 us (5%)
  other arithmetic  7.45 us (3%)
    ppermute x46, waiting for transfers between devices, send(): return lax.ppermute(x, AXES, pairs)  115 us
    ppermute x46, starting transfers between devices, send(): return lax.ppermute(x, AXES, pairs)  82.2 us
    pallas_call x5, Pallas kernels, gram(): pl.pallas_call(lambda *refs: gram_kernel(local.shape[0], layout, skip, gi...  29 us
    pallas_call x4, Pallas kernels, final(): pl.pallas_call(lambda *refs: final_kernel(out is None, skip, *refs), grid...  21.6 us
    unnamed x73, local copies, waits for them, and re-layouts  10.9 us
    pallas_call x4, Pallas kernels, mix(): pl.pallas_call(mix_kernel, grid_spec=pltpu.PrefetchScalarGridSpec(num_sca...  7.98 us
  transfers between devices with their start and end apart: 46, of which 13 were waited for; matrix products, arithmetic and copies ran while one was open for 3% of the time, Pallas kernels for 19%

profile of v5, /device:TPU:1, one launch (start us, length us, event | category | flops | bytes accessed | tf_op | source)
XLA Modules:
  0.0 277.9 jit_solution(801970685925876449)
XLA Ops:
  3.4 4.6 %collective-permute-start.10 = (bf16[128,2048]{1,0:T(8,128)(2,1)S(1)}, bf16[128,2048]{1,0:T(8,128)(2,1)}, u32[]{:S(2)}, u32[]{:S(2)}) collective-permute-start(bf16[128,2048]{1,0:T(8,128)(2,1)S(1)} %get-tuple-element.48), channel_id=1, source_target_pairs={{0,1},{1,2},{2,3},{3,0},{4,5},{5,6},{6,7},{7,4},{8,9},{9,10},{10,1... | collective-permute-start | bytes 1572872 | tf_op jit(solution)/shard_map/ppermute | solution.py:296
  8.0 2.7 collective-permute-start.3
  13.0 5.6 %collective-permute-done.10 = bf16[128,2048]{1,0:T(8,128)(2,1)} collective-permute-done((bf16[128,2048]{1,0:T(8,128)(2,1)S(1)}, bf16[128,2048]{1,0:T(8,128)(2,1)}, u32[]{:S(2)}, u32[]{:S(2)}) %collective-permute-start.10) | collective-permute-done | bytes 524320 | tf_op jit(solution)/shard_map/ppermute | solution.py:296
  28.7 2.8 %collective-permute-start.2 = (f32[256]{0:T(256)S(1)}, f32[256]{0:T(256)S(1)}, u32[]{:S(2)}, u32[]{:S(2)}) collective-permute-start(f32[256]{0:T(256)S(1)} %add.628), channel_id=1, source_target_pairs={{0,64},{1,65},{2,66},{3,67},{4,68},{5,69},{6,70},{7,71},{8,72},{9,... | collective-permute-start | bytes 3080 | tf_op jit(solution)/shard_map/ppermute | solution.py:296
  31.9 4.0 %collective-permute-done.2 = f32[256]{0:T(256)S(1)} collective-permute-done((f32[256]{0:T(256)S(1)}, f32[256]{0:T(256)S(1)}, u32[]{:S(2)}, u32[]{:S(2)}) %collective-permute-start.2) | collective-permute-done | bytes 1056 | tf_op jit(solution)/shard_map/ppermute | solution.py:296
  35.9 3.8 %collective-permute-start.35 = (bf16[256,2048]{1,0:T(8,128)(2,1)}, bf16[256,2048]{1,0:T(8,128)(2,1)S(1)}, u32[]{:S(2)}, u32[]{:S(2)}) collective-permute-start(bf16[256,2048]{1,0:T(8,128)(2,1)} %pad_maximum_fusion.2.refs_5_), channel_id=1, source_target_pairs={{0,24},{1,25},{2,26},{3,27},{4,28},{5,29},{6,30},{7,31},{8,16},{9,... | collective-permute-start | bytes 3145736 | tf_op jit(solution)/shard_map/ppermute | solution.py:296
  39.7 3.4 %collective-permute-start.34 = (bf16[256,2048]{1,0:T(8,128)(2,1)}, bf16[256,2048]{1,0:T(8,128)(2,1)S(1)}, u32[]{:S(2)}, u32[]{:S(2)}) collective-permute-start(bf16[256,2048]{1,0:T(8,128)(2,1)} %pad_maximum_fusion.refs_4_), channel_id=1, source_target_pairs={{0,3},{1,2},{2,1},{3,0},{4,7},{5,6},{6,5},{7,4},{8,11},{9,10},{10,... | collective-permute-start | bytes 3145736 | tf_op jit(solution)/shard_map/ppermute | solution.py:296
  43.4 25.3 %collective-permute-done.7.refs_6_ = bf16[128,2048]{1,0:T(8,128)(2,1)S(1)} collective-permute-done((bf16[128,2048]{1,0:T(8,128)(2,1)}, bf16[128,2048]{1,0:T(8,128)(2,1)S(1)}, u32[]{:S(2)}, u32[]{:S(2)}) %collective-permute-start.7) | collective-permute-done | bytes 524320 | tf_op jit(solution)/shard_map/ppermute | solution.py:296
  68.7 3.4 %collective-permute-start.30 = (bf16[128,2048]{1,0:T(8,128)(2,1)S(1)}, bf16[128,2048]{1,0:T(8,128)(2,1)S(1)}, u32[]{:S(2)}, u32[]{:S(2)}) collective-permute-start(bf16[128,2048]{1,0:T(8,128)(2,1)S(1)} %get-tuple-element.30), channel_id=1, source_target_pairs={{0,3},{1,2},{2,1},{3,0},{4,7},{5,6},{6,5},{7,4},{8,11},{9,10},{10,... | collective-permute-start | bytes 1572872 | tf_op jit(solution)/shard_map/ppermute | solution.py:296
  72.1 3.0 %collective-permute-start.15 = (bf16[256,2048]{1,0:T(8,128)(2,1)S(1)}, bf16[256,2048]{1,0:T(8,128)(2,1)S(1)}, u32[]{:S(2)}, u32[]{:S(2)}) collective-permute-start(bf16[256,2048]{1,0:T(8,128)(2,1)S(1)} %pad_maximum_fusion.3), channel_id=1, source_target_pairs={{0,24},{1,25},{2,26},{3,27},{4,28},{5,29},{6,30},{7,31},{8,16},{9,... | collective-permute-start | bytes 3145736 | tf_op jit(solution)/shard_map/ppermute | solution.py:296
  76.2 6.6 %shard_map.75 = (f32[2,256,1280]{2,1,0:T(8,128)}, f32[2,256,1280]{2,1,0:T(8,128)}, bf16[2,256,768]{2,1,0:T(8,128)(2,1)}) custom-call(s32[8]{0:T(128)S(1)} %get-tuple-element.23.refs_0_, bf16[256,2048]{1,0:T(8,128)(2,1)S(1)} %fusion.refs_1_.refs_3_, bf16[256,2048]{1,0:T(8,128)(2,1)S(1)} %collective-permute-done.refs_2_.refs_8_, ...), custom_call_target="tpu_custom_call" | custom-call | flops 2684354560 | bytes 15728640 | tf_op jit(solution)/shard_map/pallas_call | solution.py:139
  85.1 11.6 %collective-permute-done.31.refs_5_ = bf16[128,2048]{1,0:T(8,128)(2,1)S(1)} collective-permute-done((bf16[128,2048]{1,0:T(8,128)(2,1)S(1)}, bf16[128,2048]{1,0:T(8,128)(2,1)S(1)}, u32[]{:S(2)}, u32[]{:S(2)}) %collective-permute-start.31) | collective-permute-done | bytes 524320 | tf_op jit(solution)/shard_map/ppermute | solution.py:296
  97.4 11.2 %collective-permute-done.32.refs_6_ = bf16[128,2048]{1,0:T(8,128)(2,1)S(1)} collective-permute-done((bf16[128,2048]{1,0:T(8,128)(2,1)S(1)}, bf16[128,2048]{1,0:T(8,128)(2,1)S(1)}, u32[]{:S(2)}, u32[]{:S(2)}) %collective-permute-start.32) | collective-permute-done | bytes 524320 | tf_op jit(solution)/shard_map/ppermute | solution.py:296
  111.1 9.6 %collective-permute-done.22.refs_3_ = bf16[256,2048]{1,0:T(8,128)(2,1)S(1)} collective-permute-done((bf16[256,2048]{1,0:T(8,128)(2,1)S(1)}, bf16[256,2048]{1,0:T(8,128)(2,1)S(1)}, u32[]{:S(2)}, u32[]{:S(2)}) %collective-permute-start.22) | collective-permute-done | bytes 1048608 | tf_op jit(solution)/shard_map/ppermute | solution.py:296
  121.3 10.2 %collective-permute-done.23.refs_5_ = bf16[256,2048]{1,0:T(8,128)(2,1)S(1)} collective-permute-done((bf16[256,2048]{1,0:T(8,128)(2,1)S(1)}, bf16[256,2048]{1,0:T(8,128)(2,1)S(1)}, u32[]{:S(2)}, u32[]{:S(2)}) %collective-permute-start.23) | collective-permute-done | bytes 1048608 | tf_op jit(solution)/shard_map/ppermute | solution.py:296
  134.2 7.3 %shard_map.73 = (f32[2,256,1024]{2,1,0:T(8,128)}, f32[2,256,1024]{2,1,0:T(8,128)}, bf16[2,256,1024]{2,1,0:T(8,128)(2,1)}) custom-call(s32[8]{0:T(128)S(1)} %get-tuple-element.23.refs_0_, bf16[256,2048]{1,0:T(8,128)(2,1)S(1)} %copy-done.1, bf16[256,2048]{1,0:T(8,128)(2,1)S(1)} %copy-done.9, bf16[256,2048]{1,0:T(8,128)(2,1)} %collective-permute-done.5.refs_3_, ...), custom_call_target="tpu_custom_call" | custom-call | flops 2147483648 | bytes 12582912 | tf_op jit(solution)/shard_map/pallas_call | solution.py:139
  141.5 5.9 %collective-permute-start.36 = (f32[2,256,1024]{2,1,0:T(8,128)}, f32[2,256,1024]{2,1,0:T(8,128)S(1)}, u32[]{:S(2)}, u32[]{:S(2)}) collective-permute-start(f32[2,256,1024]{2,1,0:T(8,128)} %get-tuple-element.35.mine), channel_id=1, source_target_pairs={{0,32},{1,33},{2,34},{3,35},{4,36},{5,37},{6,38},{7,39},{8,40},{9,... | collective-permute-start | bytes 6291464 | tf_op jit(solution)/shard_map/ppermute | solution.py:296
  148.1 6.1 %shard_map.70 = (f32[2,256,1024]{2,1,0:T(8,128)}, f32[2,256,1024]{2,1,0:T(8,128)}, bf16[2,256,512]{2,1,0:T(8,128)(2,1)}) custom-call(s32[8]{0:T(128)S(1)} %get-tuple-element.23.refs_0_, bf16[256,2048]{1,0:T(8,128)(2,1)S(1)} %copy-done.1, bf16[256,2048]{1,0:T(8,128)(2,1)S(1)} %copy-done.9, bf16[256,2048]{1,0:T(8,128)(2,1)S(1)} %collective-permute-done.22.refs_3_, ...), custom_call_target="tpu_custom_call" | custom-call | flops 2147483648 | bytes 12582912 | tf_op jit(solution)/shard_map/pallas_call | solution.py:139
  154.4 2.7 collective-permute-start.24
  157.1 6.2 %shard_map.68 = (f32[2,256,1024]{2,1,0:T(8,128)}, f32[2,256,1024]{2,1,0:T(8,128)}, bf16[2,256,1024]{2,1,0:T(8,128)(2,1)}) custom-call(s32[8]{0:T(128)S(1)} %get-tuple-element.23.refs_0_, bf16[256,2048]{1,0:T(8,128)(2,1)S(1)} %copy-done.1, bf16[256,2048]{1,0:T(8,128)(2,1)S(1)} %copy-done.9, bf16[256,2048]{1,0:T(8,128)(2,1)S(1)} %collective-permute-done.6.refs_3_, ...), custom_call_target="tpu_custom_call" | custom-call | flops 2147483648 | bytes 12582912 | tf_op jit(solution)/shard_map/pallas_call | solution.py:139
  166.9 9.9 %collective-permute-done.39.refs_6_ = bf16[2,256,1024]{2,1,0:T(8,128)(2,1)S(1)} collective-permute-done((bf16[2,256,1024]{2,1,0:T(8,128)(2,1)S(1)}, bf16[2,256,1024]{2,1,0:T(8,128)(2,1)S(1)}, u32[]{:S(2)}, u32[]{:S(2)}) %collective-permute-start.39) | collective-permute-done | bytes 1048608 | tf_op jit(solution)/shard_map/ppermute | solution.py:296
  177.0 11.0 %collective-permute-done.27.refs_6_ = bf16[2,256,512]{2,1,0:T(8,128)(2,1)S(1)} collective-permute-done((bf16[2,256,512]{2,1,0:T(8,128)(2,1)S(1)}, bf16[2,256,512]{2,1,0:T(8,128)(2,1)S(1)}, u32[]{:S(2)}, u32[]{:S(2)}) %collective-permute-start.27) | collective-permute-done | bytes 524320 | tf_op jit(solution)/shard_map/ppermute | solution.py:296
  188.1 3.4 %collective-permute-start.40 = (bf16[2,256,1024]{2,1,0:T(8,128)(2,1)S(1)}, bf16[2,256,1024]{2,1,0:T(8,128)(2,1)S(1)}, u32[]{:S(2)}, u32[]{:S(2)}) collective-permute-start(bf16[2,256,1024]{2,1,0:T(8,128)(2,1)S(1)} %collective-permute-done.39.refs_6_), channel_id=1, source_target_pairs={{0,32},{1,33},{2,34},{3,35},{4,36},{5,37},{6,38},{7,39},{8,40},{9,... | collective-permute-start | bytes 3145736 | tf_op jit(solution)/shard_map/ppermute | solution.py:296
  194.4 9.8 %collective-permute-start.43 = (bf16[256,1024]{1,0:T(8,128)(2,1)S(1)}, bf16[256,1024]{1,0:T(8,128)(2,1)S(1)}, u32[]{:S(2)}, u32[]{:S(2)}) collective-permute-start(bf16[256,1024]{1,0:T(8,128)(2,1)S(1)} %collective-permute-done.42.refs_4_), channel_id=1, source_target_pairs={{0,32},{1,33},{2,34},{3,35},{4,36},{5,37},{6,38},{7,39},{8,40},{9,... | collective-permute-start | bytes 1572872 | tf_op jit(solution)/shard_map/ppermute | solution.py:296
  206.2 18.6 %collective-permute-start.38 = (bf16[256,1024]{1,0:T(8,128)(2,1)S(1)}, bf16[256,1024]{1,0:T(8,128)(2,1)S(1)}, u32[]{:S(2)}, u32[]{:S(2)}) collective-permute-start(bf16[256,1024]{1,0:T(8,128)(2,1)S(1)} %collective-permute-done.37.refs_4_), channel_id=1, source_target_pairs={{0,32},{1,33},{2,34},{3,35},{4,36},{5,37},{6,38},{7,39},{8,40},{9,... | collective-permute-start | bytes 1572872 | tf_op jit(solution)/shard_map/ppermute | solution.py:296
  231.2 2.9 %shard_map.72 = (f32[2,256,512]{2,1,0:T(8,128)}, f32[1,256,512]{2,1,0:T(8,128)}) custom-call(s32[8]{0:T(128)S(1)} %get-tuple-element.23.refs_0_, bf16[256,2048]{1,0:T(8,128)(2,1)S(1)} %copy-done.1, bf16[256,2048]{1,0:T(8,128)(2,1)S(1)} %copy-done.10, bf16[128,2048]{1,0:T(8,128)(2,1)S(1)} %collective-permute-done.29.refs_3_, ...), custom_call_target="tpu_custom_call" | custom-call | flops 1073741824 | bytes 6291456 | tf_op jit(solution)/shard_map/pallas_call | solution.py:139
  236.2 9.4 %collective-permute-done.25.refs_4_ = bf16[256,1024]{1,0:T(8,128)(2,1)} collective-permute-done((bf16[256,1024]{1,0:T(8,128)(2,1)}, bf16[256,1024]{1,0:T(8,128)(2,1)}, u32[]{:S(2)}, u32[]{:S(2)}) %collective-permute-start.25) | collective-permute-done | bytes 524320 | tf_op jit(solution)/shard_map/ppermute | solution.py:296
  245.6 5.6 %collective-permute-done.18.refs_4_ = bf16[256,1024]{1,0:T(8,128)(2,1)} collective-permute-done((bf16[256,1024]{1,0:T(8,128)(2,1)}, bf16[256,1024]{1,0:T(8,128)(2,1)}, u32[]{:S(2)}, u32[]{:S(2)}) %collective-permute-start.18) | collective-permute-done | bytes 524320 | tf_op jit(solution)/shard_map/ppermute | solution.py:296
  256.0 5.4 %shard_map.77.refs_8_ = f32[2,256,8192]{2,1,0:T(8,128)} custom-call(s32[1]{0:T(128)} %bitcast.r_ref.refs_0_, s32[16]{0:T(128)S(1)} %stack.283.refs_1_, f32[2,256,1280]{2,1,0:T(8,128)} %get-tuple-element.37.refs_2_.refs_8_, f32[2,256,1280]{2,1,0:T(8,128)S(1)} %collective-permute-done.41.theirs.refs_3_.refs_9_, bf16[256,1024]{1,0:T(8,128)(2,1)S(1)} %copy-done.20, ...), custom_call_target="tpu_custom_call" | custom-call | flops 1048576 | bytes 9437184 | tf_op jit(solution)/shard_map/pallas_call | solution.py:259
  261.5 5.0 %shard_map.78.refs_10_ = f32[2,256,8192]{2,1,0:T(8,128)} custom-call(s32[1]{0:T(128)} %bitcast.r_ref.refs_0_, s32[16]{0:T(128)S(1)} %stack.266.refs_1_, f32[2,256,1024]{2,1,0:T(8,128)} %get-tuple-element.34.refs_2_, f32[2,256,1024]{2,1,0:T(8,128)S(1)} %copy-done.3, bf16[256,1024]{1,0:T(8,128)(2,1)S(1)} %copy-done.22, ...), custom_call_target="tpu_custom_call", output_to_operand_aliasing={{}: (8, {})} | custom-call | flops 1048576 | bytes 9437184 | tf_op jit(solution)/shard_map/pallas_call | solution.py:259
  266.5 5.6 %shard_map.79.refs_8_ = f32[2,256,8192]{2,1,0:T(8,128)} custom-call(s32[1]{0:T(128)} %bitcast.r_ref.refs_0_, s32[16]{0:T(128)S(1)} %stack.249.refs_1_, f32[2,256,1024]{2,1,0:T(8,128)} %get-tuple-element.27.refs_2_, f32[2,256,1024]{2,1,0:T(8,128)S(1)} %copy-done.7, ...), custom_call_target="tpu_custom_call", output_to_operand_aliasing={{}: (10, {})} | custom-call | flops 1048576 | bytes 9437184 | tf_op jit(solution)/shard_map/pallas_call | solution.py:259
  272.1 5.6 %shard_map.80 = f32[2,256,8192]{2,1,0:T(8,128)} custom-call(s32[1]{0:T(128)} %bitcast.r_ref.refs_0_, s32[16]{0:T(128)S(1)} %stack.229.refs_1_, f32[2,256,1024]{2,1,0:T(8,128)} %get-tuple-element.24.refs_2_, f32[2,256,1024]{2,1,0:T(8,128)S(1)} %copy-done.5, bf16[256,1024]{1,0:T(8,128)(2,1)} %collective-permute-done.18.refs_4_, ...), custom_call_target="tpu_custom_call", output_to_operand_aliasing={{}: (8, {})} | custom-call | flops 1048576 | bytes 9437184 | tf_op jit(solution)/shard_map/pallas_call | solution.py:259
  (176 shorter events, 48.4 us)
Async XLA Ops:
  10.7 29.0 %collective-permute-start = (bf16[256,2048]{1,0:T(8,128)(2,1)S(1)}, bf16[256,2048]{1,0:T(8,128)(2,1)S(1)}, u32[]{:S(2)}, u32[]{:S(2)}) collective-permute-start(bf16[256,2048]{1,0:T(8,128)(2,1)S(1)} %fusion.refs_1_.refs_3_), channel_id=1, source_target_pairs={{0,4},{1,5},{2,6},{3,7},{4,0},{5,1},{6,2},{7,3},{8,12},{9,13},{10,... | collective-permute-start | bytes 3145736 | tf_op jit(solution)/shard_map/ppermute | solution.py:296
  23.8 44.9 %collective-permute-start.12 = (bf16[256,2048]{1,0:T(8,128)(2,1)}, bf16[256,2048]{1,0:T(8,128)(2,1)}, u32[]{:S(2)}, u32[]{:S(2)}) collective-permute-start(bf16[256,2048]{1,0:T(8,128)(2,1)} %pad_maximum_fusion.2.refs_5_), channel_id=1, source_target_pairs={{0,8},{1,9},{2,10},{3,11},{4,12},{5,13},{6,14},{7,15},{8,0},{9,1},... | collective-permute-start | bytes 3145736 | tf_op jit(solution)/shard_map/ppermute | solution.py:296
  28.6 43.5 %collective-permute-start.5 = (bf16[256,2048]{1,0:T(8,128)(2,1)}, bf16[256,2048]{1,0:T(8,128)(2,1)}, u32[]{:S(2)}, u32[]{:S(2)}) collective-permute-start(bf16[256,2048]{1,0:T(8,128)(2,1)} %pad_maximum_fusion.refs_4_), channel_id=1, source_target_pairs={{0,1},{1,0},{2,3},{3,2},{4,5},{5,4},{6,7},{7,6},{8,9},{9,8},{10,11... | collective-permute-start | bytes 3145736 | tf_op jit(solution)/shard_map/ppermute | solution.py:296
  35.9 46.9 %collective-permute-start.35 = (bf16[256,2048]{1,0:T(8,128)(2,1)}, bf16[256,2048]{1,0:T(8,128)(2,1)S(1)}, u32[]{:S(2)}, u32[]{:S(2)}) collective-permute-start(bf16[256,2048]{1,0:T(8,128)(2,1)} %pad_maximum_fusion.2.refs_5_), channel_id=1, source_target_pairs={{0,24},{1,25},{2,26},{3,27},{4,28},{5,29},{6,30},{7,31},{8,16},{9,... | collective-permute-start | bytes 3145736 | tf_op jit(solution)/shard_map/ppermute | solution.py:296
  39.7 43.3 %collective-permute-start.34 = (bf16[256,2048]{1,0:T(8,128)(2,1)}, bf16[256,2048]{1,0:T(8,128)(2,1)S(1)}, u32[]{:S(2)}, u32[]{:S(2)}) collective-permute-start(bf16[256,2048]{1,0:T(8,128)(2,1)} %pad_maximum_fusion.refs_4_), channel_id=1, source_target_pairs={{0,3},{1,2},{2,1},{3,0},{4,7},{5,6},{6,5},{7,4},{8,11},{9,10},{10,... | collective-permute-start | bytes 3145736 | tf_op jit(solution)/shard_map/ppermute | solution.py:296
  43.2 25.5 %collective-permute-start.7 = (bf16[128,2048]{1,0:T(8,128)(2,1)}, bf16[128,2048]{1,0:T(8,128)(2,1)S(1)}, u32[]{:S(2)}, u32[]{:S(2)}) collective-permute-start(bf16[128,2048]{1,0:T(8,128)(2,1)} %collective-permute-done.3), channel_id=1, source_target_pairs={{0,8},{1,9},{2,10},{3,11},{4,12},{5,13},{6,14},{7,15},{8,16},{9,17... | collective-permute-start | bytes 1572872 | tf_op jit(solution)/shard_map/ppermute | solution.py:296
  72.1 38.5 %collective-permute-start.15 = (bf16[256,2048]{1,0:T(8,128)(2,1)S(1)}, bf16[256,2048]{1,0:T(8,128)(2,1)S(1)}, u32[]{:S(2)}, u32[]{:S(2)}) collective-permute-start(bf16[256,2048]{1,0:T(8,128)(2,1)S(1)} %pad_maximum_fusion.3), channel_id=1, source_target_pairs={{0,24},{1,25},{2,26},{3,27},{4,28},{5,29},{6,30},{7,31},{8,16},{9,... | collective-permute-start | bytes 3145736 | tf_op jit(solution)/shard_map/ppermute | solution.py:296
  82.8 28.3 %collective-permute-start.8 = (bf16[256,2048]{1,0:T(8,128)(2,1)S(1)}, bf16[256,2048]{1,0:T(8,128)(2,1)S(1)}, u32[]{:S(2)}, u32[]{:S(2)}) collective-permute-start(bf16[256,2048]{1,0:T(8,128)(2,1)S(1)} %pad_maximum_fusion.1), channel_id=1, source_target_pairs={{0,3},{1,2},{2,1},{3,0},{4,7},{5,6},{6,5},{7,4},{8,11},{9,10},{10,... | collective-permute-start | bytes 3145736 | tf_op jit(solution)/shard_map/ppermute | solution.py:296
  83.0 25.6 %collective-permute-start.44 = (bf16[2,256,768]{2,1,0:T(8,128)(2,1)}, bf16[2,256,768]{2,1,0:T(8,128)(2,1)S(1)}, u32[]{:S(2)}, u32[]{:S(2)}) collective-permute-start(bf16[2,256,768]{2,1,0:T(8,128)(2,1)} %get-tuple-element.39), channel_id=1, source_target_pairs={{0,4},{1,5},{2,6},{3,7},{4,0},{5,1},{6,2},{7,3},{8,12},{9,13},{10,... | collective-permute-start | bytes 2359304 | tf_op jit(solution)/shard_map/ppermute | solution.py:296
  83.3 25.3 %collective-permute-start.32 = (bf16[128,2048]{1,0:T(8,128)(2,1)S(1)}, bf16[128,2048]{1,0:T(8,128)(2,1)S(1)}, u32[]{:S(2)}, u32[]{:S(2)}) collective-permute-start(bf16[128,2048]{1,0:T(8,128)(2,1)S(1)} %get-tuple-element.31), channel_id=1, source_target_pairs={{0,24},{1,25},{2,26},{3,27},{4,28},{5,29},{6,30},{7,31},{8,16},{9,... | collective-permute-start | bytes 1572872 | tf_op jit(solution)/shard_map/ppermute | solution.py:296
  96.7 24.0 %collective-permute-start.22 = (bf16[256,2048]{1,0:T(8,128)(2,1)S(1)}, bf16[256,2048]{1,0:T(8,128)(2,1)S(1)}, u32[]{:S(2)}, u32[]{:S(2)}) collective-permute-start(bf16[256,2048]{1,0:T(8,128)(2,1)S(1)} %pad_maximum_fusion.1), channel_id=1, source_target_pairs={{0,1},{1,0},{2,3},{3,2},{4,5},{5,4},{6,7},{7,6},{8,9},{9,8},{10,11... | collective-permute-start | bytes 3145736 | tf_op jit(solution)/shard_map/ppermute | solution.py:296
  108.6 22.9 %collective-permute-start.23 = (bf16[256,2048]{1,0:T(8,128)(2,1)S(1)}, bf16[256,2048]{1,0:T(8,128)(2,1)S(1)}, u32[]{:S(2)}, u32[]{:S(2)}) collective-permute-start(bf16[256,2048]{1,0:T(8,128)(2,1)S(1)} %pad_maximum_fusion.3), channel_id=1, source_target_pairs={{0,8},{1,9},{2,10},{3,11},{4,12},{5,13},{6,14},{7,15},{8,0},{9,1},... | collective-permute-start | bytes 3145736 | tf_op jit(solution)/shard_map/ppermute | solution.py:296
  108.6 54.8 %collective-permute-start.41 = (f32[2,256,1280]{2,1,0:T(8,128)}, f32[2,256,1280]{2,1,0:T(8,128)S(1)}, u32[]{:S(2)}, u32[]{:S(2)}) collective-permute-start(f32[2,256,1280]{2,1,0:T(8,128)} %get-tuple-element.38.mine), channel_id=1, source_target_pairs={{0,32},{1,33},{2,34},{3,35},{4,36},{5,37},{6,38},{7,39},{8,40},{9,... | collective-permute-start | bytes 7864328 | tf_op jit(solution)/shard_map/ppermute | solution.py:296
  110.5 31.0 %collective-permute-start.13 = (bf16[256,2048]{1,0:T(8,128)(2,1)}, bf16[256,2048]{1,0:T(8,128)(2,1)S(1)}, u32[]{:S(2)}, u32[]{:S(2)}) collective-permute-start(bf16[256,2048]{1,0:T(8,128)(2,1)} %collective-permute-done.12.refs_5_), channel_id=1, source_target_pairs={{0,24},{1,25},{2,26},{3,27},{4,28},{5,29},{6,30},{7,31},{8,16},{9,... | collective-permute-start | bytes 3145736 | tf_op jit(solution)/shard_map/ppermute | solution.py:296
  111.1 36.3 %collective-permute-start.6 = (bf16[256,2048]{1,0:T(8,128)(2,1)}, bf16[256,2048]{1,0:T(8,128)(2,1)S(1)}, u32[]{:S(2)}, u32[]{:S(2)}) collective-permute-start(bf16[256,2048]{1,0:T(8,128)(2,1)} %collective-permute-done.5.refs_3_), channel_id=1, source_target_pairs={{0,3},{1,2},{2,1},{3,0},{4,7},{5,6},{6,5},{7,4},{8,11},{9,10},{10,... | collective-permute-start | bytes 3145736 | tf_op jit(solution)/shard_map/ppermute | solution.py:296
  120.7 33.5 %collective-permute-start.16 = (bf16[256,2048]{1,0:T(8,128)(2,1)S(1)}, bf16[256,2048]{1,0:T(8,128)(2,1)S(1)}, u32[]{:S(2)}, u32[]{:S(2)}) collective-permute-start(bf16[256,2048]{1,0:T(8,128)(2,1)S(1)} %collective-permute-done.15.refs_6_), channel_id=1, source_target_pairs={{0,8},{1,9},{2,10},{3,11},{4,12},{5,13},{6,14},{7,15},{8,0},{9,1},... | collective-permute-start | bytes 3145736 | tf_op jit(solution)/shard_map/ppermute | solution.py:296
  131.5 22.9 %collective-permute-start.9 = (bf16[256,2048]{1,0:T(8,128)(2,1)S(1)}, bf16[256,2048]{1,0:T(8,128)(2,1)S(1)}, u32[]{:S(2)}, u32[]{:S(2)}) collective-permute-start(bf16[256,2048]{1,0:T(8,128)(2,1)S(1)} %collective-permute-done.8.refs_4_), channel_id=1, source_target_pairs={{0,1},{1,0},{2,3},{3,2},{4,5},{5,4},{6,7},{7,6},{8,9},{9,8},{10,11... | collective-permute-start | bytes 3145736 | tf_op jit(solution)/shard_map/ppermute | solution.py:296
  141.5 46.5 %collective-permute-start.36 = (f32[2,256,1024]{2,1,0:T(8,128)}, f32[2,256,1024]{2,1,0:T(8,128)S(1)}, u32[]{:S(2)}, u32[]{:S(2)}) collective-permute-start(f32[2,256,1024]{2,1,0:T(8,128)} %get-tuple-element.35.mine), channel_id=1, source_target_pairs={{0,32},{1,33},{2,34},{3,35},{4,36},{5,37},{6,38},{7,39},{8,40},{9,... | collective-permute-start | bytes 6291464 | tf_op jit(solution)/shard_map/ppermute | solution.py:296
  154.3 22.5 %collective-permute-start.39 = (bf16[2,256,1024]{2,1,0:T(8,128)(2,1)S(1)}, bf16[2,256,1024]{2,1,0:T(8,128)(2,1)S(1)}, u32[]{:S(2)}, u32[]{:S(2)}) collective-permute-start(bf16[2,256,1024]{2,1,0:T(8,128)(2,1)S(1)} %copy-done.34), channel_id=1, source_target_pairs={{0,4},{1,5},{2,6},{3,7},{4,0},{5,1},{6,2},{7,3},{8,12},{9,13},{10,... | collective-permute-start | bytes 3145736 | tf_op jit(solution)/shard_map/ppermute | solution.py:296
  154.4 40.0 %collective-permute-start.24 = (f32[2,256,1024]{2,1,0:T(8,128)}, f32[2,256,1024]{2,1,0:T(8,128)S(1)}, u32[]{:S(2)}, u32[]{:S(2)}) collective-permute-start(f32[2,256,1024]{2,1,0:T(8,128)} %get-tuple-element.28.mine), channel_id=1, source_target_pairs={{0,32},{1,33},{2,34},{3,35},{4,36},{5,37},{6,38},{7,39},{8,40},{9,... | collective-permute-start | bytes 6291464 | tf_op jit(solution)/shard_map/ppermute | solution.py:296
  163.3 61.5 %collective-permute-start.17 = (f32[2,256,1024]{2,1,0:T(8,128)}, f32[2,256,1024]{2,1,0:T(8,128)S(1)}, u32[]{:S(2)}, u32[]{:S(2)}) collective-permute-start(f32[2,256,1024]{2,1,0:T(8,128)} %get-tuple-element.25.mine), channel_id=1, source_target_pairs={{0,32},{1,33},{2,34},{3,35},{4,36},{5,37},{6,38},{7,39},{8,40},{9,... | collective-permute-start | bytes 6291464 | tf_op jit(solution)/shard_map/ppermute | solution.py:296
  163.4 24.6 %collective-permute-start.27 = (bf16[2,256,512]{2,1,0:T(8,128)(2,1)S(1)}, bf16[2,256,512]{2,1,0:T(8,128)(2,1)S(1)}, u32[]{:S(2)}, u32[]{:S(2)}) collective-permute-start(bf16[2,256,512]{2,1,0:T(8,128)(2,1)S(1)} %copy-done.35), channel_id=1, source_target_pairs={{0,4},{1,5},{2,6},{3,7},{4,0},{5,1},{6,2},{7,3},{8,12},{9,13},{10,... | collective-permute-start | bytes 1572872 | tf_op jit(solution)/shard_map/ppermute | solution.py:296
  188.0 41.2 %collective-permute-start.20 = (bf16[2,256,1024]{2,1,0:T(8,128)(2,1)S(1)}, bf16[2,256,1024]{2,1,0:T(8,128)(2,1)}, u32[]{:S(2)}, u32[]{:S(2)}) collective-permute-start(bf16[2,256,1024]{2,1,0:T(8,128)(2,1)S(1)} %copy-done.33), channel_id=1, source_target_pairs={{0,4},{1,5},{2,6},{3,7},{4,0},{5,1},{6,2},{7,3},{8,12},{9,13},{10,... | collective-permute-start | bytes 3145736 | tf_op jit(solution)/shard_map/ppermute | solution.py:296
  188.1 41.3 %collective-permute-start.40 = (bf16[2,256,1024]{2,1,0:T(8,128)(2,1)S(1)}, bf16[2,256,1024]{2,1,0:T(8,128)(2,1)S(1)}, u32[]{:S(2)}, u32[]{:S(2)}) collective-permute-start(bf16[2,256,1024]{2,1,0:T(8,128)(2,1)S(1)} %collective-permute-done.39.refs_6_), channel_id=1, source_target_pairs={{0,32},{1,33},{2,34},{3,35},{4,36},{5,37},{6,38},{7,39},{8,40},{9,... | collective-permute-start | bytes 3145736 | tf_op jit(solution)/shard_map/ppermute | solution.py:296
  194.4 39.7 %collective-permute-start.43 = (bf16[256,1024]{1,0:T(8,128)(2,1)S(1)}, bf16[256,1024]{1,0:T(8,128)(2,1)S(1)}, u32[]{:S(2)}, u32[]{:S(2)}) collective-permute-start(bf16[256,1024]{1,0:T(8,128)(2,1)S(1)} %collective-permute-done.42.refs_4_), channel_id=1, source_target_pairs={{0,32},{1,33},{2,34},{3,35},{4,36},{5,37},{6,38},{7,39},{8,40},{9,... | collective-permute-start | bytes 1572872 | tf_op jit(solution)/shard_map/ppermute | solution.py:296
  206.2 28.9 %collective-permute-start.38 = (bf16[256,1024]{1,0:T(8,128)(2,1)S(1)}, bf16[256,1024]{1,0:T(8,128)(2,1)S(1)}, u32[]{:S(2)}, u32[]{:S(2)}) collective-permute-start(bf16[256,1024]{1,0:T(8,128)(2,1)S(1)} %collective-permute-done.37.refs_4_), channel_id=1, source_target_pairs={{0,32},{1,33},{2,34},{3,35},{4,36},{5,37},{6,38},{7,39},{8,40},{9,... | collective-permute-start | bytes 1572872 | tf_op jit(solution)/shard_map/ppermute | solution.py:296
  229.2 42.9 %collective-permute-start.21 = (bf16[2,256,1024]{2,1,0:T(8,128)(2,1)}, bf16[2,256,1024]{2,1,0:T(8,128)(2,1)}, u32[]{:S(2)}, u32[]{:S(2)}) collective-permute-start(bf16[2,256,1024]{2,1,0:T(8,128)(2,1)} %collective-permute-done.20.refs_6_), channel_id=1, source_target_pairs={{0,32},{1,33},{2,34},{3,35},{4,36},{5,37},{6,38},{7,39},{8,40},{9,... | collective-permute-start | bytes 3145736 | tf_op jit(solution)/shard_map/ppermute | solution.py:296
  230.3 20.9 %collective-permute-start.18 = (bf16[256,1024]{1,0:T(8,128)(2,1)}, bf16[256,1024]{1,0:T(8,128)(2,1)}, u32[]{:S(2)}, u32[]{:S(2)}) collective-permute-start(bf16[256,1024]{1,0:T(8,128)(2,1)} %shard_map.69), channel_id=1, source_target_pairs={{0,64},{1,65},{2,66},{3,67},{4,68},{5,69},{6,70},{7,71},{8,72},{9,... | collective-permute-start | bytes 1572872 | tf_op jit(solution)/shard_map/ppermute | solution.py:296
  234.9 31.5 %collective-permute-start.33 = (f32[1,256,512]{2,1,0:T(8,128)}, f32[1,256,512]{2,1,0:T(8,128)}, u32[]{:S(2)}, u32[]{:S(2)}) collective-permute-start(f32[1,256,512]{2,1,0:T(8,128)} %get-tuple-element.33), channel_id=1, source_target_pairs={{0,32},{1,33},{2,34},{3,35},{4,36},{5,37},{6,38},{7,39},{8,40},{9,... | collective-permute-start | bytes 1572872 | tf_op jit(solution)/shard_map/ppermute | solution.py:296
  236.0 30.5 %collective-permute-start.28 = (bf16[2,256,512]{2,1,0:T(8,128)(2,1)S(1)}, bf16[2,256,512]{2,1,0:T(8,128)(2,1)}, u32[]{:S(2)}, u32[]{:S(2)}) collective-permute-start(bf16[2,256,512]{2,1,0:T(8,128)(2,1)S(1)} %collective-permute-done.27.refs_6_), channel_id=1, source_target_pairs={{0,32},{1,33},{2,34},{3,35},{4,36},{5,37},{6,38},{7,39},{8,40},{9,... | collective-permute-start | bytes 1572872 | tf_op jit(solution)/shard_map/ppermute | solution.py:296
  245.6 20.9 %collective-permute-start.26 = (bf16[256,1024]{1,0:T(8,128)(2,1)}, bf16[256,1024]{1,0:T(8,128)(2,1)}, u32[]{:S(2)}, u32[]{:S(2)}) collective-permute-start(bf16[256,1024]{1,0:T(8,128)(2,1)} %collective-permute-done.25.refs_4_), channel_id=1, source_target_pairs={{0,32},{1,33},{2,34},{3,35},{4,36},{5,37},{6,38},{7,39},{8,40},{9,... | collective-permute-start | bytes 1572872 | tf_op jit(solution)/shard_map/ppermute | solution.py:296
  251.2 20.9 %collective-permute-start.19 = (bf16[256,1024]{1,0:T(8,128)(2,1)}, bf16[256,1024]{1,0:T(8,128)(2,1)}, u32[]{:S(2)}, u32[]{:S(2)}) collective-permute-start(bf16[256,1024]{1,0:T(8,128)(2,1)} %collective-permute-done.18.refs_4_), channel_id=1, source_target_pairs={{0,32},{1,33},{2,34},{3,35},{4,36},{5,37},{6,38},{7,39},{8,40},{9,... | collective-permute-start | bytes 1572872 | tf_op jit(solution)/shard_map/ppermute | solution.py:296
  (50 other events, 588.4 us)
